TPU v7x, 128 devices: a whole 4x4x4 slice. The times are simulated.
128 devices in a mesh: ctx: 8 (over z, core), head: 16 (over x, y).
Axes of the slice: x: 4, y: 4, z: 4, core: 2. Of those that a mesh axis runs over, the one named last changes fastest.
Arguments:
- queries: bfloat16 [24576, 8192], P('ctx', 'head'), may hold values from -64 to 64
- key_vectors: bfloat16 [24576, 8192], P('ctx', 'head'), may hold values from -5 to 5
- value_vectors: bfloat16 [24576, 8192], P('ctx', 'head'), may hold values from -6 to 6
- step_sizes: float32 [16, 24576], P('head', 'ctx'), may hold values from 0.0003 to 0.003
- w_in: bfloat16 [16, 512, 512], P('head'), may hold values from -0.25 to 0.25
- w_up: bfloat16 [16, 512, 512], P('head'), may hold values from -0.25 to 0.25
- w_out: bfloat16 [16, 512, 512], P('head'), may hold values from -0.125 to 0.125
- out_gate: bfloat16 [24576, 8192], P('ctx', 'head'), may hold values from -6 to 6
- norm_gain: float32 [8192], replicated, may hold values from 0.5 to 1.5
Outputs:
- layer_out: bfloat16 [24576, 8192], P(('ctx', 'head'))
All inputs are finite; a program needn't handle non-finite values.
Results may differ from a plain program's by a relative error of at most 0.025.
Values may be sent and summed in bfloat16 or wider, within the bound.
No kernel may reach another device: no remote copies, remote signals or barrier semaphores. Data moves between devices by JAX's collectives and lax.ppermute only.
A program may use at most 128 MiB of HBM per device.

v0:
```python
import functools

import jax
import jax.numpy as jnp
from jax import lax
from jax.experimental import pallas as pl
from jax.experimental.pallas import tpu as pltpu
from jax.sharding import PartitionSpec as P


WINDOW = 1024
EPSILON = 1e-06
LOG2E = 1.4426950408889634


F32 = jnp.float32
BF16 = jnp.bfloat16
NT = (((1,), (1,)), ((), ()))


def sigmoid(x):
    return 0.5 * jnp.tanh(0.5 * x) + 0.5


def dot_nt(a, b):
    return lax.dot_general(a, b, NT, preferred_element_type=F32)


def dot_nn(a, b):
    return jnp.dot(a, b, preferred_element_type=F32)


def whole(shape):
    return pl.BlockSpec(shape, lambda *_: (0,) * len(shape))


def increments_kernel(pos, k_ref, v_ref, rate_ref, wi_ref, wu_ref, wo_ref,
                      keep_ref, send_ref, slice_ref, wt, acc):
    step = pl.program_id(0)
    tile = k_ref.shape[0]

    @pl.when(step == 0)
    def _():
        wt[0] = wi_ref[0].T
        wt[1] = wu_ref[0].T
        wt[2] = wo_ref[0].T
        acc[...] = jnp.zeros_like(acc)

    k = k_ref[...]
    rate = jnp.broadcast_to(rate_ref[...], (128, tile)).T
    rate = jnp.concatenate([rate] * (v_ref.shape[1] // 128), axis=1)
    scaled = (rate * v_ref[...].astype(F32)).astype(BF16)
    gate = dot_nt(wt[0], k)
    up = dot_nt(wt[1], k)
    back = dot_nt(wt[2], scaled)
    sig = sigmoid(gate)
    act = gate * sig
    hidden = (act * up).astype(BF16)
    grad_gate = (back * up * (sig * (1.0 + gate * (1.0 - sig)))).astype(BF16)
    grad_up = (back * act).astype(BF16)
    acc[0] += dot_nn(grad_gate, k)
    acc[1] += dot_nn(grad_up, k)
    acc[2] += dot_nn(hidden, scaled)

    @pl.when(step == pl.num_programs(0) - 1)
    def _():
        half = keep_ref.shape[1]
        part = slice_ref.shape[1]
        mine = pl.multiple_of(pos[1] * half, half)
        other = pl.multiple_of((1 - pos[1]) * half, half)
        keep_ref[...] = acc[:, pl.ds(mine, half), :].astype(BF16)
        send_ref[...] = acc[:, pl.ds(other, half), :].astype(BF16)
        own = pl.multiple_of(pos[1] * half + pos[0] * part, part)
        slice_ref[...] = wt[:, pl.ds(own, part), :]


def increments(pos, k, v, rate, w_in, w_up, w_out, z_size):
    rows, hd = k.shape
    fh = w_in.shape[2]
    tile = 512
    half, part = fh // 2, fh // 2 // z_size
    row_spec = pl.BlockSpec((tile, hd), lambda i, *_: (i, 0))
    w_spec = whole((1, hd, fh))
    return pl.pallas_call(
        increments_kernel,
        grid_spec=pltpu.PrefetchScalarGridSpec(
            num_scalar_prefetch=1,
            grid=(rows // tile,),
            in_specs=[row_spec, row_spec, pl.BlockSpec((1, tile), lambda i, *_: (0, i)),
                      w_spec, w_spec, w_spec],
            out_specs=[whole((3, half, hd)), whole((3, half, hd)), whole((3, part, hd))],
            scratch_shapes=[pltpu.VMEM((3, fh, hd), BF16), pltpu.VMEM((3, fh, hd), F32)],
        ),
        out_shape=[jax.ShapeDtypeStruct((3, half, hd), BF16),
                   jax.ShapeDtypeStruct((3, half, hd), BF16),
                   jax.ShapeDtypeStruct((3, part, hd), BF16)],
        cost_estimate=pl.CostEstimate(flops=12 * rows * hd * fh, bytes_accessed=9 << 20,
                                      transcendentals=rows * fh),
        name="increments",
    )(pos, k, v, rate, w_in, w_up, w_out)


def pair_sum_kernel(pos, keep_ref, got_ref, *outs):
    count = len(outs)
    part = outs[0].shape[1]
    for d in range(count):
        at = pl.multiple_of(lax.rem(pos[0] + d, count) * part, part)
        rows = pl.ds(at, part)
        outs[d][...] = (keep_ref[:, rows, :].astype(F32) + got_ref[:, rows, :].astype(F32)).astype(BF16)


def pair_sum(pos, keep, got, z_size):
    three, half, hd = keep.shape
    part = half // z_size
    return pl.pallas_call(
        pair_sum_kernel,
        grid_spec=pltpu.PrefetchScalarGridSpec(
            num_scalar_prefetch=1, grid=(1,),
            in_specs=[whole(keep.shape)] * 2,
            out_specs=[whole((three, part, hd))] * z_size,
        ),
        out_shape=[jax.ShapeDtypeStruct((three, part, hd), BF16)] * z_size,
        name="pair_sum",
    )(pos, keep, got)


def renorm_kernel(w_ref, *refs):
    parts, out_ref = refs[:-1], refs[-1]
    w = w_ref[...].astype(F32)
    total = parts[0][...].astype(F32)
    for p in parts[1:]:
        total = total + p[...].astype(F32)
    updated = w + total
    size = w.shape[-1]
    before = jnp.sum(w * w, axis=-1, keepdims=True) / size + EPSILON
    after = jnp.sum(updated * updated, axis=-1, keepdims=True) / size + EPSILON
    out_ref[...] = (updated * (jnp.sqrt(before) / jnp.sqrt(after))).astype(BF16)


def renormed(w, parts):
    return pl.pallas_call(
        renorm_kernel,
        out_shape=jax.ShapeDtypeStruct(w.shape, BF16),
        name="renorm",
    )(w, *parts)


def attend_rows(q, k_at, v_at, lo, first, scale):
    tq = q.shape[0]
    blocks = WINDOW // tq + 1
    row = lax.broadcasted_iota(jnp.int32, (tq, tq), 0)
    col = lax.broadcasted_iota(jnp.int32, (tq, tq), 1)
    scores = []
    for j in range(blocks):
        s = dot_nt(q, k_at(j))
        ok = None
        if j == 0:
            ok = col > row
        if j == blocks - 1:
            ok = col <= row
        if lo is not None and j < blocks - 1:
            inside = col >= lo - (first + j * tq)
            ok = inside if ok is None else ok & inside
        scores.append(s if ok is None else jnp.where(ok, s, -1e30))
    top = functools.reduce(jnp.maximum, scores)
    top = jnp.max(top, axis=1, keepdims=True) * scale
    out, total = None, None
    for j in range(blocks):
        p = jnp.exp2(scores[j] * scale - top)
        total = p if total is None else total + p
        o = dot_nn(p.astype(BF16), v_at(j))
        out = o if out is None else out + o
    return out / jnp.sum(total, axis=1, keepdims=True)


def attention_own_kernel(q_ref, k_ref, v_ref, o_ref, *, tq, skip, scale):
    step = pl.program_id(0)
    per = q_ref.shape[0] // tq
    for n in range(per):
        base = (step + skip) * per * tq + n * tq - WINDOW

        def at(ref, j):
            return ref[pl.ds(pl.multiple_of(base + j * tq, tq), tq), :]

        o_ref[n * tq:(n + 1) * tq, :] = attend_rows(
            q_ref[n * tq:(n + 1) * tq, :], lambda j: at(k_ref, j), lambda j: at(v_ref, j),
            None, None, scale).astype(BF16)


def attention_first_kernel(pos, q_ref, kb_ref, vb_ref, k_ref, v_ref, _, o_ref, ek, ev, *, tq, scale):
    step = pl.program_id(0)

    @pl.when(step == 0)
    def _():
        ek[:WINDOW, :] = kb_ref[...]
        ek[WINDOW:, :] = k_ref[...]
        ev[:WINDOW, :] = vb_ref[...]
        ev[WINDOW:, :] = v_ref[...]

    lo = jnp.where(pos[0] + pos[1] == 0, WINDOW, 0)
    per = q_ref.shape[0] // tq
    for n in range(per):
        base = step * per * tq + n * tq

        def at(ref, j):
            return ref[pl.ds(pl.multiple_of(base + j * tq, tq), tq), :]

        o_ref[n * tq:(n + 1) * tq, :] = attend_rows(
            q_ref[n * tq:(n + 1) * tq, :], lambda j: at(ek, j), lambda j: at(ev, j),
            lo, base, scale).astype(BF16)


def attention_own(q, k, v, tq=256, tile=512):
    rows, hd = q.shape
    skip = WINDOW // tile
    scale = hd ** -0.5 * LOG2E
    count = rows // tile - skip
    tile_spec = pl.BlockSpec((tile, hd), lambda i: (i + skip, 0))
    return pl.pallas_call(
        functools.partial(attention_own_kernel, tq=tq, skip=skip, scale=scale),
        grid=(count,),
        in_specs=[tile_spec, whole((rows, hd)), whole((rows, hd))],
        out_specs=tile_spec,
        out_shape=jax.ShapeDtypeStruct((rows, hd), BF16),
        cost_estimate=pl.CostEstimate(flops=4 * count * tile * (WINDOW + tq) * hd,
                                      bytes_accessed=10 << 20, transcendentals=count * tile * WINDOW),
        name="attention_own",
    )(q, k, v)


def attention_first(pos, q, k_before, v_before, k, v, attended, tq=256, tile=512):
    hd = q.shape[1]
    scale = hd ** -0.5 * LOG2E
    count = WINDOW // tile
    tile_spec = pl.BlockSpec((tile, hd), lambda i, *_: (i, 0))
    return pl.pallas_call(
        functools.partial(attention_first_kernel, tq=tq, scale=scale),
        grid_spec=pltpu.PrefetchScalarGridSpec(
            num_scalar_prefetch=1, grid=(count,),
            in_specs=[tile_spec] + [whole((WINDOW, hd))] * 4 + [pl.BlockSpec(memory_space=pl.ANY)],
            out_specs=tile_spec,
            scratch_shapes=[pltpu.VMEM((2 * WINDOW, hd), BF16)] * 2,
        ),
        out_shape=jax.ShapeDtypeStruct(attended.shape, BF16),
        input_output_aliases={6: 0},
        cost_estimate=pl.CostEstimate(flops=4 * WINDOW * (WINDOW + tq) * hd,
                                      bytes_accessed=6 << 20, transcendentals=WINDOW * WINDOW),
        name="attention_first",
    )(pos, q, k_before, v_before, k, v, attended)


EXTRA = 8
LANES = 256


def apply_kernel(pos, q_ref, attended_ref, gate_ref, gain_ref, *refs):
    pieces, (y_ref, wt) = refs[:-2], refs[-2:]
    step = pl.program_id(0)

    @pl.when(step == 0)
    def _():
        at = 0
        for p in pieces:
            rows = p.shape[1]
            wt[:, at:at + rows, :] = p[...]
            at += rows

    q = q_ref[...]
    gate = dot_nt(q, wt[0])
    up = dot_nt(q, wt[1])
    hidden = (gate * sigmoid(gate) * up).astype(BF16)
    fast = dot_nn(hidden, wt[2])
    head = (attended_ref[...].astype(F32) + fast).astype(BF16).astype(F32)
    squares = jnp.sum(head * head, axis=1, keepdims=True)
    g = gate_ref[...].astype(F32)
    y = (head * (gain_ref[...] * (g * sigmoid(g)))).astype(BF16)
    share = y_ref.shape[1] - EXTRA
    for n in range(y_ref.shape[0]):
        rows = slice(n * share, (n + 1) * share)
        y_ref[n, :share, :] = y[rows]
        column = jnp.concatenate([squares[rows], jnp.zeros((LANES - share, 1), F32)], axis=0)
        line = jnp.broadcast_to(column, (LANES, 128)).T[:EXTRA, :]
        high = line.astype(BF16)
        low = (line - high.astype(F32)).astype(BF16)
        y_ref[n, share:, :LANES] = high
        y_ref[n, share:, LANES:] = low


def applied(pos, q, attended, out_gate, gain, pieces, n_head, per=4):
    rows, hd = q.shape
    share = rows // n_head
    tile = per * share
    fh = sum(p.shape[1] for p in pieces)
    row_spec = pl.BlockSpec((tile, hd), lambda i, *_: (i, 0))
    return pl.pallas_call(
        apply_kernel,
        grid_spec=pltpu.PrefetchScalarGridSpec(
            num_scalar_prefetch=1, grid=(n_head // per,),
            in_specs=[row_spec, row_spec, row_spec,
                      pl.BlockSpec((1, hd), lambda i, pos: (0, pos[2]))] + [whole(p.shape) for p in pieces],
            out_specs=pl.BlockSpec((per, share + EXTRA, hd), lambda i, *_: (i, 0, 0)),
            scratch_shapes=[pltpu.VMEM((3, fh, hd), BF16)],
        ),
        out_shape=jax.ShapeDtypeStruct((n_head, share + EXTRA, hd), BF16),
        cost_estimate=pl.CostEstimate(flops=6 * rows * hd * fh, bytes_accessed=14 << 20,
                                      transcendentals=2 * rows * fh),
        name="apply_fast",
    )(pos, q, attended, out_gate, gain, *pieces)


def scale_kernel(y_ref, squares_ref, o_ref, factor):
    share = o_ref.shape[0]

    @pl.when(pl.program_id(0) == 0)
    def _():
        s = squares_ref[...].astype(F32)
        line = jnp.sum(s, axis=0)
        line = line[:, :LANES] + line[:, LANES:]
        r = lax.rsqrt(line / (s.shape[0] * s.shape[2]) + EPSILON)
        factor[...] = jnp.concatenate([r] * (128 // EXTRA), axis=0).T

    r = factor[:share, :]
    width = y_ref.shape[2]
    r = jnp.concatenate([r] * (width // 128), axis=1)
    for h in range(y_ref.shape[0]):
        o_ref[:, h * width:(h + 1) * width] = (y_ref[h, :share, :].astype(F32) * r).astype(BF16)


def scaled_rows(y, per=4):
    heads, rows, hd = y.shape
    share = rows - EXTRA
    return pl.pallas_call(
        scale_kernel,
        grid=(heads // per,),
        in_specs=[pl.BlockSpec((per, rows, hd), lambda i: (i, 0, 0)),
                  pl.BlockSpec((heads, EXTRA, hd), lambda i: (0, share // EXTRA, 0))],
        out_specs=pl.BlockSpec((share, per * hd), lambda i: (0, i)),
        out_shape=jax.ShapeDtypeStruct((share, heads * hd), BF16),
        scratch_shapes=[pltpu.VMEM((LANES, 128), F32)],
        name="scale_rows",
    )(y, y)


def layer(queries, key_vectors, value_vectors, step_sizes, w_in, w_up, w_out, out_gate, norm_gain):
    rows, _ = queries.shape
    n_ctx, n_head = lax.axis_size("ctx"), lax.axis_size("head")
    z_size = n_ctx // 2
    ctx = lax.axis_index("ctx")
    pos = jnp.stack([ctx >> 1, ctx & 1, lax.axis_index("head")]).astype(jnp.int32)
    tied = lax.optimization_barrier

    onward = [(i, i + 1) for i in range(n_ctx - 1)]
    k_before = lax.ppermute(key_vectors[rows - WINDOW:], "ctx", onward)
    v_before = lax.ppermute(value_vectors[rows - WINDOW:], "ctx", onward)

    keep, send, w_slice = increments(pos, key_vectors, value_vectors, step_sizes, w_in, w_up, w_out, z_size)
    partner = [(i, i ^ 1) for i in range(n_ctx)]

    def along_z(d):
        return [(i, ((i // 2 + d) % z_size) * 2 + i % 2) for i in range(n_ctx)]

    got = lax.ppermute(send, "ctx", partner)
    parts = pair_sum(pos, keep, got, z_size)
    order = sorted(range(1, z_size), key=lambda d: -min(d, z_size - d))
    arrived = [lax.ppermute(parts[d], "ctx", along_z(d)) for d in order]
    q_own, own_part = tied((queries, parts[0]))
    attended = attention_own(q_own, key_vectors, value_vectors)
    attended, arrived = tied((attended, arrived))
    new_piece = renormed(w_slice, [own_part] + arrived)
    rest = [lax.ppermute(new_piece, "ctx", along_z(d)) for d in order]
    q_first, own_piece = tied((queries, new_piece))
    attended = attention_first(pos, q_first, k_before, v_before, key_vectors, value_vectors, attended)
    attended, rest = tied((attended, rest))
    chip = [own_piece] + rest
    other = [lax.ppermute(p, "ctx", partner) for p in chip]

    y = applied(pos, queries, attended, out_gate, norm_gain.reshape(1, -1), chip + other, n_head)
    y = lax.all_to_all(y, "head", split_axis=0, concat_axis=0, tiled=True)
    return scaled_rows(y)


def solution(mesh):
    return jax.shard_map(
        layer,
        mesh=mesh,
        in_specs=(
            P("ctx", "head"), P("ctx", "head"), P("ctx", "head"), P("head", "ctx"),
            P("head", None, None), P("head", None, None), P("head", None, None),
            P("ctx", "head"), P(),
        ),
        out_specs=P(("ctx", "head"), None),
        check_vma=False,
    )
```

profile of v0, /device:TPU:1, one launch (start us, length us, event | category | flops | bytes accessed | tf_op | source)
XLA Modules:
  0.0 145.7 jit_solution(7409089390860970391)
XLA Ops:
  0.0 0.6 pad_add_fusion.pos
  0.6 16.8 %increments.1 = (bf16[3,256,512]{2,1,0:T(8,128)(2,1)}, bf16[3,256,512]{2,1,0:T(8,128)(2,1)}, bf16[3,64,512]{2,1,0:T(8,128)(2,1)}) custom-call(s32[3]{0:T(128)} %pad_add_fusion.pos, bf16[3072,512]{1,0:T(8,128)(2,1)} %k_ref.5, bf16[3072,512]{1,0:T(8,128)(2,1)} %v_ref.5, f32[1,3072]{1,0:T(1,128)} %rate_ref.1, bf16[1,512,512]{2,1,0:T(8,128)(2,1)} %wi_ref.1, ...), custom_call_target="tpu_custom_call" | custom-call | flops 9663676416 | bytes 9437184 | tf_op jit(solution)/shard_map/increments/pallas_call | solution.py:84
  17.4 1.4 collective-permute-start
  18.8 2.3 %slice.7 = bf16[1024,512]{1,0:T(8,128)(2,1)} slice(bf16[3072,512]{1,0:T(8,128)(2,1)} %v_ref.5), slice={[2048:3072], [0:512]} | slice | bytes 2097152 | tf_op jit(solution)/shard_map/slice | solution.py:354
  21.1 3.5 %collective-permute-start.5 = (bf16[1024,512]{1,0:T(8,128)(2,1)}, bf16[1024,512]{1,0:T(8,128)(2,1)S(1)}, u32[]{:S(2)}, u32[]{:S(2)}) collective-permute-start(bf16[1024,512]{1,0:T(8,128)(2,1)} %slice.7), channel_id=1, source_target_pairs={{0,16},{16,32},{32,48},{48,64},{64,80},{80,96},{96,112},{1,17},{17... | collective-permute-start | bytes 3145736 | tf_op jit(solution)/shard_map/ppermute | solution.py:354
  24.6 1.3 slice.6
  25.9 2.4 %collective-permute-start.4 = (bf16[1024,512]{1,0:T(8,128)(2,1)S(1)}, bf16[1024,512]{1,0:T(8,128)(2,1)S(1)}, u32[]{:S(2)}, u32[]{:S(2)}) collective-permute-start(bf16[1024,512]{1,0:T(8,128)(2,1)S(1)} %slice.6), channel_id=1, source_target_pairs={{0,16},{16,32},{32,48},{48,64},{64,80},{80,96},{96,112},{1,17},{17... | collective-permute-start | bytes 3145736 | tf_op jit(solution)/shard_map/ppermute | solution.py:353
  28.3 0.0 collective-permute-done.got_ref
  28.4 3.0 %pair_sum.1 = (bf16[3,64,512]{2,1,0:T(8,128)(2,1)}, bf16[3,64,512]{2,1,0:T(8,128)(2,1)}, bf16[3,64,512]{2,1,0:T(8,128)(2,1)}, bf16[3,64,512]{2,1,0:T(8,128)(2,1)}) custom-call(s32[3]{0:T(128)} %pad_add_fusion.pos, bf16[3,256,512]{2,1,0:T(8,128)(2,1)} %get-tuple-element.25.keep_ref, bf16[3,256,512]{2,1,0:T(8,128)(2,1)} %collective-permute-done.got_ref), custom_call_target="tpu_custom_call" | custom-call | tf_op jit(solution)/shard_map/pair_sum/pallas_call | solution.py:115
  31.4 3.3 %collective-permute-start.1 = (bf16[3,64,512]{2,1,0:T(8,128)(2,1)}, bf16[3,64,512]{2,1,0:T(8,128)(2,1)S(1)}, u32[]{:S(2)}, u32[]{:S(2)}) collective-permute-start(bf16[3,64,512]{2,1,0:T(8,128)(2,1)} %get-tuple-element.30), channel_id=1, source_target_pairs={{0,64},{16,80},{32,96},{48,112},{64,0},{80,16},{96,32},{112,48},{1... | collective-permute-start | bytes 589832 | tf_op jit(solution)/shard_map/ppermute | solution.py:365
  34.7 0.0 collective-permute-start.2
  34.7 2.7 %collective-permute-start.3 = (bf16[3,64,512]{2,1,0:T(8,128)(2,1)}, bf16[3,64,512]{2,1,0:T(8,128)(2,1)}, u32[]{:S(2)}, u32[]{:S(2)}) collective-permute-start(bf16[3,64,512]{2,1,0:T(8,128)(2,1)} %get-tuple-element.32), channel_id=1, source_target_pairs={{0,96},{16,112},{32,0},{48,16},{64,32},{80,48},{96,64},{112,80},{1... | collective-permute-start | bytes 589832 | tf_op jit(solution)/shard_map/ppermute | solution.py:365
  37.4 14.3 %attention_own.1._ = bf16[3072,512]{1,0:T(8,128)(2,1)} custom-call(bf16[3072,512]{1,0:T(8,128)(2,1)} %q_ref.3, bf16[3072,512]{1,0:T(8,128)(2,1)} %k_ref.5, bf16[3072,512]{1,0:T(8,128)(2,1)} %v_ref.5), custom_call_target="tpu_custom_call" | custom-call | flops 5368709120 | bytes 10485760 | tf_op jit(solution)/shard_map/attention_own/pallas_call | solution.py:219
  51.7 6.2 %collective-permute-done.1.refs_1_ = bf16[3,64,512]{2,1,0:T(8,128)(2,1)S(1)} collective-permute-done((bf16[3,64,512]{2,1,0:T(8,128)(2,1)}, bf16[3,64,512]{2,1,0:T(8,128)(2,1)S(1)}, u32[]{:S(2)}, u32[]{:S(2)}) %collective-permute-start.1) | collective-permute-done | bytes 196640 | tf_op jit(solution)/shard_map/ppermute | solution.py:365
  57.9 0.0 copy-start.2
  57.9 0.0 collective-permute-done.2.refs_2_
  57.9 0.0 collective-permute-done.3.refs_3_
  57.9 0.7 copy-done.2
  58.5 0.1 copy-done.3
  58.6 2.2 %renorm.1.refs_0_ = bf16[3,64,512]{2,1,0:T(8,128)(2,1)} custom-call(bf16[3,64,512]{2,1,0:T(8,128)(2,1)} %get-tuple-element.24.w_ref, bf16[3,64,512]{2,1,0:T(8,128)(2,1)} %get-tuple-element.28.refs_0_, bf16[3,64,512]{2,1,0:T(8,128)(2,1)} %copy-done.2, bf16[3,64,512]{2,1,0:T(8,128)(2,1)} %copy-done.3, bf16[3,64,512]{2,1,0:T(8,128)(2,1)} %collective-permute-done.3.refs_3_), custom_call_target="tpu_custom_call" | custom-call | tf_op jit(solution)/shard_map/renorm/pallas_call | solution.py:141
  60.8 4.5 %collective-permute-start.8 = (bf16[3,64,512]{2,1,0:T(8,128)(2,1)}, bf16[3,64,512]{2,1,0:T(8,128)(2,1)S(1)}, u32[]{:S(2)}, u32[]{:S(2)}) collective-permute-start(bf16[3,64,512]{2,1,0:T(8,128)(2,1)} %renorm.1.refs_0_), channel_id=1, source_target_pairs={{0,96},{16,112},{32,0},{48,16},{64,32},{80,48},{96,64},{112,80},{1... | collective-permute-start | bytes 589832 | tf_op jit(solution)/shard_map/ppermute | solution.py:370
  65.4 0.0 collective-permute-start.7
  65.4 1.2 collective-permute-start.6
  66.6 0.0 collective-permute-done.5.vb_ref
  66.6 0.0 collective-permute-start.9
  66.6 0.0 collective-permute-done.4.kb_ref
  66.6 1.0 copy-done
  67.6 1.0 copy-done.1
  68.5 9.4 %attention_first.1.attended_ref = bf16[3072,512]{1,0:T(8,128)(2,1)} custom-call(s32[3]{0:T(128)} %pad_add_fusion.pos, bf16[3072,512]{1,0:T(8,128)(2,1)} %q_ref.3, bf16[1024,512]{1,0:T(8,128)(2,1)} %copy-done.1, bf16[1024,512]{1,0:T(8,128)(2,1)} %copy-done, bf16[3072,512]{1,0:T(8,128)(2,1)} %k_ref.5, ...), custom_call_target="tpu_custom_call", output_to_operand_aliasing={{}: (6, {})} | custom-call | flops 2684354560 | bytes 6291456 | tf_op jit(solution)/shard_map/attention_first/pallas_call | solution.py:236
  78.0 0.0 collective-permute-done.8.refs_3_
  78.0 0.0 collective-permute-done.7.refs_2_
  78.0 0.0 copy-start.5
  78.0 0.0 collective-permute-done.6.refs_1_
  78.0 0.1 collective-permute-start.10
  78.1 0.5 collective-permute-start.11
  78.6 0.1 collective-permute-start.12
  78.7 0.0 collective-permute-done.9.refs_4_
  78.7 1.0 collective-permute-done.10.refs_5_
  79.7 0.3 collective-permute-done.11.refs_6_
  80.0 0.3 collective-permute-done.12.refs_7_
  80.3 0.0 copy-done.4
  80.3 0.0 copy-done.5
  80.3 0.1 copy-done.6
  80.4 0.3 copy-done.7
  80.7 0.3 copy-done.8
  81.0 13.0 %apply_fast.1 = bf16[16,200,512]{2,1,0:T(8,128)(2,1)} custom-call(s32[3]{0:T(128)} %pad_add_fusion.pos, bf16[3072,512]{1,0:T(8,128)(2,1)} %q_ref.3, bf16[3072,512]{1,0:T(8,128)(2,1)} %attention_first.1.attended_ref, bf16[3072,512]{1,0:T(8,128)(2,1)} %gate_ref.1, f32[1,8192]{1,0:T(1,128)} %bitcast.4, bf16[3,64,512]{2,1,0:T(8,128)(2,1)} %renorm.1.refs_0_, ...), custom_call_target="tpu_custom_call" | custom-call | flops 4831838208 | bytes 14680064 | tf_op jit(solution)/shard_map/apply_fast/pallas_call | solution.py:295
  94.0 47.2 %all_to_all.5.y_ref.squares_ref = bf16[16,200,512]{2,1,0:T(8,128)(2,1)} all-to-all(bf16[16,200,512]{2,1,0:T(8,128)(2,1)} %apply_fast.1), channel_id=1, replica_groups=mesh['ctx'=8,'head'=16] {'head'}, dimensions={0} | all-to-all | bytes 6553600 | tf_op jit(solution)/shard_map/all_to_all | solution.py:378
  141.2 4.5 %scale_rows.1 = bf16[192,8192]{1,0:T(8,128)(2,1)} custom-call(bf16[16,200,512]{2,1,0:T(8,128)(2,1)} %all_to_all.5.y_ref.squares_ref, bf16[16,200,512]{2,1,0:T(8,128)(2,1)} %all_to_all.5.y_ref.squares_ref), custom_call_target="tpu_custom_call" | custom-call | tf_op jit(solution)/shard_map/scale_rows/pallas_call | solution.py:332
  (7 shorter events, 0.0 us)
Async XLA Ops:
  17.4 11.0 %collective-permute-start = (bf16[3,256,512]{2,1,0:T(8,128)(2,1)}, bf16[3,256,512]{2,1,0:T(8,128)(2,1)}, u32[]{:S(2)}, u32[]{:S(2)}) collective-permute-start(bf16[3,256,512]{2,1,0:T(8,128)(2,1)} %get-tuple-element.26), channel_id=1, source_target_pairs={{0,16},{16,0},{32,48},{48,32},{64,80},{80,64},{96,112},{112,96},{1... | collective-permute-start | bytes 2359304 | tf_op jit(solution)/shard_map/ppermute | solution.py:362
  21.1 45.5 %collective-permute-start.5 = (bf16[1024,512]{1,0:T(8,128)(2,1)}, bf16[1024,512]{1,0:T(8,128)(2,1)S(1)}, u32[]{:S(2)}, u32[]{:S(2)}) collective-permute-start(bf16[1024,512]{1,0:T(8,128)(2,1)} %slice.7), channel_id=1, source_target_pairs={{0,16},{16,32},{32,48},{48,64},{64,80},{80,96},{96,112},{1,17},{17... | collective-permute-start | bytes 3145736 | tf_op jit(solution)/shard_map/ppermute | solution.py:354
  25.9 40.6 %collective-permute-start.4 = (bf16[1024,512]{1,0:T(8,128)(2,1)S(1)}, bf16[1024,512]{1,0:T(8,128)(2,1)S(1)}, u32[]{:S(2)}, u32[]{:S(2)}) collective-permute-start(bf16[1024,512]{1,0:T(8,128)(2,1)S(1)} %slice.6), channel_id=1, source_target_pairs={{0,16},{16,32},{32,48},{48,64},{64,80},{80,96},{96,112},{1,17},{17... | collective-permute-start | bytes 3145736 | tf_op jit(solution)/shard_map/ppermute | solution.py:353
  31.4 26.5 %collective-permute-start.1 = (bf16[3,64,512]{2,1,0:T(8,128)(2,1)}, bf16[3,64,512]{2,1,0:T(8,128)(2,1)S(1)}, u32[]{:S(2)}, u32[]{:S(2)}) collective-permute-start(bf16[3,64,512]{2,1,0:T(8,128)(2,1)} %get-tuple-element.30), channel_id=1, source_target_pairs={{0,64},{16,80},{32,96},{48,112},{64,0},{80,16},{96,32},{112,48},{1... | collective-permute-start | bytes 589832 | tf_op jit(solution)/shard_map/ppermute | solution.py:365
  34.7 23.2 %collective-permute-start.2 = (bf16[3,64,512]{2,1,0:T(8,128)(2,1)}, bf16[3,64,512]{2,1,0:T(8,128)(2,1)S(1)}, u32[]{:S(2)}, u32[]{:S(2)}) collective-permute-start(bf16[3,64,512]{2,1,0:T(8,128)(2,1)} %get-tuple-element.31), channel_id=1, source_target_pairs={{0,32},{16,48},{32,64},{48,80},{64,96},{80,112},{96,0},{112,16},{1... | collective-permute-start | bytes 589832 | tf_op jit(solution)/shard_map/ppermute | solution.py:365
  34.7 23.2 %collective-permute-start.3 = (bf16[3,64,512]{2,1,0:T(8,128)(2,1)}, bf16[3,64,512]{2,1,0:T(8,128)(2,1)}, u32[]{:S(2)}, u32[]{:S(2)}) collective-permute-start(bf16[3,64,512]{2,1,0:T(8,128)(2,1)} %get-tuple-element.32), channel_id=1, source_target_pairs={{0,96},{16,112},{32,0},{48,16},{64,32},{80,48},{96,64},{112,80},{1... | collective-permute-start | bytes 589832 | tf_op jit(solution)/shard_map/ppermute | solution.py:365
  57.9 0.7 copy-start.2
  57.9 0.7 copy-start.3
  60.8 17.1 %collective-permute-start.8 = (bf16[3,64,512]{2,1,0:T(8,128)(2,1)}, bf16[3,64,512]{2,1,0:T(8,128)(2,1)S(1)}, u32[]{:S(2)}, u32[]{:S(2)}) collective-permute-start(bf16[3,64,512]{2,1,0:T(8,128)(2,1)} %renorm.1.refs_0_), channel_id=1, source_target_pairs={{0,96},{16,112},{32,0},{48,16},{64,32},{80,48},{96,64},{112,80},{1... | collective-permute-start | bytes 589832 | tf_op jit(solution)/shard_map/ppermute | solution.py:370
  65.4 12.6 %collective-permute-start.7 = (bf16[3,64,512]{2,1,0:T(8,128)(2,1)}, bf16[3,64,512]{2,1,0:T(8,128)(2,1)S(1)}, u32[]{:S(2)}, u32[]{:S(2)}) collective-permute-start(bf16[3,64,512]{2,1,0:T(8,128)(2,1)} %renorm.1.refs_0_), channel_id=1, source_target_pairs={{0,32},{16,48},{32,64},{48,80},{64,96},{80,112},{96,0},{112,16},{1... | collective-permute-start | bytes 589832 | tf_op jit(solution)/shard_map/ppermute | solution.py:370
  65.4 12.6 %collective-permute-start.6 = (bf16[3,64,512]{2,1,0:T(8,128)(2,1)}, bf16[3,64,512]{2,1,0:T(8,128)(2,1)}, u32[]{:S(2)}, u32[]{:S(2)}) collective-permute-start(bf16[3,64,512]{2,1,0:T(8,128)(2,1)} %renorm.1.refs_0_), channel_id=1, source_target_pairs={{0,64},{16,80},{32,96},{48,112},{64,0},{80,16},{96,32},{112,48},{1... | collective-permute-start | bytes 589832 | tf_op jit(solution)/shard_map/ppermute | solution.py:370
  66.6 1.0 copy-start
  66.6 12.1 %collective-permute-start.9 = (bf16[3,64,512]{2,1,0:T(8,128)(2,1)}, bf16[3,64,512]{2,1,0:T(8,128)(2,1)}, u32[]{:S(2)}, u32[]{:S(2)}) collective-permute-start(bf16[3,64,512]{2,1,0:T(8,128)(2,1)} %renorm.1.refs_0_), channel_id=1, source_target_pairs={{0,16},{16,0},{32,48},{48,32},{64,80},{80,64},{96,112},{112,96},{1... | collective-permute-start | bytes 589832 | tf_op jit(solution)/shard_map/ppermute | solution.py:375
  67.6 1.0 copy-start.1
  78.0 2.3 %copy-start.4 = (bf16[3,64,512]{2,1,0:T(8,128)(2,1)}, bf16[3,64,512]{2,1,0:T(8,128)(2,1)S(1)}, u32[]{:S(2)}) copy-start(bf16[3,64,512]{2,1,0:T(8,128)(2,1)S(1)} %collective-permute-done.8.refs_3_) | copy-start | bytes 589828
  78.0 2.3 %copy-start.5 = (bf16[3,64,512]{2,1,0:T(8,128)(2,1)}, bf16[3,64,512]{2,1,0:T(8,128)(2,1)S(1)}, u32[]{:S(2)}) copy-start(bf16[3,64,512]{2,1,0:T(8,128)(2,1)S(1)} %collective-permute-done.7.refs_2_) | copy-start | bytes 589828
  78.0 1.7 %collective-permute-start.10 = (bf16[3,64,512]{2,1,0:T(8,128)(2,1)}, bf16[3,64,512]{2,1,0:T(8,128)(2,1)S(1)}, u32[]{:S(2)}, u32[]{:S(2)}) collective-permute-start(bf16[3,64,512]{2,1,0:T(8,128)(2,1)} %collective-permute-done.6.refs_1_), channel_id=1, source_target_pairs={{0,16},{16,0},{32,48},{48,32},{64,80},{80,64},{96,112},{112,96},{1... | collective-permute-start | bytes 589832 | tf_op jit(solution)/shard_map/ppermute | solution.py:375
  78.1 1.9 %collective-permute-start.11 = (bf16[3,64,512]{2,1,0:T(8,128)(2,1)S(1)}, bf16[3,64,512]{2,1,0:T(8,128)(2,1)S(1)}, u32[]{:S(2)}, u32[]{:S(2)}) collective-permute-start(bf16[3,64,512]{2,1,0:T(8,128)(2,1)S(1)} %collective-permute-done.7.refs_2_), channel_id=1, source_target_pairs={{0,16},{16,0},{32,48},{48,32},{64,80},{80,64},{96,112},{112,96},{1... | collective-permute-start | bytes 589832 | tf_op jit(solution)/shard_map/ppermute | solution.py:375
  78.6 1.7 %collective-permute-start.12 = (bf16[3,64,512]{2,1,0:T(8,128)(2,1)S(1)}, bf16[3,64,512]{2,1,0:T(8,128)(2,1)S(1)}, u32[]{:S(2)}, u32[]{:S(2)}) collective-permute-start(bf16[3,64,512]{2,1,0:T(8,128)(2,1)S(1)} %collective-permute-done.8.refs_3_), channel_id=1, source_target_pairs={{0,16},{16,0},{32,48},{48,32},{64,80},{80,64},{96,112},{112,96},{1... | collective-permute-start | bytes 589832 | tf_op jit(solution)/shard_map/ppermute | solution.py:375
  79.7 0.7 copy-start.6
  80.0 0.7 copy-start.7
  80.3 0.7 copy-start.8
where the time goes:
time: 147 us; the launch traced here: 146 us
  Pallas kernels  63.3 us (43%)
  blocking collectives  47.2 us (32%)
  starting transfers between devices  19.7 us (13%)
  waiting for transfers between devices  7.81 us (5%)
  local copies, waits for them, and re-layouts  6.95 us (5%)
    all_to_all x1, blocking collectives, layer(): y = lax.all_to_all(y, 'head', split_axis=0, concat_axis=0, tiled=True)  47.2 us
    pallas_call x1, Pallas kernels, increments(): pl.pallas_call(increments_kernel, grid_spec=pltpu.PrefetchScalarGridSpec(...  16.8 us
    pallas_call x1, Pallas kernels, attention_own(): pl.pallas_call(functools.partial(attention_own_kernel, tq=tq, skip=skip,...  14.3 us
    pallas_call x1, Pallas kernels, applied(): pl.pallas_call(apply_kernel, grid_spec=pltpu.PrefetchScalarGridSpec(num_s...  13 us
    pallas_call x1, Pallas kernels, attention_first(): pl.pallas_call(functools.partial(attention_first_kernel, tq=tq, scale=sca...  9.44 us
    ppermute x3, waiting for transfers between devices, layer(): arrived = [lax.ppermute(parts[d], 'ctx', along_z(d)) for d in order]  6.19 us
    ppermute x3, starting transfers between devices, layer(): arrived = [lax.ppermute(parts[d], 'ctx', along_z(d)) for d in order]  5.98 us
    ppermute x3, starting transfers between devices, layer(): rest = [lax.ppermute(new_piece, 'ctx', along_z(d)) for d in order]  5.71 us
  transfers between devices with their start and end apart: 13, of which 4 were waited for; matrix products, arithmetic and copies ran while one was open for 2% of the time, Pallas kernels for 20%

commit v1 on v0

v1 whole, which is shorter than its diff:
```python
import functools

import jax
import jax.numpy as jnp
from jax import lax
from jax.experimental import pallas as pl
from jax.experimental.pallas import tpu as pltpu
from jax.sharding import PartitionSpec as P


WINDOW = 1024
EPSILON = 1e-06
LOG2E = 1.4426950408889634


F32 = jnp.float32
BF16 = jnp.bfloat16
NT = (((1,), (1,)), ((), ()))


def sigmoid(x):
    return 0.5 * jnp.tanh(0.5 * x) + 0.5


def silu(x):
    half = 0.5 * x
    return half * jnp.tanh(half) + half


def dot_nt(a, b):
    return lax.dot_general(a, b, NT, preferred_element_type=F32)


def dot_nn(a, b):
    return jnp.dot(a, b, preferred_element_type=F32)


def whole(shape):
    return pl.BlockSpec(shape, lambda *_: (0,) * len(shape))


def increments_kernel(table, k_ref, v_ref, rate_ref, wi_ref, wu_ref, wo_ref,
                      keep_ref, send_ref, slice_ref, wt, acc):
    step = pl.program_id(0)
    tile = k_ref.shape[0]

    @pl.when(step == 0)
    def _():
        wt[0] = wi_ref[0].T
        wt[1] = wu_ref[0].T
        wt[2] = wo_ref[0].T

    k = k_ref[...]
    rate = jnp.broadcast_to(rate_ref[...], (128, tile)).T
    rate = jnp.concatenate([rate] * (v_ref.shape[1] // 128), axis=1)
    scaled = (rate * v_ref[...].astype(F32)).astype(BF16)
    gate = dot_nt(wt[0], k)
    up = dot_nt(wt[1], k)
    back = dot_nt(wt[2], scaled)
    sig = sigmoid(gate)
    act = gate * sig
    hidden = (act * up).astype(BF16)
    grad_gate = (back * up * (sig + act * (1.0 - sig))).astype(BF16)
    grad_up = (back * act).astype(BF16)
    first = step == 0
    acc[0] = jnp.where(first, 0.0, acc[0]) + dot_nn(grad_gate, k)
    acc[1] = jnp.where(first, 0.0, acc[1]) + dot_nn(grad_up, k)
    acc[2] = jnp.where(first, 0.0, acc[2]) + dot_nn(hidden, scaled)

    @pl.when(step == pl.num_programs(0) - 1)
    def _():
        half = keep_ref.shape[1]
        part = slice_ref.shape[1]
        mine = pl.multiple_of(table[CORE_AT] * half, half)
        other = pl.multiple_of((1 - table[CORE_AT]) * half, half)
        keep_ref[...] = acc[:, pl.ds(mine, half), :].astype(BF16)
        send_ref[...] = acc[:, pl.ds(other, half), :].astype(BF16)
        own = pl.multiple_of(table[CORE_AT] * half + table[Z_AT] * part, part)
        slice_ref[...] = wt[:, pl.ds(own, part), :]


def increments(table, k, v, rate, w_in, w_up, w_out, z_size):
    rows, hd = k.shape
    fh = w_in.shape[2]
    tile = 512
    half, part = fh // 2, fh // 2 // z_size
    row_spec = pl.BlockSpec((tile, hd), lambda i, *_: (i, 0))
    w_spec = whole((1, hd, fh))
    return pl.pallas_call(
        increments_kernel,
        grid_spec=pltpu.PrefetchScalarGridSpec(
            num_scalar_prefetch=1,
            grid=(rows // tile,),
            in_specs=[row_spec, row_spec, pl.BlockSpec((1, tile), lambda i, *_: (0, i)),
                      w_spec, w_spec, w_spec],
            out_specs=[whole((3, half, hd)), whole((3, half, hd)), whole((3, part, hd))],
            scratch_shapes=[pltpu.VMEM((3, fh, hd), BF16), pltpu.VMEM((3, fh, hd), F32)],
        ),
        out_shape=[jax.ShapeDtypeStruct((3, half, hd), BF16),
                   jax.ShapeDtypeStruct((3, half, hd), BF16),
                   jax.ShapeDtypeStruct((3, part, hd), BF16)],
        cost_estimate=pl.CostEstimate(flops=12 * rows * hd * fh, bytes_accessed=9 << 20,
                                      transcendentals=rows * fh),
        compiler_params=pltpu.CompilerParams(vmem_limit_bytes=28 << 20),
        name="increments",
    )(table, k, v, rate, w_in, w_up, w_out)


def pair_sum_kernel(table, keep_ref, got_ref, *outs):
    count = len(outs)
    part = outs[0].shape[1]
    for d in range(count):
        at = pl.multiple_of(lax.rem(table[Z_AT] + d, count) * part, part)
        rows = pl.ds(at, part)
        outs[d][...] = (keep_ref[:, rows, :].astype(F32) + got_ref[:, rows, :].astype(F32)).astype(BF16)


def pair_sum(table, keep, got, z_size):
    three, half, hd = keep.shape
    part = half // z_size
    return pl.pallas_call(
        pair_sum_kernel,
        grid_spec=pltpu.PrefetchScalarGridSpec(
            num_scalar_prefetch=1, grid=(1,),
            in_specs=[whole(keep.shape)] * 2,
            out_specs=[whole((three, part, hd))] * z_size,
        ),
        out_shape=[jax.ShapeDtypeStruct((three, part, hd), BF16)] * z_size,
        compiler_params=pltpu.CompilerParams(vmem_limit_bytes=8 << 20),
        name="pair_sum",
    )(table, keep, got)


def renorm_kernel(w_ref, *refs):
    parts, out_ref = refs[:-1], refs[-1]
    w = w_ref[...].astype(F32)
    total = parts[0][...].astype(F32)
    for p in parts[1:]:
        total = total + p[...].astype(F32)
    updated = w + total
    size = w.shape[-1]
    before = jnp.sum(w * w, axis=-1, keepdims=True) / size + EPSILON
    after = jnp.sum(updated * updated, axis=-1, keepdims=True) / size + EPSILON
    out_ref[...] = (updated * (jnp.sqrt(before) / jnp.sqrt(after))).astype(BF16)


def renormed(w, parts):
    return pl.pallas_call(
        renorm_kernel,
        out_shape=jax.ShapeDtypeStruct(w.shape, BF16),
        compiler_params=pltpu.CompilerParams(vmem_limit_bytes=8 << 20),
        name="renorm",
    )(w, *parts)


SIDE = 4
SHIFTS = ((1, 1), (3, 3), (2, 2), (1, 3), (3, 1), (2, 1), (1, 2), (3, 2),
          (2, 3), (2, 0), (0, 2), (1, 0), (0, 1), (3, 0), (0, 3), (0, 0))
GROUPS = (2, 4, 4, 6)
Z_AT, CORE_AT, HEAD_AT, TARGET_AT = 0, 1, 2, 3
SOURCE_AT = TARGET_AT + len(SHIFTS)


def shifted(h, dx, dy):
    return (h // SIDE + dx) % SIDE * SIDE + (h + dy) % SIDE


def load_kernel(*refs, count):
    ins, outs, (tail_ref, table, sems) = refs[:count], refs[count:2 * count], refs[2 * count:]
    rows = ins[0].shape[0]
    late, early = pl.ds(rows - WINDOW, WINDOW), pl.ds(0, rows - WINDOW)

    def moved(src, dst, n):
        c = pltpu.make_async_copy(src, dst, sems.at[n])
        c.start()
        return c

    firsts = [moved(ins[n].at[late], outs[n].at[late], n) for n in range(2)]
    rest = [moved(ins[n].at[early], outs[n].at[early], 2 + n) for n in range(2)]
    rest += [moved(ins[n], outs[n], 2 + n) for n in range(2, count)]
    ctx, head = lax.axis_index("ctx"), lax.axis_index("head")
    table[Z_AT], table[CORE_AT], table[HEAD_AT] = ctx // 2, ctx % 2, head
    for n, (dx, dy) in enumerate(SHIFTS):
        table[TARGET_AT + n] = shifted(head, dx, dy)
        table[SOURCE_AT + n] = shifted(head, SIDE - dx, SIDE - dy)
    for n, c in enumerate(firsts):
        c.wait()
        rest.append(moved(outs[n].at[late], tail_ref.at[n], 2 + count + n))
    for c in rest:
        c.wait()


def loaded(*arrays):
    _, hd = arrays[0].shape
    count = len(arrays)
    anywhere = pl.BlockSpec(memory_space=pl.ANY)
    return pl.pallas_call(
        functools.partial(load_kernel, count=count),
        in_specs=[anywhere] * count,
        out_specs=[pl.BlockSpec(memory_space=pltpu.VMEM)] * count
        + [anywhere, pl.BlockSpec(memory_space=pltpu.SMEM)],
        out_shape=[pltpu.VMEM(a.shape, a.dtype) for a in arrays]
        + [jax.ShapeDtypeStruct((2, WINDOW, hd), BF16), jax.ShapeDtypeStruct((SOURCE_AT + len(SHIFTS),), jnp.int32)],
        scratch_shapes=[pltpu.SemaphoreType.DMA((4 + count,))],
        compiler_params=pltpu.CompilerParams(vmem_limit_bytes=54 << 20),
        name="load_rows",
    )(*arrays)


def attend_rows(q, k, v, lo, scale):
    tq, span = q.shape[0], k.shape[0]
    row = lax.broadcasted_iota(jnp.int32, (tq, tq), 0)
    col = lax.broadcasted_iota(jnp.int32, (tq, tq), 1)
    s = dot_nt(q, k)
    if lo is not None:
        s = jnp.where(lax.broadcasted_iota(jnp.int32, (tq, span), 1) >= lo, s, -1e30)
    parts = [jnp.where(col > row, s[:, :tq], -1e30), s[:, tq:WINDOW], jnp.where(col <= row, s[:, WINDOW:], -1e30)]
    top = jnp.maximum(jnp.max(jnp.maximum(parts[0], parts[2]), axis=1, keepdims=True),
                      jnp.max(parts[1], axis=1, keepdims=True)) * scale
    p = jnp.concatenate([jnp.exp2(x * scale - top) for x in parts], axis=1)
    total = jnp.sum(p, axis=1, keepdims=True)
    return dot_nn(p.astype(BF16), v) * (1.0 / total)


def attention_own_kernel(q_ref, k_ref, v_ref, *refs, tq, skip, scale):
    o_ref = refs[-1]
    per = q_ref.shape[0] // tq
    for n in range(per):
        base = pl.multiple_of((pl.program_id(0) + skip) * per * tq + n * tq - WINDOW, tq)
        rows = slice(n * tq, (n + 1) * tq)
        keys = pl.ds(base, WINDOW + tq)
        o_ref[rows, :] = attend_rows(q_ref[rows, :], k_ref[keys, :], v_ref[keys, :], None, scale).astype(BF16)


def attention_first_kernel(table, q_ref, b_ref, k_ref, v_ref, _, o_ref, ek, ev, sems, *, tq, scale):
    step = pl.program_id(0)

    @pl.when(step == 0)
    def _():
        copies = [
            pltpu.make_async_copy(b_ref.at[0], ek.at[pl.ds(0, WINDOW)], sems.at[0]),
            pltpu.make_async_copy(k_ref.at[pl.ds(0, WINDOW)], ek.at[pl.ds(WINDOW, WINDOW)], sems.at[1]),
            pltpu.make_async_copy(b_ref.at[1], ev.at[pl.ds(0, WINDOW)], sems.at[2]),
            pltpu.make_async_copy(v_ref.at[pl.ds(0, WINDOW)], ev.at[pl.ds(WINDOW, WINDOW)], sems.at[3]),
        ]
        for c in copies:
            c.start()
        for c in copies:
            c.wait()

    limit = jnp.where(table[Z_AT] + table[CORE_AT] == 0, WINDOW, 0)
    per = q_ref.shape[0] // tq
    for n in range(per):
        base = pl.multiple_of(step * per * tq + n * tq, tq)
        rows = slice(n * tq, (n + 1) * tq)
        keys = pl.ds(base, WINDOW + tq)
        o_ref[rows, :] = attend_rows(q_ref[rows, :], ek[keys, :], ev[keys, :], limit - base, scale).astype(BF16)


def attention_own(q, k, v, start, stop, attended=None, tq=256, tile=512):
    rows, hd = q.shape
    skip = start // tile
    scale = hd ** -0.5 * LOG2E
    count = (stop - start) // tile
    tile_spec = pl.BlockSpec((tile, hd), lambda i: (i + skip, 0))
    into = [] if attended is None else [attended]
    return pl.pallas_call(
        functools.partial(attention_own_kernel, tq=tq, skip=skip, scale=scale),
        grid=(count,),
        in_specs=[tile_spec, whole((rows, hd)), whole((rows, hd))] + [pl.BlockSpec(memory_space=pl.ANY)] * len(into),
        out_specs=tile_spec,
        out_shape=jax.ShapeDtypeStruct((rows, hd), BF16),
        input_output_aliases={3: 0} if into else {},
        cost_estimate=pl.CostEstimate(flops=4 * count * tile * (WINDOW + tq) * hd,
                                      bytes_accessed=10 << 20, transcendentals=count * tile * WINDOW),
        compiler_params=pltpu.CompilerParams(vmem_limit_bytes=24 << 20),
        name="attention_own",
    )(q, k, v, *into)


def attention_first(table, q, before, k, v, attended, tq=256, tile=512):
    hd = q.shape[1]
    scale = hd ** -0.5 * LOG2E
    count = WINDOW // tile
    tile_spec = pl.BlockSpec((tile, hd), lambda i, *_: (i, 0))
    return pl.pallas_call(
        functools.partial(attention_first_kernel, tq=tq, scale=scale),
        grid_spec=pltpu.PrefetchScalarGridSpec(
            num_scalar_prefetch=1, grid=(count,),
            in_specs=[tile_spec] + [pl.BlockSpec(memory_space=pl.ANY)] * 4,
            out_specs=tile_spec,
            scratch_shapes=[pltpu.VMEM((2 * WINDOW, hd), BF16)] * 2 + [pltpu.SemaphoreType.DMA((4,))],
        ),
        out_shape=jax.ShapeDtypeStruct(attended.shape, BF16),
        input_output_aliases={5: 0},
        cost_estimate=pl.CostEstimate(flops=4 * WINDOW * (WINDOW + tq) * hd,
                                      bytes_accessed=6 << 20, transcendentals=WINDOW * WINDOW),
        compiler_params=pltpu.CompilerParams(vmem_limit_bytes=20 << 20),
        name="attention_first",
    )(table, q, before, k, v, attended)


EXTRA = 8
LANES = 256


def apply_kernel(*refs, count, n_pieces):
    refs = refs[1:]
    q_refs, attended_refs, gate_refs = refs[:count], refs[count:2 * count], refs[2 * count:3 * count]
    gain_ref, weights, outs = refs[3 * count], refs[3 * count + 1:3 * count + 1 + n_pieces], refs[3 * count + 1 + n_pieces:]
    if n_pieces > 1:
        wt, start = outs[-1], 0
        for p in weights:
            wt[:, start:start + p.shape[1], :] = p[...]
            start += p.shape[1]
    else:
        wt = weights[0]
    share = q_refs[0].shape[1]
    q = jnp.concatenate([r[0] for r in q_refs], axis=0)
    hidden = (silu(dot_nt(q, wt[0])) * dot_nt(q, wt[1])).astype(BF16)
    fast = dot_nn(hidden, wt[2])
    for n in range(count):
        rows = slice(n * share, (n + 1) * share)
        head = (attended_refs[n][0].astype(F32) + fast[rows]).astype(BF16).astype(F32)
        squares = jnp.sum(head * head, axis=1, keepdims=True)
        y = outs[n]
        y[:share, :] = (head * (gain_ref[...] * silu(gate_refs[n][0].astype(F32)))).astype(BF16)
        column = jnp.concatenate([squares, jnp.zeros((LANES - share, 1), F32)], axis=0)
        line = jnp.broadcast_to(column, (LANES, 128)).T[:EXTRA, :]
        high = line.astype(BF16)
        low = (line - high.astype(F32)).astype(BF16)
        y[share:, :LANES] = high
        y[share:, LANES:] = low


def applied(table, q, attended, out_gate, gain, weights, n_head, at, count):
    rows, hd = q.shape
    share = rows // n_head
    fh = sum(p.shape[1] for p in weights)
    blocks = [a.reshape(n_head, share, hd) for a in (q, attended, out_gate)]
    specs = [pl.BlockSpec((1, share, hd), lambda i, t, j=TARGET_AT + at + j: (t[j], 0, 0)) for j in range(count)]
    first = len(weights) > 1
    outs = [jax.ShapeDtypeStruct((share + EXTRA, hd), BF16)] * count
    outs += [jax.ShapeDtypeStruct((3, fh, hd), BF16)] * first
    return pl.pallas_call(
        functools.partial(apply_kernel, count=count, n_pieces=len(weights)),
        grid_spec=pltpu.PrefetchScalarGridSpec(
            num_scalar_prefetch=1, grid=(1,),
            in_specs=specs * 3 + [pl.BlockSpec((1, hd), lambda i, t: (0, t[HEAD_AT]))] + [whole(p.shape) for p in weights],
            out_specs=[whole(o.shape) for o in outs],
        ),
        out_shape=outs,
        cost_estimate=pl.CostEstimate(flops=6 * count * share * hd * fh, bytes_accessed=count << 20,
                                      transcendentals=2 * count * share * fh),
        compiler_params=pltpu.CompilerParams(vmem_limit_bytes=18 << 20),
        name="apply_fast",
    )(table, *[b for b in blocks for _ in range(count)], gain, *weights)


def scale_kernel(table, *refs):
    count = (len(refs) - 2) // 1 - 1
    y_refs, (o_ref, buf, sems) = refs[:count], refs[count:]
    share, width = buf.shape[1:]
    s = y_refs[0][share:, :].astype(F32)
    for y in y_refs[1:]:
        s = s + y[share:, :].astype(F32)
    line = s[:, :LANES] + s[:, LANES:]
    r = lax.rsqrt(line / (count * width) + EPSILON)
    r = jnp.concatenate([r] * (128 // EXTRA), axis=0).T[:share, :]
    r = jnp.concatenate([r] * (width // 128), axis=1)
    copies = []
    for n in range(count):
        buf[n] = (y_refs[n][:share, :].astype(F32) * r).astype(BF16)
        columns = pl.ds(pl.multiple_of(table[SOURCE_AT + n] * width, width), width)
        copies.append(pltpu.make_async_copy(buf.at[n], o_ref.at[:, columns], sems.at[n]))
        copies[-1].start()
    for c in copies:
        c.wait()


def scaled_rows(table, parts):
    rows, hd = parts[0].shape
    share, count = rows - EXTRA, len(parts)
    return pl.pallas_call(
        scale_kernel,
        grid_spec=pltpu.PrefetchScalarGridSpec(
            num_scalar_prefetch=1, grid=(1,),
            in_specs=[whole((rows, hd))] * count,
            out_specs=pl.BlockSpec(memory_space=pl.ANY),
            scratch_shapes=[pltpu.VMEM((count, share, hd), BF16), pltpu.SemaphoreType.DMA((count,))],
        ),
        out_shape=jax.ShapeDtypeStruct((share, count * hd), BF16),
        compiler_params=pltpu.CompilerParams(vmem_limit_bytes=16 << 20),
        name="scale_rows",
    )(table, *parts)


def layer(queries, key_vectors, value_vectors, step_sizes, w_in, w_up, w_out, out_gate, norm_gain):
    rows, _ = queries.shape
    n_ctx, n_head = lax.axis_size("ctx"), lax.axis_size("head")
    z_size = n_ctx // 2
    tied = lax.optimization_barrier

    key_vectors, value_vectors, w_in, w_up, w_out, tail, table = loaded(key_vectors, value_vectors, w_in, w_up, w_out)
    before = lax.ppermute(tail, "ctx", [(i, i + 1) for i in range(n_ctx - 1)])
    keep, send, w_slice = increments(table, key_vectors, value_vectors, step_sizes, w_in, w_up, w_out, z_size)
    partner = [(i, i ^ 1) for i in range(n_ctx)]

    def along_z(d):
        return [(i, ((i // 2 + d) % z_size) * 2 + i % 2) for i in range(n_ctx)]

    got = lax.ppermute(send, "ctx", partner)
    parts = pair_sum(table, keep, got, z_size)
    order = sorted(range(1, z_size), key=lambda d: -min(d, z_size - d))
    arrived = [lax.ppermute(parts[d], "ctx", along_z(d)) for d in order]
    q_own, own_part = tied((queries, parts[0]))
    cut = rows - WINDOW // 2
    attended = attention_own(q_own, key_vectors, value_vectors, WINDOW, cut)
    attended, arrived = tied((attended, arrived))
    new_piece = renormed(w_slice, [own_part] + arrived)
    rest = [lax.ppermute(new_piece, "ctx", along_z(d)) for d in order]
    q_first, own_piece = tied((queries, new_piece))
    attended = attention_own(q_first, key_vectors, value_vectors, cut, rows, attended)
    attended = attention_first(table, q_first, before, key_vectors, value_vectors, attended)
    attended, rest = tied((attended, rest))
    chip = [own_piece] + rest
    other = [lax.ppermute(p, "ctx", partner) for p in chip]

    weights, gain = chip + other, norm_gain.reshape(1, -1)
    parts, at = [], 0
    for count in GROUPS:
        outs = applied(table, queries, attended, out_gate, gain, weights, n_head, at, count)
        if len(outs) > count:
            weights = outs[count:]
        for y, (dx, dy) in zip(outs, SHIFTS[at:at + count]):
            if dx or dy:
                y = lax.ppermute(y, "head", [(h, shifted(h, dx, dy)) for h in range(n_head)])
            parts.append(y)
        at += count
    return scaled_rows(table, parts)


def solution(mesh):
    return jax.shard_map(
        layer,
        mesh=mesh,
        in_specs=(
            P("ctx", "head"), P("ctx", "head"), P("ctx", "head"), P("head", "ctx"),
            P("head", None, None), P("head", None, None), P("head", None, None),
            P("ctx", "head"), P(),
        ),
        out_specs=P(("ctx", "head"), None),
        check_vma=False,
    )
```

time: 147 us -> 120 us (0.82)
  the two profiles are of different devices: /device:TPU:1 before, /device:TPU:0 now
where the time goes in v1:
time: 120 us
  starting transfers between devices  63 us (52%)
  Pallas kernels  46.7 us (39%)
  waiting for transfers between devices  9.63 us (8%)
    ppermute x15, starting transfers between devices, layer(): lax.ppermute(y, 'head', [(h, shifted(h, dx, dy)) for h in range(n_head)])  44 us
    pallas_call x1, Pallas kernels, increments(): pl.pallas_call(increments_kernel, grid_spec=pltpu.PrefetchScalarGridSpec(...  13 us
    pallas_call x4, Pallas kernels, applied(): pl.pallas_call(functools.partial(apply_kernel, count=count, n_pieces=len(...  11.4 us
    pallas_call x2, Pallas kernels, attention_own(): pl.pallas_call(functools.partial(attention_own_kernel, tq=tq, skip=skip,...  8.87 us
    ppermute x3, starting transfers between devices, layer(): arrived = [lax.ppermute(parts[d], 'ctx', along_z(d)) for d in order]  6.9 us
    ppermute x15, waiting for transfers between devices, layer(): lax.ppermute(y, 'head', [(h, shifted(h, dx, dy)) for h in range(n_head)])  6.3 us
    pallas_call x1, Pallas kernels, attention_first(): pl.pallas_call(functools.partial(attention_first_kernel, tq=tq, scale=sca...  5.35 us
    pallas_call x1, Pallas kernels, loaded(): pl.pallas_call(functools.partial(load_kernel, count=count), in_specs=[any...  4.57 us
  transfers between devices with their start and end apart: 27, of which 7 were waited for; matrix products, arithmetic and copies ran while one was open for 0% of the time, Pallas kernels for 31%

profile of v1, /device:TPU:0, one launch (start us, length us, event | category | flops | bytes accessed | tf_op | source)
XLA Modules:
  0.0 120.3 jit_solution(4719960686307183208)
XLA Ops:
  0.0 4.6 %load_rows.1 = (bf16[3072,512]{1,0:T(8,128)(2,1)S(1)}, bf16[3072,512]{1,0:T(8,128)(2,1)S(1)}, bf16[1,512,512]{2,1,0:T(8,128)(2,1)S(1)}, bf16[1,512,512]{2,1,0:T(...) custom-call(bf16[3072,512]{1,0:T(8,128)(2,1)} %refs_0_.1, ...), custom_call_target="tpu_custom_call" | custom-call | tf_op jit(solution)/shard_map/load_rows/pallas_call | solution.py:197
  4.6 1.4 %collective-permute-start.4 = (bf16[2,1024,512]{2,1,0:T(8,128)(2,1)}, bf16[2,1024,512]{2,1,0:T(8,128)(2,1)S(1)}, u32[]{:S(2)}, u32[]{:S(2)}) collective-permute-start(bf16[2,1024,512]{2,1,0:T(8,128)(2,1)} %get-tuple-element.67), channel_id=1, source_target_pairs={{0,16},{16,32},{32,48},{48,64},{64,80},{80,96},{96,112},{1,17},{17... | collective-permute-start | bytes 6291464 | tf_op jit(solution)/shard_map/ppermute | solution.py:405
  6.0 0.6 copy-done.3
  6.6 13.0 %increments.1 = (bf16[3,256,512]{2,1,0:T(8,128)(2,1)S(1)}, bf16[3,256,512]{2,1,0:T(8,128)(2,1)S(1)}, bf16[3,64,512]{2,1,0:T(8,128)(2,1)S(1)}) custom-call(s32[35]{0:T(128)S(1)} %copy-done.3, bf16[3072,512]{1,0:T(8,128)(2,1)S(1)} %get-tuple-element.49.k_ref, bf16[3072,512]{1,0:T(8,128)(2,1)S(1)} %get-tuple-element.50.v_ref, f32[1,3072]{1,0:T(1,128)S(1)} %copy-done.5, ...), custom_call_target="tpu_custom_call" | custom-call | flops 9663676416 | bytes 9437184 | tf_op jit(solution)/shard_map/increments/pallas_call | solution.py:89
  19.7 2.7 %collective-permute-start = (bf16[3,256,512]{2,1,0:T(8,128)(2,1)S(1)}, bf16[3,256,512]{2,1,0:T(8,128)(2,1)S(1)}, u32[]{:S(2)}, u32[]{:S(2)}) collective-permute-start(bf16[3,256,512]{2,1,0:T(8,128)(2,1)S(1)} %get-tuple-element.56), channel_id=1, source_target_pairs={{0,16},{16,0},{32,48},{48,32},{64,80},{80,64},{96,112},{112,96},{1... | collective-permute-start | bytes 2359304 | tf_op jit(solution)/shard_map/ppermute | solution.py:412
  22.4 1.9 %collective-permute-done.got_ref = bf16[3,256,512]{2,1,0:T(8,128)(2,1)S(1)} collective-permute-done((bf16[3,256,512]{2,1,0:T(8,128)(2,1)S(1)}, bf16[3,256,512]{2,1,0:T(8,128)(2,1)S(1)}, u32[]{:S(2)}, u32[]{:S(2)}) %collective-permute-start) | collective-permute-done | bytes 786464 | tf_op jit(solution)/shard_map/ppermute | solution.py:412
  24.3 0.8 pair_sum.1
  25.1 3.7 %collective-permute-start.1 = (bf16[3,64,512]{2,1,0:T(8,128)(2,1)S(1)}, bf16[3,64,512]{2,1,0:T(8,128)(2,1)S(1)}, u32[]{:S(2)}, u32[]{:S(2)}) collective-permute-start(bf16[3,64,512]{2,1,0:T(8,128)(2,1)S(1)} %get-tuple-element.60), channel_id=1, source_target_pairs={{0,64},{16,80},{32,96},{48,112},{64,0},{80,16},{96,32},{112,48},{1... | collective-permute-start | bytes 589832 | tf_op jit(solution)/shard_map/ppermute | solution.py:415
  28.7 0.0 collective-permute-start.2
  28.7 3.2 %collective-permute-start.3 = (bf16[3,64,512]{2,1,0:T(8,128)(2,1)S(1)}, bf16[3,64,512]{2,1,0:T(8,128)(2,1)S(1)}, u32[]{:S(2)}, u32[]{:S(2)}) collective-permute-start(bf16[3,64,512]{2,1,0:T(8,128)(2,1)S(1)} %get-tuple-element.62), channel_id=1, source_target_pairs={{0,96},{16,112},{32,0},{48,16},{64,32},{80,48},{96,64},{112,80},{1... | collective-permute-start | bytes 589832 | tf_op jit(solution)/shard_map/ppermute | solution.py:415
  32.0 6.7 %attention_own.2.refs_0_ = bf16[3072,512]{1,0:T(8,128)(2,1)S(1)} custom-call(bf16[3072,512]{1,0:T(8,128)(2,1)S(1)} %copy-done, bf16[3072,512]{1,0:T(8,128)(2,1)S(1)} %get-tuple-element.49.k_ref, bf16[3072,512]{1,0:T(8,128)(2,1)S(1)} %get-tuple-element.50.v_ref), custom_call_target="tpu_custom_call" | custom-call | flops 4026531840 | bytes 10485760 | tf_op jit(solution)/shard_map/attention_own/pallas_call | solution.py:267
  38.6 0.0 collective-permute-done.2.refs_2_
  38.7 0.3 renorm.1.refs_8_
  38.9 1.8 %collective-permute-start.7 = (bf16[3,64,512]{2,1,0:T(8,128)(2,1)S(1)}, bf16[3,64,512]{2,1,0:T(8,128)(2,1)S(1)}, u32[]{:S(2)}, u32[]{:S(2)}) collective-permute-start(bf16[3,64,512]{2,1,0:T(8,128)(2,1)S(1)} %renorm.1.refs_8_), channel_id=1, source_target_pairs={{0,96},{16,112},{32,0},{48,16},{64,32},{80,48},{96,64},{112,80},{1... | collective-permute-start | bytes 589832 | tf_op jit(solution)/shard_map/ppermute | solution.py:421
  40.8 0.4 collective-permute-start.6
  41.1 2.0 %collective-permute-start.5 = (bf16[3,64,512]{2,1,0:T(8,128)(2,1)S(1)}, bf16[3,64,512]{2,1,0:T(8,128)(2,1)S(1)}, u32[]{:S(2)}, u32[]{:S(2)}) collective-permute-start(bf16[3,64,512]{2,1,0:T(8,128)(2,1)S(1)} %renorm.1.refs_8_), channel_id=1, source_target_pairs={{0,64},{16,80},{32,96},{48,112},{64,0},{80,16},{96,32},{112,48},{1... | collective-permute-start | bytes 589832 | tf_op jit(solution)/shard_map/ppermute | solution.py:421
  43.1 3.1 %collective-permute-start.8 = (bf16[3,64,512]{2,1,0:T(8,128)(2,1)S(1)}, bf16[3,64,512]{2,1,0:T(8,128)(2,1)S(1)}, u32[]{:S(2)}, u32[]{:S(2)}) collective-permute-start(bf16[3,64,512]{2,1,0:T(8,128)(2,1)S(1)} %renorm.1.refs_8_), channel_id=1, source_target_pairs={{0,16},{16,0},{32,48},{48,32},{64,80},{80,64},{96,112},{112,96},{1... | collective-permute-start | bytes 589832 | tf_op jit(solution)/shard_map/ppermute | solution.py:427
  46.2 2.2 %attention_own.3._ = bf16[3072,512]{1,0:T(8,128)(2,1)S(1)} custom-call(bf16[3072,512]{1,0:T(8,128)(2,1)S(1)} %copy-done, bf16[3072,512]{1,0:T(8,128)(2,1)S(1)} %get-tuple-element.49.k_ref, bf16[3072,512]{1,0:T(8,128)(2,1)S(1)} %get-tuple-element.50.v_ref, bf16[3072,512]{1,0:T(8,128)(2,1)S(1)} %attention_own.2.refs_0_), custom_call_target="tpu_custom_call", output_to_operand_aliasing={{}: (3, {})} | custom-call | flops 1342177280 | bytes 10485760 | tf_op jit(solution)/shard_map/attention_own/pallas_call | solution.py:267
  48.4 0.0 copy-start.1
  48.5 0.0 copy-start.2
  48.5 5.3 %attention_first.1 = bf16[3072,512]{1,0:T(8,128)(2,1)S(1)} custom-call(s32[35]{0:T(128)S(1)} %copy-done.4, bf16[3072,512]{1,0:T(8,128)(2,1)S(1)} %copy-done, bf16[2,1024,512]{2,1,0:T(8,128)(2,1)S(1)} %collective-permute-done.4.b_ref, bf16[3072,512]{1,0:T(8,128)(2,1)S(1)} %get-tuple-element.49.k_ref, ...), custom_call_target="tpu_custom_call", output_to_operand_aliasing={{}: (5, {})} | custom-call | flops 2684354560 | bytes 6291456 | tf_op jit(solution)/shard_map/attention_first/pallas_call | solution.py:286
  53.9 0.1 collective-permute-start.9
  54.0 0.5 collective-permute-start.10
  54.5 0.1 collective-permute-start.11
  54.6 0.8 collective-permute-done.9.refs_13_
  55.4 0.3 collective-permute-done.10.refs_14_
  55.7 0.3 collective-permute-done.11.refs_15_
  56.0 1.8 %apply_fast.4 = (bf16[200,512]{1,0:T(8,128)(2,1)S(1)}, bf16[200,512]{1,0:T(8,128)(2,1)S(1)}, bf16[3,512,512]{2,1,0:T(8,128)(2,1)S(1)}) custom-call(s32[35]{0:T(128)S(1)} %copy-done.4, bf16[16,192,512]{2,1,0:T(8,128)(2,1)S(1)} %bitcast.4, bf16[16,192,512]{2,1,0:T(8,128)(2,1)S(1)} %bitcast.5, bf16[16,192,512]{2,1,0:T(8,128)(2,1)S(1)} %bitcast.20, ...), custom_call_target="tpu_custom_call" | custom-call | flops 603979776 | bytes 2097152 | tf_op jit(solution)/shard_map/apply_fast/pallas_call | solution.py:345
  57.8 2.6 %collective-permute-start.12 = (bf16[200,512]{1,0:T(8,128)(2,1)S(1)}, bf16[200,512]{1,0:T(8,128)(2,1)S(1)}, u32[]{:S(2)}, u32[]{:S(2)}) collective-permute-start(bf16[200,512]{1,0:T(8,128)(2,1)S(1)} %get-tuple-element.74), channel_id=1, source_target_pairs={{0,5},{1,6},{2,7},{3,4},{4,9},{5,10},{6,11},{7,8},{8,13},{9,14},{1... | collective-permute-start | bytes 614408 | tf_op jit(solution)/shard_map/ppermute | solution.py:437
  60.4 2.8 %collective-permute-start.13 = (bf16[200,512]{1,0:T(8,128)(2,1)S(1)}, bf16[200,512]{1,0:T(8,128)(2,1)S(1)}, u32[]{:S(2)}, u32[]{:S(2)}) collective-permute-start(bf16[200,512]{1,0:T(8,128)(2,1)S(1)} %get-tuple-element.75), channel_id=1, source_target_pairs={{0,15},{1,12},{2,13},{3,14},{4,3},{5,0},{6,1},{7,2},{8,7},{9,4},{1... | collective-permute-start | bytes 614408 | tf_op jit(solution)/shard_map/ppermute | solution.py:437
  63.2 2.8 %apply_fast.6 = (bf16[200,512]{1,0:T(8,128)(2,1)S(1)}, bf16[200,512]{1,0:T(8,128)(2,1)S(1)}, bf16[200,512]{1,0:T(8,128)(2,1)S(1)}, bf16[200,512]{1,0:T(8,128)(2,1)S(1)}) custom-call(s32[35]{0:T(128)S(1)} %copy-done.4, bf16[16,192,512]{2,1,0:T(8,128)(2,1)S(1)} %bitcast.6, bf16[16,192,512]{2,1,0:T(8,128)(2,1)S(1)} %bitcast.7, ...), custom_call_target="tpu_custom_call" | custom-call | flops 1207959552 | bytes 4194304 | tf_op jit(solution)/shard_map/apply_fast/pallas_call | solution.py:345
  66.0 1.7 %collective-permute-start.18 = (bf16[200,512]{1,0:T(8,128)(2,1)S(1)}, bf16[200,512]{1,0:T(8,128)(2,1)S(1)}, u32[]{:S(2)}, u32[]{:S(2)}) collective-permute-start(bf16[200,512]{1,0:T(8,128)(2,1)S(1)} %get-tuple-element.81), channel_id=1, source_target_pairs={{0,6},{1,7},{2,4},{3,5},{4,10},{5,11},{6,8},{7,9},{8,14},{9,15},{1... | collective-permute-start | bytes 614408 | tf_op jit(solution)/shard_map/ppermute | solution.py:437
  67.8 3.9 %collective-permute-start.19 = (bf16[200,512]{1,0:T(8,128)(2,1)S(1)}, bf16[200,512]{1,0:T(8,128)(2,1)S(1)}, u32[]{:S(2)}, u32[]{:S(2)}) collective-permute-start(bf16[200,512]{1,0:T(8,128)(2,1)S(1)} %get-tuple-element.82), channel_id=1, source_target_pairs={{0,14},{1,15},{2,12},{3,13},{4,2},{5,3},{6,0},{7,1},{8,6},{9,7},{1... | collective-permute-start | bytes 614408 | tf_op jit(solution)/shard_map/ppermute | solution.py:437
  71.7 1.8 %collective-permute-start.20 = (bf16[200,512]{1,0:T(8,128)(2,1)S(1)}, bf16[200,512]{1,0:T(8,128)(2,1)S(1)}, u32[]{:S(2)}, u32[]{:S(2)}) collective-permute-start(bf16[200,512]{1,0:T(8,128)(2,1)S(1)} %get-tuple-element.83), channel_id=1, source_target_pairs={{0,11},{1,8},{2,9},{3,10},{4,15},{5,12},{6,13},{7,14},{8,3},{9,0},... | collective-permute-start | bytes 614408 | tf_op jit(solution)/shard_map/ppermute | solution.py:437
  73.6 2.8 %apply_fast.5 = (bf16[200,512]{1,0:T(8,128)(2,1)S(1)}, bf16[200,512]{1,0:T(8,128)(2,1)S(1)}, bf16[200,512]{1,0:T(8,128)(2,1)S(1)}, bf16[200,512]{1,0:T(8,128)(2,1)S(1)}) custom-call(s32[35]{0:T(128)S(1)} %copy-done.4, bf16[16,192,512]{2,1,0:T(8,128)(2,1)S(1)} %bitcast.10, bf16[16,192,512]{2,1,0:T(8,128)(2,1)S(1)} %bitcast.11, ...), custom_call_target="tpu_custom_call" | custom-call | flops 1207959552 | bytes 4194304 | tf_op jit(solution)/shard_map/apply_fast/pallas_call | solution.py:345
  76.4 3.0 %collective-permute-start.21 = (bf16[200,512]{1,0:T(8,128)(2,1)S(1)}, bf16[200,512]{1,0:T(8,128)(2,1)S(1)}, u32[]{:S(2)}, u32[]{:S(2)}) collective-permute-start(bf16[200,512]{1,0:T(8,128)(2,1)S(1)} %get-tuple-element.84), channel_id=1, source_target_pairs={{0,8},{1,9},{2,10},{3,11},{4,12},{5,13},{6,14},{7,15},{8,0},{9,1},... | collective-permute-start | bytes 614408 | tf_op jit(solution)/shard_map/ppermute | solution.py:437
  79.4 0.7 collective-permute-start.14
  80.1 0.5 collective-permute-done.18.refs_6_
  80.6 1.8 %collective-permute-start.15 = (bf16[200,512]{1,0:T(8,128)(2,1)S(1)}, bf16[200,512]{1,0:T(8,128)(2,1)S(1)}, u32[]{:S(2)}, u32[]{:S(2)}) collective-permute-start(bf16[200,512]{1,0:T(8,128)(2,1)S(1)} %get-tuple-element.78), channel_id=1, source_target_pairs={{0,7},{1,4},{2,5},{3,6},{4,11},{5,8},{6,9},{7,10},{8,15},{9,12},{1... | collective-permute-start | bytes 614408 | tf_op jit(solution)/shard_map/ppermute | solution.py:437
  82.4 8.9 %collective-permute-start.16 = (bf16[200,512]{1,0:T(8,128)(2,1)S(1)}, bf16[200,512]{1,0:T(8,128)(2,1)S(1)}, u32[]{:S(2)}, u32[]{:S(2)}) collective-permute-start(bf16[200,512]{1,0:T(8,128)(2,1)S(1)} %get-tuple-element.79), channel_id=1, source_target_pairs={{0,13},{1,14},{2,15},{3,12},{4,1},{5,2},{6,3},{7,0},{8,5},{9,6},{1... | collective-permute-start | bytes 614408 | tf_op jit(solution)/shard_map/ppermute | solution.py:437
  91.3 3.9 %apply_fast.7 = (bf16[200,512]{1,0:T(8,128)(2,1)S(1)}, bf16[200,512]{1,0:T(8,128)(2,1)S(1)}, bf16[200,512]{1,0:T(8,128)(2,1)S(1)}, bf16[200,512]{1,0:T(8,128)(2,...) custom-call(s32[35]{0:T(128)S(1)} %copy-done.4, bf16[16,192,512]{2,1,0:T(8,128)(2,1)S(1)} %bitcast.14, ...), custom_call_target="tpu_custom_call" | custom-call | flops 1811939328 | bytes 6291456 | tf_op jit(solution)/shard_map/apply_fast/pallas_call | solution.py:345
  95.2 5.4 %collective-permute-start.22 = (bf16[200,512]{1,0:T(8,128)(2,1)S(1)}, bf16[200,512]{1,0:T(8,128)(2,1)S(1)}, u32[]{:S(2)}, u32[]{:S(2)}) collective-permute-start(bf16[200,512]{1,0:T(8,128)(2,1)S(1)} %get-tuple-element.85), channel_id=1, source_target_pairs={{0,2},{1,3},{2,0},{3,1},{4,6},{5,7},{6,4},{7,5},{8,10},{9,11},{10,... | collective-permute-start | bytes 614408 | tf_op jit(solution)/shard_map/ppermute | solution.py:437
  100.6 2.1 %collective-permute-start.23 = (bf16[200,512]{1,0:T(8,128)(2,1)S(1)}, bf16[200,512]{1,0:T(8,128)(2,1)S(1)}, u32[]{:S(2)}, u32[]{:S(2)}) collective-permute-start(bf16[200,512]{1,0:T(8,128)(2,1)S(1)} %get-tuple-element.86), channel_id=1, source_target_pairs={{0,4},{1,5},{2,6},{3,7},{4,8},{5,9},{6,10},{7,11},{8,12},{9,13},{1... | collective-permute-start | bytes 614408 | tf_op jit(solution)/shard_map/ppermute | solution.py:437
  102.8 4.2 %collective-permute-start.24 = (bf16[200,512]{1,0:T(8,128)(2,1)S(1)}, bf16[200,512]{1,0:T(8,128)(2,1)S(1)}, u32[]{:S(2)}, u32[]{:S(2)}) collective-permute-start(bf16[200,512]{1,0:T(8,128)(2,1)S(1)} %get-tuple-element.87), channel_id=1, source_target_pairs={{0,1},{1,2},{2,3},{3,0},{4,5},{5,6},{6,7},{7,4},{8,9},{9,10},{10,1... | collective-permute-start | bytes 614408 | tf_op jit(solution)/shard_map/ppermute | solution.py:437
  107.0 4.9 %collective-permute-start.25 = (bf16[200,512]{1,0:T(8,128)(2,1)S(1)}, bf16[200,512]{1,0:T(8,128)(2,1)S(1)}, u32[]{:S(2)}, u32[]{:S(2)}) collective-permute-start(bf16[200,512]{1,0:T(8,128)(2,1)S(1)} %get-tuple-element.88), channel_id=1, source_target_pairs={{0,12},{1,13},{2,14},{3,15},{4,0},{5,1},{6,2},{7,3},{8,4},{9,5},{1... | collective-permute-start | bytes 614408 | tf_op jit(solution)/shard_map/ppermute | solution.py:437
  112.0 3.2 %collective-permute-done.25.refs_13_ = bf16[200,512]{1,0:T(8,128)(2,1)S(1)} collective-permute-done((bf16[200,512]{1,0:T(8,128)(2,1)S(1)}, bf16[200,512]{1,0:T(8,128)(2,1)S(1)}, u32[]{:S(2)}, u32[]{:S(2)}) %collective-permute-start.25) | collective-permute-done | bytes 204832 | tf_op jit(solution)/shard_map/ppermute | solution.py:437
  115.2 2.5 %collective-permute-done.26.refs_14_ = bf16[200,512]{1,0:T(8,128)(2,1)S(1)} collective-permute-done((bf16[200,512]{1,0:T(8,128)(2,1)S(1)}, bf16[200,512]{1,0:T(8,128)(2,1)S(1)}, u32[]{:S(2)}, u32[]{:S(2)}) %collective-permute-start.26) | collective-permute-done | bytes 204832 | tf_op jit(solution)/shard_map/ppermute | solution.py:437
  117.7 2.5 %scale_rows.1 = bf16[192,8192]{1,0:T(8,128)(2,1)} custom-call(s32[35]{0:T(128)S(1)} %copy-done.4, bf16[200,512]{1,0:T(8,128)(2,1)S(1)} %collective-permute-done.12.refs_0_, bf16[200,512]{1,0:T(8,128)(2,1)S(1)} %collective-permute-done.13.refs_1_, bf16[200,512]{1,0:T(8,128)(2,1)S(1)} %collective-permute-done.14.refs_2_, ...), custom_call_target="tpu_custom_call" | custom-call | tf_op jit(solution)/shard_map/scale_rows/pallas_call | solution.py:384
  (30 shorter events, 0.1 us)
Async XLA Ops:
  0.0 6.0 %copy-start.5 = (f32[1,3072]{1,0:T(1,128)S(1)}, f32[1,3072]{1,0:T(1,128)}, u32[]{:S(2)}) copy-start(f32[1,3072]{1,0:T(1,128)} %rate_ref.1) | copy-start | bytes 36868
  4.6 43.9 %collective-permute-start.4 = (bf16[2,1024,512]{2,1,0:T(8,128)(2,1)}, bf16[2,1024,512]{2,1,0:T(8,128)(2,1)S(1)}, u32[]{:S(2)}, u32[]{:S(2)}) collective-permute-start(bf16[2,1024,512]{2,1,0:T(8,128)(2,1)} %get-tuple-element.67), channel_id=1, source_target_pairs={{0,16},{16,32},{32,48},{48,64},{64,80},{80,96},{96,112},{1,17},{17... | collective-permute-start | bytes 6291464 | tf_op jit(solution)/shard_map/ppermute | solution.py:405
  6.0 0.6 copy-start.3
  6.6 25.3 %copy-start = (bf16[3072,512]{1,0:T(8,128)(2,1)S(1)}, bf16[3072,512]{1,0:T(8,128)(2,1)}, u32[]{:S(2)}) copy-start(bf16[3072,512]{1,0:T(8,128)(2,1)} %q_ref.2) | copy-start | bytes 9437188
  19.7 4.6 %collective-permute-start = (bf16[3,256,512]{2,1,0:T(8,128)(2,1)S(1)}, bf16[3,256,512]{2,1,0:T(8,128)(2,1)S(1)}, u32[]{:S(2)}, u32[]{:S(2)}) collective-permute-start(bf16[3,256,512]{2,1,0:T(8,128)(2,1)S(1)} %get-tuple-element.56), channel_id=1, source_target_pairs={{0,16},{16,0},{32,48},{48,32},{64,80},{80,64},{96,112},{112,96},{1... | collective-permute-start | bytes 2359304 | tf_op jit(solution)/shard_map/ppermute | solution.py:412
  25.1 13.6 %collective-permute-start.1 = (bf16[3,64,512]{2,1,0:T(8,128)(2,1)S(1)}, bf16[3,64,512]{2,1,0:T(8,128)(2,1)S(1)}, u32[]{:S(2)}, u32[]{:S(2)}) collective-permute-start(bf16[3,64,512]{2,1,0:T(8,128)(2,1)S(1)} %get-tuple-element.60), channel_id=1, source_target_pairs={{0,64},{16,80},{32,96},{48,112},{64,0},{80,16},{96,32},{112,48},{1... | collective-permute-start | bytes 589832 | tf_op jit(solution)/shard_map/ppermute | solution.py:415
  28.7 9.9 %collective-permute-start.2 = (bf16[3,64,512]{2,1,0:T(8,128)(2,1)S(1)}, bf16[3,64,512]{2,1,0:T(8,128)(2,1)S(1)}, u32[]{:S(2)}, u32[]{:S(2)}) collective-permute-start(bf16[3,64,512]{2,1,0:T(8,128)(2,1)S(1)} %get-tuple-element.61), channel_id=1, source_target_pairs={{0,32},{16,48},{32,64},{48,80},{64,96},{80,112},{96,0},{112,16},{1... | collective-permute-start | bytes 589832 | tf_op jit(solution)/shard_map/ppermute | solution.py:415
  28.7 9.9 %collective-permute-start.3 = (bf16[3,64,512]{2,1,0:T(8,128)(2,1)S(1)}, bf16[3,64,512]{2,1,0:T(8,128)(2,1)S(1)}, u32[]{:S(2)}, u32[]{:S(2)}) collective-permute-start(bf16[3,64,512]{2,1,0:T(8,128)(2,1)S(1)} %get-tuple-element.62), channel_id=1, source_target_pairs={{0,96},{16,112},{32,0},{48,16},{64,32},{80,48},{96,64},{112,80},{1... | collective-permute-start | bytes 589832 | tf_op jit(solution)/shard_map/ppermute | solution.py:415
  38.9 9.5 %copy-start.4 = (s32[35]{0:T(128)S(1)}, s32[35]{0:T(128)}, u32[]{:S(2)}) copy-start(s32[35]{0:T(128)} %get-tuple-element.48.table.refs_0_) | copy-start | bytes 424
  38.9 14.9 %collective-permute-start.7 = (bf16[3,64,512]{2,1,0:T(8,128)(2,1)S(1)}, bf16[3,64,512]{2,1,0:T(8,128)(2,1)S(1)}, u32[]{:S(2)}, u32[]{:S(2)}) collective-permute-start(bf16[3,64,512]{2,1,0:T(8,128)(2,1)S(1)} %renorm.1.refs_8_), channel_id=1, source_target_pairs={{0,96},{16,112},{32,0},{48,16},{64,32},{80,48},{96,64},{112,80},{1... | collective-permute-start | bytes 589832 | tf_op jit(solution)/shard_map/ppermute | solution.py:421
  40.8 13.1 %collective-permute-start.6 = (bf16[3,64,512]{2,1,0:T(8,128)(2,1)S(1)}, bf16[3,64,512]{2,1,0:T(8,128)(2,1)S(1)}, u32[]{:S(2)}, u32[]{:S(2)}) collective-permute-start(bf16[3,64,512]{2,1,0:T(8,128)(2,1)S(1)} %renorm.1.refs_8_), channel_id=1, source_target_pairs={{0,32},{16,48},{32,64},{48,80},{64,96},{80,112},{96,0},{112,16},{1... | collective-permute-start | bytes 589832 | tf_op jit(solution)/shard_map/ppermute | solution.py:421
  41.1 12.7 %collective-permute-start.5 = (bf16[3,64,512]{2,1,0:T(8,128)(2,1)S(1)}, bf16[3,64,512]{2,1,0:T(8,128)(2,1)S(1)}, u32[]{:S(2)}, u32[]{:S(2)}) collective-permute-start(bf16[3,64,512]{2,1,0:T(8,128)(2,1)S(1)} %renorm.1.refs_8_), channel_id=1, source_target_pairs={{0,64},{16,80},{32,96},{48,112},{64,0},{80,16},{96,32},{112,48},{1... | collective-permute-start | bytes 589832 | tf_op jit(solution)/shard_map/ppermute | solution.py:421
  43.1 11.4 %collective-permute-start.8 = (bf16[3,64,512]{2,1,0:T(8,128)(2,1)S(1)}, bf16[3,64,512]{2,1,0:T(8,128)(2,1)S(1)}, u32[]{:S(2)}, u32[]{:S(2)}) collective-permute-start(bf16[3,64,512]{2,1,0:T(8,128)(2,1)S(1)} %renorm.1.refs_8_), channel_id=1, source_target_pairs={{0,16},{16,0},{32,48},{48,32},{64,80},{80,64},{96,112},{112,96},{1... | collective-permute-start | bytes 589832 | tf_op jit(solution)/shard_map/ppermute | solution.py:427
  48.4 7.5 %copy-start.1 = (bf16[3072,512]{1,0:T(8,128)(2,1)S(1)}, bf16[3072,512]{1,0:T(8,128)(2,1)}, u32[]{:S(2)}) copy-start(bf16[3072,512]{1,0:T(8,128)(2,1)} %param.16) | copy-start | bytes 9437188
  48.5 7.5 %copy-start.2 = (f32[8192]{0:T(1024)S(1)}, f32[8192]{0:T(1024)}, u32[]{:S(2)}) copy-start(f32[8192]{0:T(1024)} %param.17) | copy-start | bytes 98308
  53.9 1.5 %collective-permute-start.9 = (bf16[3,64,512]{2,1,0:T(8,128)(2,1)S(1)}, bf16[3,64,512]{2,1,0:T(8,128)(2,1)S(1)}, u32[]{:S(2)}, u32[]{:S(2)}) collective-permute-start(bf16[3,64,512]{2,1,0:T(8,128)(2,1)S(1)} %collective-permute-done.5.refs_9_), channel_id=1, source_target_pairs={{0,16},{16,0},{32,48},{48,32},{64,80},{80,64},{96,112},{112,96},{1... | collective-permute-start | bytes 589832 | tf_op jit(solution)/shard_map/ppermute | solution.py:427
  54.0 1.7 %collective-permute-start.10 = (bf16[3,64,512]{2,1,0:T(8,128)(2,1)S(1)}, bf16[3,64,512]{2,1,0:T(8,128)(2,1)S(1)}, u32[]{:S(2)}, u32[]{:S(2)}) collective-permute-start(bf16[3,64,512]{2,1,0:T(8,128)(2,1)S(1)} %collective-permute-done.6.refs_10_), channel_id=1, source_target_pairs={{0,16},{16,0},{32,48},{48,32},{64,80},{80,64},{96,112},{112,96},{1... | collective-permute-start | bytes 589832 | tf_op jit(solution)/shard_map/ppermute | solution.py:427
  54.5 1.5 %collective-permute-start.11 = (bf16[3,64,512]{2,1,0:T(8,128)(2,1)S(1)}, bf16[3,64,512]{2,1,0:T(8,128)(2,1)S(1)}, u32[]{:S(2)}, u32[]{:S(2)}) collective-permute-start(bf16[3,64,512]{2,1,0:T(8,128)(2,1)S(1)} %collective-permute-done.7.refs_11_), channel_id=1, source_target_pairs={{0,16},{16,0},{32,48},{48,32},{64,80},{80,64},{96,112},{112,96},{1... | collective-permute-start | bytes 589832 | tf_op jit(solution)/shard_map/ppermute | solution.py:427
  57.8 18.6 %collective-permute-start.12 = (bf16[200,512]{1,0:T(8,128)(2,1)S(1)}, bf16[200,512]{1,0:T(8,128)(2,1)S(1)}, u32[]{:S(2)}, u32[]{:S(2)}) collective-permute-start(bf16[200,512]{1,0:T(8,128)(2,1)S(1)} %get-tuple-element.74), channel_id=1, source_target_pairs={{0,5},{1,6},{2,7},{3,4},{4,9},{5,10},{6,11},{7,8},{8,13},{9,14},{1... | collective-permute-start | bytes 614408 | tf_op jit(solution)/shard_map/ppermute | solution.py:437
  60.4 19.1 %collective-permute-start.13 = (bf16[200,512]{1,0:T(8,128)(2,1)S(1)}, bf16[200,512]{1,0:T(8,128)(2,1)S(1)}, u32[]{:S(2)}, u32[]{:S(2)}) collective-permute-start(bf16[200,512]{1,0:T(8,128)(2,1)S(1)} %get-tuple-element.75), channel_id=1, source_target_pairs={{0,15},{1,12},{2,13},{3,14},{4,3},{5,0},{6,1},{7,2},{8,7},{9,4},{1... | collective-permute-start | bytes 614408 | tf_op jit(solution)/shard_map/ppermute | solution.py:437
  66.0 14.6 %collective-permute-start.18 = (bf16[200,512]{1,0:T(8,128)(2,1)S(1)}, bf16[200,512]{1,0:T(8,128)(2,1)S(1)}, u32[]{:S(2)}, u32[]{:S(2)}) collective-permute-start(bf16[200,512]{1,0:T(8,128)(2,1)S(1)} %get-tuple-element.81), channel_id=1, source_target_pairs={{0,6},{1,7},{2,4},{3,5},{4,10},{5,11},{6,8},{7,9},{8,14},{9,15},{1... | collective-permute-start | bytes 614408 | tf_op jit(solution)/shard_map/ppermute | solution.py:437
  67.8 14.6 %collective-permute-start.19 = (bf16[200,512]{1,0:T(8,128)(2,1)S(1)}, bf16[200,512]{1,0:T(8,128)(2,1)S(1)}, u32[]{:S(2)}, u32[]{:S(2)}) collective-permute-start(bf16[200,512]{1,0:T(8,128)(2,1)S(1)} %get-tuple-element.82), channel_id=1, source_target_pairs={{0,14},{1,15},{2,12},{3,13},{4,2},{5,3},{6,0},{7,1},{8,6},{9,7},{1... | collective-permute-start | bytes 614408 | tf_op jit(solution)/shard_map/ppermute | solution.py:437
  71.7 19.5 %collective-permute-start.20 = (bf16[200,512]{1,0:T(8,128)(2,1)S(1)}, bf16[200,512]{1,0:T(8,128)(2,1)S(1)}, u32[]{:S(2)}, u32[]{:S(2)}) collective-permute-start(bf16[200,512]{1,0:T(8,128)(2,1)S(1)} %get-tuple-element.83), channel_id=1, source_target_pairs={{0,11},{1,8},{2,9},{3,10},{4,15},{5,12},{6,13},{7,14},{8,3},{9,0},... | collective-permute-start | bytes 614408 | tf_op jit(solution)/shard_map/ppermute | solution.py:437
  76.4 18.8 %collective-permute-start.21 = (bf16[200,512]{1,0:T(8,128)(2,1)S(1)}, bf16[200,512]{1,0:T(8,128)(2,1)S(1)}, u32[]{:S(2)}, u32[]{:S(2)}) collective-permute-start(bf16[200,512]{1,0:T(8,128)(2,1)S(1)} %get-tuple-element.84), channel_id=1, source_target_pairs={{0,8},{1,9},{2,10},{3,11},{4,12},{5,13},{6,14},{7,15},{8,0},{9,1},... | collective-permute-start | bytes 614408 | tf_op jit(solution)/shard_map/ppermute | solution.py:437
  79.4 21.2 %collective-permute-start.14 = (bf16[200,512]{1,0:T(8,128)(2,1)S(1)}, bf16[200,512]{1,0:T(8,128)(2,1)S(1)}, u32[]{:S(2)}, u32[]{:S(2)}) collective-permute-start(bf16[200,512]{1,0:T(8,128)(2,1)S(1)} %get-tuple-element.77), channel_id=1, source_target_pairs={{0,10},{1,11},{2,8},{3,9},{4,14},{5,15},{6,12},{7,13},{8,2},{9,3},... | collective-permute-start | bytes 614408 | tf_op jit(solution)/shard_map/ppermute | solution.py:437
  80.6 22.1 %collective-permute-start.15 = (bf16[200,512]{1,0:T(8,128)(2,1)S(1)}, bf16[200,512]{1,0:T(8,128)(2,1)S(1)}, u32[]{:S(2)}, u32[]{:S(2)}) collective-permute-start(bf16[200,512]{1,0:T(8,128)(2,1)S(1)} %get-tuple-element.78), channel_id=1, source_target_pairs={{0,7},{1,4},{2,5},{3,6},{4,11},{5,8},{6,9},{7,10},{8,15},{9,12},{1... | collective-permute-start | bytes 614408 | tf_op jit(solution)/shard_map/ppermute | solution.py:437
  82.4 24.6 %collective-permute-start.16 = (bf16[200,512]{1,0:T(8,128)(2,1)S(1)}, bf16[200,512]{1,0:T(8,128)(2,1)S(1)}, u32[]{:S(2)}, u32[]{:S(2)}) collective-permute-start(bf16[200,512]{1,0:T(8,128)(2,1)S(1)} %get-tuple-element.79), channel_id=1, source_target_pairs={{0,13},{1,14},{2,15},{3,12},{4,1},{5,2},{6,3},{7,0},{8,5},{9,6},{1... | collective-permute-start | bytes 614408 | tf_op jit(solution)/shard_map/ppermute | solution.py:437
  91.3 20.7 %collective-permute-start.17 = (bf16[200,512]{1,0:T(8,128)(2,1)S(1)}, bf16[200,512]{1,0:T(8,128)(2,1)S(1)}, u32[]{:S(2)}, u32[]{:S(2)}) collective-permute-start(bf16[200,512]{1,0:T(8,128)(2,1)S(1)} %get-tuple-element.80), channel_id=1, source_target_pairs={{0,9},{1,10},{2,11},{3,8},{4,13},{5,14},{6,15},{7,12},{8,1},{9,2},... | collective-permute-start | bytes 614408 | tf_op jit(solution)/shard_map/ppermute | solution.py:437
  95.2 16.7 %collective-permute-start.22 = (bf16[200,512]{1,0:T(8,128)(2,1)S(1)}, bf16[200,512]{1,0:T(8,128)(2,1)S(1)}, u32[]{:S(2)}, u32[]{:S(2)}) collective-permute-start(bf16[200,512]{1,0:T(8,128)(2,1)S(1)} %get-tuple-element.85), channel_id=1, source_target_pairs={{0,2},{1,3},{2,0},{3,1},{4,6},{5,7},{6,4},{7,5},{8,10},{9,11},{10,... | collective-permute-start | bytes 614408 | tf_op jit(solution)/shard_map/ppermute | solution.py:437
  100.6 11.3 %collective-permute-start.23 = (bf16[200,512]{1,0:T(8,128)(2,1)S(1)}, bf16[200,512]{1,0:T(8,128)(2,1)S(1)}, u32[]{:S(2)}, u32[]{:S(2)}) collective-permute-start(bf16[200,512]{1,0:T(8,128)(2,1)S(1)} %get-tuple-element.86), channel_id=1, source_target_pairs={{0,4},{1,5},{2,6},{3,7},{4,8},{5,9},{6,10},{7,11},{8,12},{9,13},{1... | collective-permute-start | bytes 614408 | tf_op jit(solution)/shard_map/ppermute | solution.py:437
  102.8 9.2 %collective-permute-start.24 = (bf16[200,512]{1,0:T(8,128)(2,1)S(1)}, bf16[200,512]{1,0:T(8,128)(2,1)S(1)}, u32[]{:S(2)}, u32[]{:S(2)}) collective-permute-start(bf16[200,512]{1,0:T(8,128)(2,1)S(1)} %get-tuple-element.87), channel_id=1, source_target_pairs={{0,1},{1,2},{2,3},{3,0},{4,5},{5,6},{6,7},{7,4},{8,9},{9,10},{10,1... | collective-permute-start | bytes 614408 | tf_op jit(solution)/shard_map/ppermute | solution.py:437
  107.0 8.2 %collective-permute-start.25 = (bf16[200,512]{1,0:T(8,128)(2,1)S(1)}, bf16[200,512]{1,0:T(8,128)(2,1)S(1)}, u32[]{:S(2)}, u32[]{:S(2)}) collective-permute-start(bf16[200,512]{1,0:T(8,128)(2,1)S(1)} %get-tuple-element.88), channel_id=1, source_target_pairs={{0,12},{1,13},{2,14},{3,15},{4,0},{5,1},{6,2},{7,3},{8,4},{9,5},{1... | collective-permute-start | bytes 614408 | tf_op jit(solution)/shard_map/ppermute | solution.py:437
  111.9 5.8 %collective-permute-start.26 = (bf16[200,512]{1,0:T(8,128)(2,1)S(1)}, bf16[200,512]{1,0:T(8,128)(2,1)S(1)}, u32[]{:S(2)}, u32[]{:S(2)}) collective-permute-start(bf16[200,512]{1,0:T(8,128)(2,1)S(1)} %get-tuple-element.89), channel_id=1, source_target_pairs={{0,3},{1,0},{2,1},{3,2},{4,7},{5,4},{6,5},{7,6},{8,11},{9,8},{10,9... | collective-permute-start | bytes 614408 | tf_op jit(solution)/shard_map/ppermute | solution.py:437

commit v2 on v1

v2 whole, which is shorter than its diff:
```python
import functools

import jax
import jax.numpy as jnp
from jax import lax
from jax.experimental import pallas as pl
from jax.experimental.pallas import tpu as pltpu
from jax.sharding import PartitionSpec as P


WINDOW = 1024
EPSILON = 1e-06
LOG2E = 1.4426950408889634


F32 = jnp.float32
BF16 = jnp.bfloat16
NT = (((1,), (1,)), ((), ()))


def sigmoid(x):
    return 0.5 * jnp.tanh(0.5 * x) + 0.5


def silu(x):
    half = 0.5 * x
    return half * jnp.tanh(half) + half


def dot_nt(a, b):
    return lax.dot_general(a, b, NT, preferred_element_type=F32)


def dot_nn(a, b):
    return jnp.dot(a, b, preferred_element_type=F32)


def whole(shape):
    return pl.BlockSpec(shape, lambda *_: (0,) * len(shape))


def position():
    ctx = lax.axis_index("ctx")
    return ctx // 2, ctx % 2


TILE = 512


STEP = 1024


def increments_kernel(k_hbm, v_hbm, rate_ref, wi_hbm, wu_hbm, wo_hbm,
                      keep_ref, send_ref, slice_ref, k_ref, v_ref, w, wt, acc, w_sems, sems):
    rows = k_ref.shape[0]
    loads = [pltpu.make_async_copy(src.at[0], w.at[n], w_sems.at[n]) for n, src in enumerate((wi_hbm, wu_hbm, wo_hbm))]

    def tile_loads(t):
        at = pl.ds(pl.multiple_of(t * TILE, TILE), TILE)
        return (pltpu.make_async_copy(k_hbm.at[at], k_ref.at[at], sems.at[2 * t]),
                pltpu.make_async_copy(v_hbm.at[at], v_ref.at[at], sems.at[2 * t + 1]))

    ahead = 2
    for c in loads:
        c.start()
    for t in range(ahead):
        for c in tile_loads(t):
            c.start()
    for n, c in enumerate(loads):
        c.wait()
        wt[n] = w[n].T
    for t in range(ahead, rows // TILE):
        for c in tile_loads(t):
            c.start()

    def one(t, carry):
        for n in range(STEP // TILE):
            for c in tile_loads(t * (STEP // TILE) + n):
                c.wait()
        at = pl.ds(pl.multiple_of(t * STEP, STEP), STEP)
        k = k_ref[at, :]
        rate = jnp.broadcast_to(rate_ref[:, at], (128, STEP)).T
        rate = jnp.concatenate([rate] * (v_ref.shape[1] // 128), axis=1)
        scaled = (rate * v_ref[at, :].astype(F32)).astype(BF16)
        gate = dot_nt(wt[0], k)
        up = dot_nt(wt[1], k)
        back = dot_nt(wt[2], scaled)
        sig = sigmoid(gate)
        act = gate * sig
        hidden = (act * up).astype(BF16)
        grad_gate = (back * up * (sig + act * (1.0 - sig))).astype(BF16)
        grad_up = (back * act).astype(BF16)
        first = t == 0
        acc[0] = jnp.where(first, 0.0, acc[0]) + dot_nn(grad_gate, k)
        acc[1] = jnp.where(first, 0.0, acc[1]) + dot_nn(grad_up, k)
        acc[2] = jnp.where(first, 0.0, acc[2]) + dot_nn(hidden, scaled)
        return carry

    lax.fori_loop(0, rows // STEP, one, 0)
    z, core = position()
    half, part = keep_ref.shape[1], slice_ref.shape[1]
    mine = pl.multiple_of(core * half, half)
    other = pl.multiple_of((1 - core) * half, half)
    send_ref[...] = acc[:, pl.ds(other, half), :].astype(BF16)
    keep_ref[...] = acc[:, pl.ds(mine, half), :].astype(BF16)
    slice_ref[...] = wt[:, pl.ds(pl.multiple_of(core * half + z * part, part), part), :]


def increments(k, v, rate, w_in, w_up, w_out, z_size):
    rows, hd = k.shape
    fh = w_in.shape[2]
    half, part = fh // 2, fh // 2 // z_size
    anywhere, inside = pl.BlockSpec(memory_space=pl.ANY), pl.BlockSpec(memory_space=pltpu.VMEM)
    return pl.pallas_call(
        increments_kernel,
        in_specs=[anywhere, anywhere, inside, anywhere, anywhere, anywhere],
        out_specs=[inside] * 5,
        out_shape=[pltpu.VMEM((3, half, hd), BF16), pltpu.VMEM((3, half, hd), BF16), pltpu.VMEM((3, part, hd), BF16),
                   pltpu.VMEM((rows, hd), BF16), pltpu.VMEM((rows, hd), BF16)],
        scratch_shapes=[pltpu.VMEM((3, hd, fh), BF16), pltpu.VMEM((3, fh, hd), BF16), pltpu.VMEM((3, fh, hd), F32),
                        pltpu.SemaphoreType.DMA((3,)), pltpu.SemaphoreType.DMA((2 * rows // TILE,))],
        cost_estimate=pl.CostEstimate(flops=12 * rows * hd * fh, bytes_accessed=9 << 20,
                                      transcendentals=rows * fh),
        compiler_params=pltpu.CompilerParams(vmem_limit_bytes=48 << 20),
        name="increments",
    )(k, v, rate, w_in, w_up, w_out)


def small_call(kernel, outs, *args):
    return pl.pallas_call(kernel, out_shape=outs, compiler_params=pltpu.CompilerParams(vmem_limit_bytes=8 << 20))(*args)


def pair_sum_kernel(keep_ref, got_ref, *outs):
    count = len(outs)
    part = outs[0].shape[1]
    z, _ = position()
    for d in range(count):
        rows = pl.ds(pl.multiple_of((z + d) % count * part, part), part)
        outs[d][...] = (keep_ref[:, rows, :].astype(F32) + got_ref[:, rows, :].astype(F32)).astype(BF16)


def pair_sum(keep, got, z_size):
    three, half, hd = keep.shape
    return small_call(pair_sum_kernel, [jax.ShapeDtypeStruct((three, half // z_size, hd), BF16)] * z_size,
                      keep, got)


def renorm_kernel(w_ref, *refs):
    parts, out_ref = refs[:-1], refs[-1]
    w = w_ref[...].astype(F32)
    total = parts[0][...].astype(F32)
    for p in parts[1:]:
        total = total + p[...].astype(F32)
    updated = w + total
    size = w.shape[-1]
    before = jnp.sum(w * w, axis=-1, keepdims=True) / size + EPSILON
    after = jnp.sum(updated * updated, axis=-1, keepdims=True) / size + EPSILON
    out_ref[...] = (updated * (jnp.sqrt(before) / jnp.sqrt(after))).astype(BF16)


SIDE = 4
SHIFTS = ((1, 1), (3, 3), (2, 2), (1, 3), (3, 1), (2, 1), (1, 2), (3, 2),
          (2, 3), (2, 0), (0, 2), (1, 0), (0, 1), (3, 0), (0, 3), (0, 0))
GROUPS = (2, 4, 4, 5, 1)
HEAD_AT, TARGET_AT = 0, 1
SOURCE_AT = TARGET_AT + len(SHIFTS)


def shifted(h, dx, dy):
    return (h // SIDE + dx) % SIDE * SIDE + (h + dy) % SIDE


def tail_kernel(k_ref, v_ref, tail_ref, table, sems):
    rows = pl.ds(k_ref.shape[0] - WINDOW, WINDOW)
    copies = [pltpu.make_async_copy(ref.at[rows], tail_ref.at[n], sems.at[n]) for n, ref in enumerate((k_ref, v_ref))]
    for c in copies:
        c.start()
    head = lax.axis_index("head")
    table[HEAD_AT] = head
    for n, (dx, dy) in enumerate(SHIFTS):
        table[TARGET_AT + n] = shifted(head, dx, dy)
        table[SOURCE_AT + n] = shifted(head, SIDE - dx, SIDE - dy)
    for c in copies:
        c.wait()


def tails(k, v):
    hd = k.shape[1]
    return pl.pallas_call(
        tail_kernel,
        in_specs=[pl.BlockSpec(memory_space=pl.ANY)] * 2,
        out_specs=[pl.BlockSpec(memory_space=pltpu.VMEM), pl.BlockSpec(memory_space=pltpu.SMEM)],
        out_shape=[pltpu.VMEM((2, WINDOW, hd), BF16), jax.ShapeDtypeStruct((SOURCE_AT + len(SHIFTS),), jnp.int32)],
        scratch_shapes=[pltpu.SemaphoreType.DMA((2,))],
        compiler_params=pltpu.CompilerParams(vmem_limit_bytes=60 << 20),
        name="tails",
    )(k, v)


def softmax_parts(s, lo, scale):
    tq, span = s.shape[0], s.shape[1]
    row = lax.broadcasted_iota(jnp.int32, (tq, tq), 0)
    col = lax.broadcasted_iota(jnp.int32, (tq, tq), 1)
    if lo is not None:
        s = jnp.where(lax.broadcasted_iota(jnp.int32, (tq, span), 1) >= lo, s, -1e30)
    parts = [jnp.where(col > row, s[:, :tq], -1e30), s[:, tq:WINDOW], jnp.where(col <= row, s[:, WINDOW:], -1e30)]
    top = jnp.maximum(jnp.max(jnp.maximum(parts[0], parts[2]), axis=1, keepdims=True),
                      jnp.max(parts[1], axis=1, keepdims=True)) * scale
    p = jnp.concatenate([jnp.exp2(x * scale - top) for x in parts], axis=1)
    return p.astype(BF16), 1.0 / jnp.sum(p, axis=1, keepdims=True)


def attend(q_ref, o_ref, key_rows, value_rows, lo, tq, scale):
    count = q_ref.shape[0] // tq

    def rows(n):
        return slice(n * tq, (n + 1) * tq)

    scores = dot_nt(q_ref[rows(0), :], key_rows(0))
    for n in range(count):
        ahead = dot_nt(q_ref[rows(n + 1), :], key_rows(n + 1)) if n + 1 < count else None
        p, inverse = softmax_parts(scores, None if lo is None else lo - n * tq, scale)
        o_ref[rows(n), :] = (dot_nn(p, value_rows(n)) * inverse).astype(BF16)
        scores = ahead


def attention_own_kernel(q_ref, k_ref, v_ref, *refs, tq, skip, scale):
    def window(ref):
        def rows(n):
            base = (pl.program_id(0) + skip) * q_ref.shape[0] + n * tq - WINDOW
            return ref[pl.ds(pl.multiple_of(base, tq), WINDOW + tq), :]

        return rows

    attend(q_ref, refs[-1], window(k_ref), window(v_ref), None, tq, scale)


def attention_first_kernel(q_ref, b_ref, k_ref, v_ref, *refs, at, tq, scale):
    o_ref, ek, ev, sems = refs[-4:]
    old, new = WINDOW - at, ek.shape[0] - WINDOW + at
    copies = []
    for n, (keys, held) in enumerate(((k_ref, ek), (v_ref, ev))):
        copies.append(pltpu.make_async_copy(b_ref.at[n, pl.ds(at, old)], held.at[pl.ds(0, old)], sems.at[2 * n]))
        copies.append(pltpu.make_async_copy(keys.at[pl.ds(0, new)], held.at[pl.ds(old, new)], sems.at[2 * n + 1]))
    for c in copies:
        c.start()
    for c in copies:
        c.wait()
    z, core = position()
    lo = jnp.where(z + core == 0, WINDOW, 0) - at

    def window(ref):
        return lambda n: ref[n * tq:n * tq + WINDOW + tq, :]

    attend(q_ref, o_ref, window(ek), window(ev), lo, tq, scale)


def attention_own(q, k, v, start, stop, attended=None, tq=256, tile=512):
    rows, hd = q.shape
    skip = start // tile
    scale = hd ** -0.5 * LOG2E
    count = (stop - start) // tile
    tile_spec = pl.BlockSpec((tile, hd), lambda i: (i + skip, 0))
    into = [] if attended is None else [attended]
    return pl.pallas_call(
        functools.partial(attention_own_kernel, tq=tq, skip=skip, scale=scale),
        grid=(count,),
        in_specs=[tile_spec, whole((rows, hd)), whole((rows, hd))] + [pl.BlockSpec(memory_space=pl.ANY)] * len(into),
        out_specs=tile_spec,
        out_shape=jax.ShapeDtypeStruct((rows, hd), BF16),
        input_output_aliases={3: 0} if into else {},
        cost_estimate=pl.CostEstimate(flops=4 * count * tile * (WINDOW + tq) * hd,
                                      bytes_accessed=10 << 20, transcendentals=count * tile * WINDOW),
        compiler_params=pltpu.CompilerParams(vmem_limit_bytes=24 << 20),
        name="attention_own",
    )(q, k, v, *into)


def attention_first(q, before, k, v, attended, at, tq=256, tile=512):
    hd = q.shape[1]
    scale = hd ** -0.5 * LOG2E
    tile_spec = pl.BlockSpec((tile, hd), lambda i: (at // tile, 0))
    return pl.pallas_call(
        functools.partial(attention_first_kernel, at=at, tq=tq, scale=scale),
        grid=(1,),
        in_specs=[tile_spec] + [pl.BlockSpec(memory_space=pl.ANY)] * 4,
        out_specs=tile_spec,
        scratch_shapes=[pltpu.VMEM((WINDOW + tile, hd), BF16)] * 2 + [pltpu.SemaphoreType.DMA((4,))],
        out_shape=jax.ShapeDtypeStruct(attended.shape, BF16),
        input_output_aliases={4: 0},
        cost_estimate=pl.CostEstimate(flops=4 * tile * (WINDOW + tq) * hd,
                                      bytes_accessed=4 << 20, transcendentals=tile * WINDOW),
        compiler_params=pltpu.CompilerParams(vmem_limit_bytes=20 << 20),
        name="attention_first",
    )(q, before, k, v, attended)


EXTRA = 8
LANES = 256


def apply_kernel(*refs, count, n_pieces, at):
    refs = refs[1:]
    q_refs, attended_refs, gate_refs = refs[:count], refs[count:2 * count], refs[2 * count:3 * count]
    gain_ref, weights, outs = refs[3 * count], refs[3 * count + 1:3 * count + 1 + n_pieces], refs[3 * count + 1 + n_pieces:]
    if n_pieces > 1:
        wt, start = outs[-1], 0
        for p in weights:
            wt[:, start:start + p.shape[1], :] = p[...]
            start += p.shape[1]
    else:
        wt = weights[0]
    share = q_refs[0].shape[1]
    q = jnp.concatenate([r[0] for r in q_refs], axis=0)
    hidden = (silu(dot_nt(q, wt[0])) * dot_nt(q, wt[1])).astype(BF16)
    fast = dot_nn(hidden, wt[2])
    for n in range(count):
        rows = slice(n * share, (n + 1) * share)
        head = (attended_refs[n][0].astype(F32) + fast[rows]).astype(BF16).astype(F32)
        squares = jnp.sum(head * head, axis=1, keepdims=True)
        y = outs[n]
        y[:share, :] = (head * (gain_ref[...] * silu(gate_refs[n][0].astype(F32)))).astype(BF16)
        column = jnp.concatenate([squares, jnp.zeros((LANES - share, 1), F32)], axis=0)
        line = jnp.broadcast_to(column, (LANES, 128)).T[:EXTRA, :]
        high = line.astype(BF16)
        low = (line - high.astype(F32)).astype(BF16)
        y[share:, :LANES] = high
        y[share:, LANES:] = low


def applied(table, q, attended, out_gate, gain, weights, n_head, at, count):
    rows, hd = q.shape
    share = rows // n_head
    fh = sum(p.shape[1] for p in weights)
    blocks = [a.reshape(n_head, share, hd) for a in (q, attended, out_gate)]
    specs = [pl.BlockSpec((1, share, hd), lambda i, t, j=TARGET_AT + at + j: (t[j], 0, 0)) for j in range(count)]
    first = len(weights) > 1
    outs = [jax.ShapeDtypeStruct((share + EXTRA, hd), BF16)] * count
    outs += [jax.ShapeDtypeStruct((3, fh, hd), BF16)] * first
    return pl.pallas_call(
        functools.partial(apply_kernel, count=count, n_pieces=len(weights), at=at),
        grid_spec=pltpu.PrefetchScalarGridSpec(
            num_scalar_prefetch=1, grid=(1,),
            in_specs=specs * 3 + [pl.BlockSpec((1, hd), lambda i, t: (0, t[HEAD_AT]))] + [whole(p.shape) for p in weights],
            out_specs=[whole(o.shape) for o in outs],
        ),
        out_shape=outs,
        cost_estimate=pl.CostEstimate(flops=6 * count * share * hd * fh, bytes_accessed=count << 20,
                                      transcendentals=2 * count * share * fh),
        compiler_params=pltpu.CompilerParams(vmem_limit_bytes=18 << 20),
        name="apply_fast",
    )(table, *[b for b in blocks for _ in range(count)], gain, *weights)


def scale_kernel(table, *refs):
    count = (len(refs) - 2) // 1 - 1
    y_refs, (o_ref, buf, sems) = refs[:count], refs[count:]
    share, width = buf.shape[1:]
    s = y_refs[0][share:, :].astype(F32)
    for y in y_refs[1:]:
        s = s + y[share:, :].astype(F32)
    line = s[:, :LANES] + s[:, LANES:]
    r = lax.rsqrt(line / (count * width) + EPSILON)
    r = jnp.concatenate([r] * (128 // EXTRA), axis=0).T[:share, :]
    r = jnp.concatenate([r] * (width // 128), axis=1)
    copies = []
    for n in range(count):
        buf[n] = (y_refs[n][:share, :].astype(F32) * r).astype(BF16)
        columns = pl.ds(pl.multiple_of(table[SOURCE_AT + n] * width, width), width)
        copies.append(pltpu.make_async_copy(buf.at[n], o_ref.at[:, columns], sems.at[n]))
        copies[-1].start()
    for c in copies:
        c.wait()


def scaled_rows(table, parts):
    rows, hd = parts[0].shape
    share, count = rows - EXTRA, len(parts)
    return pl.pallas_call(
        scale_kernel,
        grid_spec=pltpu.PrefetchScalarGridSpec(
            num_scalar_prefetch=1, grid=(1,),
            in_specs=[whole((rows, hd))] * count,
            out_specs=pl.BlockSpec(memory_space=pl.ANY),
            scratch_shapes=[pltpu.VMEM((count, share, hd), BF16), pltpu.SemaphoreType.DMA((count,))],
        ),
        out_shape=jax.ShapeDtypeStruct((share, count * hd), BF16),
        compiler_params=pltpu.CompilerParams(vmem_limit_bytes=16 << 20),
        name="scale_rows",
    )(table, *parts)


def layer(queries, key_vectors, value_vectors, step_sizes, w_in, w_up, w_out, out_gate, norm_gain):
    rows, _ = queries.shape
    n_ctx, n_head = lax.axis_size("ctx"), lax.axis_size("head")
    z_size = n_ctx // 2
    tied = lax.optimization_barrier

    def along_z(x, d):
        return lax.ppermute(x, "ctx", [(i, ((i // 2 + d) % z_size) * 2 + i % 2) for i in range(n_ctx)])

    def swapped(x):
        return lax.ppermute(x, "ctx", [(i, i ^ 1) for i in range(n_ctx)])

    tail, table = tails(key_vectors, value_vectors)
    before = lax.ppermute(tail, "ctx", [(i, i + 1) for i in range(n_ctx - 1)])
    keep, send, w_slice, keys, values = increments(
        key_vectors, value_vectors, step_sizes, w_in, w_up, w_out, z_size)

    order = sorted(range(1, z_size), key=lambda d: -min(d, z_size - d))
    parts = pair_sum(keep, swapped(send), z_size)
    arrived = [along_z(parts[d], d) for d in order]
    q, own = tied((queries, parts[0]))
    attended = attention_own(q, keys, values, WINDOW, rows)
    attended, arrived = tied((attended, arrived))
    piece = small_call(renorm_kernel, jax.ShapeDtypeStruct(own.shape, BF16), w_slice, own, *arrived)
    rest = [along_z(piece, d) for d in order]
    q, piece = tied((queries, piece))
    attended = attention_first(q, before, keys, values, attended, 0)
    attended = attention_first(q, before, keys, values, attended, TILE)
    attended, rest = tied((attended, rest))
    chip = [piece] + rest
    other = [swapped(p) for p in chip]

    weights, gain = chip + other, norm_gain.reshape(1, -1)
    parts, at = [], 0
    for count in GROUPS:
        outs = applied(table, queries, attended, out_gate, gain, weights, n_head, at, count)
        if len(outs) > count:
            weights = outs[count:]
        for y, (dx, dy) in zip(outs, SHIFTS[at:at + count]):
            if dx or dy:
                y = lax.ppermute(y, "head", [(h, shifted(h, dx, dy)) for h in range(n_head)])
            parts.append(y)
        at += count
    return scaled_rows(table, parts)


def solution(mesh):
    return jax.shard_map(
        layer,
        mesh=mesh,
        in_specs=(
            P("ctx", "head"), P("ctx", "head"), P("ctx", "head"), P("head", "ctx"),
            P("head", None, None), P("head", None, None), P("head", None, None),
            P("ctx", "head"), P(),
        ),
        out_specs=P(("ctx", "head"), None),
        check_vma=False,
    )
```

time: 120 us -> 118 us (0.983)
  Pallas kernels: 46.7 us -> 42.3 us
  starting transfers between devices: 63 us -> 66.1 us
    pallas_call x5 -> x6, Pallas kernels: 24 us -> 20.7 us  [the longest x1 14.1 us: increments(): pl.pallas_call(increments_kernel, in_specs=[anywhere, anywhere, inside, a...]
    ppermute x11, starting transfers between devices: 17.6 us -> 19.8 us  [the longest x6 11 us: along_z(): lax.ppermute(x, 'ctx', [(i, (i // 2 + d) % z_size * 2 + i % 2) for i in r...]
    pallas_call x2 -> x1, Pallas kernels: 8.87 us -> 6.78 us  [attention_own(): pl.pallas_call(functools.partial(attention_own_kernel, tq=tq, skip=skip,...]
    ppermute x15, waiting for transfers between devices: 6.3 us -> 4.83 us  [layer(): lax.ppermute(y, 'head', [(h, shifted(h, dx, dy)) for h in range(n_head)])]
    pallas_call x4 -> x5, Pallas kernels: 11.4 us -> 12.4 us  [applied(): pl.pallas_call(functools.partial(apply_kernel, count=count, n_pieces=len(...]
  transfers between devices with their start and end apart: 27 -> 27, of which waited for: 7 -> 8; matrix products, arithmetic and copies ran while one was open for 0% -> 0% of each run, Pallas kernels for 31% -> 31%
where the time goes in v2:
time: 118 us
  starting transfers between devices  66.1 us (56%)
  Pallas kernels  42.3 us (36%)
  waiting for transfers between devices  8.93 us (8%)
    ppermute x15, starting transfers between devices, layer(): lax.ppermute(y, 'head', [(h, shifted(h, dx, dy)) for h in range(n_head)])  44.6 us
    pallas_call x1, Pallas kernels, increments(): pl.pallas_call(increments_kernel, in_specs=[anywhere, anywhere, inside, a...  14.1 us
    pallas_call x5, Pallas kernels, applied(): pl.pallas_call(functools.partial(apply_kernel, count=count, n_pieces=len(...  12.4 us
    ppermute x6, starting transfers between devices, along_z(): lax.ppermute(x, 'ctx', [(i, (i // 2 + d) % z_size * 2 + i % 2) for i in r...  11 us
    ppermute x5, starting transfers between devices, swapped(): return lax.ppermute(x, 'ctx', [(i, i ^ 1) for i in range(n_ctx)])  8.81 us
    pallas_call x1, Pallas kernels, attention_own(): pl.pallas_call(functools.partial(attention_own_kernel, tq=tq, skip=skip,...  6.78 us
    ppermute x15, waiting for transfers between devices, layer(): lax.ppermute(y, 'head', [(h, shifted(h, dx, dy)) for h in range(n_head)])  4.83 us
    pallas_call x2, Pallas kernels, attention_first(): pl.pallas_call(functools.partial(attention_first_kernel, at=at, tq=tq, sc...  4 us
  transfers between devices with their start and end apart: 27, of which 8 were waited for; matrix products, arithmetic and copies ran while one was open for 0% of the time, Pallas kernels for 31%

profile of v2, /device:TPU:0, one launch (start us, length us, event | category | flops | bytes accessed | tf_op | source)
XLA Modules:
  0.0 117.7 jit_solution(12873030106524670007)
XLA Ops:
  0.0 2.1 %tails.1 = (bf16[2,1024,512]{2,1,0:T(8,128)(2,1)S(1)}, s32[33]{0:T(128)}) custom-call(bf16[3072,512]{1,0:T(8,128)(2,1)} %k_hbm.1, bf16[3072,512]{1,0:T(8,128)(2,1)} %v_hbm.1), custom_call_target="tpu_custom_call" | custom-call | tf_op jit(solution)/shard_map/tails/pallas_call | solution.py:189
  2.1 0.0 copy-start
  2.1 1.7 %collective-permute-start.4 = (bf16[2,1024,512]{2,1,0:T(8,128)(2,1)S(1)}, bf16[2,1024,512]{2,1,0:T(8,128)(2,1)S(1)}, u32[]{:S(2)}, u32[]{:S(2)}) collective-permute-start(bf16[2,1024,512]{2,1,0:T(8,128)(2,1)S(1)} %get-tuple-element.60), channel_id=1, source_target_pairs={{0,16},{16,32},{32,48},{48,64},{64,80},{80,96},{96,112},{1,17},{17... | collective-permute-start | bytes 6291464 | tf_op jit(solution)/shard_map/ppermute | solution.py:406
  3.8 14.1 %increments.1 = (bf16[3,256,512]{2,1,0:T(8,128)(2,1)S(1)}, bf16[3,256,512]{2,1,0:T(8,128)(2,1)S(1)}, bf16[3,64,512]{2,1,0:T(8,128)(2,1)S(1)}, bf16[3072,512]{1,0:T(8,128)(2,1)S(1)}, bf16[3072,512]{1,0:T(8,128)(2,1)S(1)}) custom-call(bf16[3072,512]{1,0:T(8,128)(2,1)} %k_hbm.1, bf16[3072,512]{1,0:T(8,128)(2,1)} %v_hbm.1, f32[1,3072]{1,0:T(1,128)} %rate_ref.1, ...), custom_call_target="tpu_custom_call" | custom-call | flops 9663676416 | bytes 9437184 | tf_op jit(solution)/shard_map/increments/pallas_call | solution.py:114
  17.9 2.7 %collective-permute-start = (bf16[3,256,512]{2,1,0:T(8,128)(2,1)S(1)}, bf16[3,256,512]{2,1,0:T(8,128)(2,1)S(1)}, u32[]{:S(2)}, u32[]{:S(2)}) collective-permute-start(bf16[3,256,512]{2,1,0:T(8,128)(2,1)S(1)} %get-tuple-element.47), channel_id=1, source_target_pairs={{0,16},{16,0},{32,48},{48,32},{64,80},{80,64},{96,112},{112,96},{1... | collective-permute-start | bytes 2359304 | tf_op jit(solution)/shard_map/ppermute | solution.py:403
  20.6 1.9 %collective-permute-done.got_ref = bf16[3,256,512]{2,1,0:T(8,128)(2,1)S(1)} collective-permute-done((bf16[3,256,512]{2,1,0:T(8,128)(2,1)S(1)}, bf16[3,256,512]{2,1,0:T(8,128)(2,1)S(1)}, u32[]{:S(2)}, u32[]{:S(2)}) %collective-permute-start) | collective-permute-done | bytes 786464 | tf_op jit(solution)/shard_map/ppermute | solution.py:403
  22.6 0.2 shard_map.91
  22.7 3.7 %collective-permute-start.1 = (bf16[3,64,512]{2,1,0:T(8,128)(2,1)S(1)}, bf16[3,64,512]{2,1,0:T(8,128)(2,1)S(1)}, u32[]{:S(2)}, u32[]{:S(2)}) collective-permute-start(bf16[3,64,512]{2,1,0:T(8,128)(2,1)S(1)} %get-tuple-element.53), channel_id=1, source_target_pairs={{0,64},{16,80},{32,96},{48,112},{64,0},{80,16},{96,32},{112,48},{1... | collective-permute-start | bytes 589832 | tf_op jit(solution)/shard_map/ppermute | solution.py:400
  26.4 3.2 %collective-permute-start.3 = (bf16[3,64,512]{2,1,0:T(8,128)(2,1)S(1)}, bf16[3,64,512]{2,1,0:T(8,128)(2,1)S(1)}, u32[]{:S(2)}, u32[]{:S(2)}) collective-permute-start(bf16[3,64,512]{2,1,0:T(8,128)(2,1)S(1)} %get-tuple-element.55), channel_id=1, source_target_pairs={{0,96},{16,112},{32,0},{48,16},{64,32},{80,48},{96,64},{112,80},{1... | collective-permute-start | bytes 589832 | tf_op jit(solution)/shard_map/ppermute | solution.py:400
  29.7 6.8 %attention_own.1.refs_0_ = bf16[3072,512]{1,0:T(8,128)(2,1)S(1)} custom-call(bf16[3072,512]{1,0:T(8,128)(2,1)S(1)} %copy-done, bf16[3072,512]{1,0:T(8,128)(2,1)S(1)} %get-tuple-element.51.k_ref, bf16[3072,512]{1,0:T(8,128)(2,1)S(1)} %get-tuple-element.52.v_ref), custom_call_target="tpu_custom_call" | custom-call | flops 5368709120 | bytes 10485760 | tf_op jit(solution)/shard_map/attention_own/pallas_call | solution.py:265
  36.5 0.3 shard_map.92.refs_8_
  36.7 1.7 %collective-permute-start.7 = (bf16[3,64,512]{2,1,0:T(8,128)(2,1)S(1)}, bf16[3,64,512]{2,1,0:T(8,128)(2,1)S(1)}, u32[]{:S(2)}, u32[]{:S(2)}) collective-permute-start(bf16[3,64,512]{2,1,0:T(8,128)(2,1)S(1)} %shard_map.92.refs_8_), channel_id=1, source_target_pairs={{0,96},{16,112},{32,0},{48,16},{64,32},{80,48},{96,64},{112,80},{1... | collective-permute-start | bytes 589832 | tf_op jit(solution)/shard_map/ppermute | solution.py:400
  38.4 0.4 collective-permute-start.6
  38.8 2.0 %collective-permute-start.5 = (bf16[3,64,512]{2,1,0:T(8,128)(2,1)S(1)}, bf16[3,64,512]{2,1,0:T(8,128)(2,1)S(1)}, u32[]{:S(2)}, u32[]{:S(2)}) collective-permute-start(bf16[3,64,512]{2,1,0:T(8,128)(2,1)S(1)} %shard_map.92.refs_8_), channel_id=1, source_target_pairs={{0,64},{16,80},{32,96},{48,112},{64,0},{80,16},{96,32},{112,48},{1... | collective-permute-start | bytes 589832 | tf_op jit(solution)/shard_map/ppermute | solution.py:400
  40.8 2.7 %collective-permute-start.8 = (bf16[3,64,512]{2,1,0:T(8,128)(2,1)S(1)}, bf16[3,64,512]{2,1,0:T(8,128)(2,1)S(1)}, u32[]{:S(2)}, u32[]{:S(2)}) collective-permute-start(bf16[3,64,512]{2,1,0:T(8,128)(2,1)S(1)} %shard_map.92.refs_8_), channel_id=1, source_target_pairs={{0,16},{16,0},{32,48},{48,32},{64,80},{80,64},{96,112},{112,96},{1... | collective-permute-start | bytes 589832 | tf_op jit(solution)/shard_map/ppermute | solution.py:403
  43.5 2.0 %attention_first.2.refs_0_ = bf16[3072,512]{1,0:T(8,128)(2,1)S(1)} custom-call(bf16[3072,512]{1,0:T(8,128)(2,1)S(1)} %copy-done, bf16[2,1024,512]{2,1,0:T(8,128)(2,1)S(1)} %collective-permute-done.4.b_ref, bf16[3072,512]{1,0:T(8,128)(2,1)S(1)} %get-tuple-element.51.k_ref, ...), custom_call_target="tpu_custom_call", output_to_operand_aliasing={{}: (4, {})} | custom-call | flops 1342177280 | bytes 4194304 | tf_op jit(solution)/shard_map/attention_first/pallas_call | solution.py:283
  45.5 0.0 copy-start.2
  45.5 0.0 copy-start.3
  45.5 2.0 %attention_first.3 = bf16[3072,512]{1,0:T(8,128)(2,1)S(1)} custom-call(bf16[3072,512]{1,0:T(8,128)(2,1)S(1)} %copy-done, bf16[2,1024,512]{2,1,0:T(8,128)(2,1)S(1)} %collective-permute-done.4.b_ref, bf16[3072,512]{1,0:T(8,128)(2,1)S(1)} %get-tuple-element.51.k_ref, bf16[3072,512]{1,0:T(8,128)(2,1)S(1)} %get-tuple-element.52.v_ref, ...), custom_call_target="tpu_custom_call", output_to_operand_aliasing={{}: (4, {})} | custom-call | flops 1342177280 | bytes 4194304 | tf_op jit(solution)/shard_map/attention_first/pallas_call | solution.py:283
  47.6 1.0 collective-permute-done.5.refs_9_
  48.5 2.9 %collective-permute-start.9 = (bf16[3,64,512]{2,1,0:T(8,128)(2,1)S(1)}, bf16[3,64,512]{2,1,0:T(8,128)(2,1)S(1)}, u32[]{:S(2)}, u32[]{:S(2)}) collective-permute-start(bf16[3,64,512]{2,1,0:T(8,128)(2,1)S(1)} %collective-permute-done.5.refs_9_), channel_id=1, source_target_pairs={{0,16},{16,0},{32,48},{48,32},{64,80},{80,64},{96,112},{112,96},{1... | collective-permute-start | bytes 589832 | tf_op jit(solution)/shard_map/ppermute | solution.py:403
  51.5 0.5 collective-permute-start.11
  52.0 0.6 collective-permute-done.9.refs_13_
  52.5 0.4 collective-permute-done.10.refs_14_
  52.9 0.3 collective-permute-done.11.refs_15_
  53.2 1.8 %apply_fast.5 = (bf16[200,512]{1,0:T(8,128)(2,1)S(1)}, bf16[200,512]{1,0:T(8,128)(2,1)S(1)}, bf16[3,512,512]{2,1,0:T(8,128)(2,1)S(1)}) custom-call(s32[33]{0:T(128)S(1)} %copy-done.3, bf16[16,192,512]{2,1,0:T(8,128)(2,1)S(1)} %bitcast.4, bf16[16,192,512]{2,1,0:T(8,128)(2,1)S(1)} %bitcast.5, bf16[16,192,512]{2,1,0:T(8,128)(2,1)S(1)} %bitcast.20, ...), custom_call_target="tpu_custom_call" | custom-call | flops 603979776 | bytes 2097152 | tf_op jit(solution)/shard_map/apply_fast/pallas_call | solution.py:340
  55.0 2.6 %collective-permute-start.12 = (bf16[200,512]{1,0:T(8,128)(2,1)S(1)}, bf16[200,512]{1,0:T(8,128)(2,1)S(1)}, u32[]{:S(2)}, u32[]{:S(2)}) collective-permute-start(bf16[200,512]{1,0:T(8,128)(2,1)S(1)} %get-tuple-element.67), channel_id=1, source_target_pairs={{0,5},{1,6},{2,7},{3,4},{4,9},{5,10},{6,11},{7,8},{8,13},{9,14},{1... | collective-permute-start | bytes 614408 | tf_op jit(solution)/shard_map/ppermute | solution.py:433
  57.6 2.9 %collective-permute-start.13 = (bf16[200,512]{1,0:T(8,128)(2,1)S(1)}, bf16[200,512]{1,0:T(8,128)(2,1)S(1)}, u32[]{:S(2)}, u32[]{:S(2)}) collective-permute-start(bf16[200,512]{1,0:T(8,128)(2,1)S(1)} %get-tuple-element.68), channel_id=1, source_target_pairs={{0,15},{1,12},{2,13},{3,14},{4,3},{5,0},{6,1},{7,2},{8,7},{9,4},{1... | collective-permute-start | bytes 614408 | tf_op jit(solution)/shard_map/ppermute | solution.py:433
  60.5 2.8 %apply_fast.7 = (bf16[200,512]{1,0:T(8,128)(2,1)S(1)}, bf16[200,512]{1,0:T(8,128)(2,1)S(1)}, bf16[200,512]{1,0:T(8,128)(2,1)S(1)}, bf16[200,512]{1,0:T(8,128)(2,1)S(1)}) custom-call(s32[33]{0:T(128)S(1)} %copy-done.3, bf16[16,192,512]{2,1,0:T(8,128)(2,1)S(1)} %bitcast.6, bf16[16,192,512]{2,1,0:T(8,128)(2,1)S(1)} %bitcast.7, ...), custom_call_target="tpu_custom_call" | custom-call | flops 1207959552 | bytes 4194304 | tf_op jit(solution)/shard_map/apply_fast/pallas_call | solution.py:340
  63.3 1.7 %collective-permute-start.18 = (bf16[200,512]{1,0:T(8,128)(2,1)S(1)}, bf16[200,512]{1,0:T(8,128)(2,1)S(1)}, u32[]{:S(2)}, u32[]{:S(2)}) collective-permute-start(bf16[200,512]{1,0:T(8,128)(2,1)S(1)} %get-tuple-element.74), channel_id=1, source_target_pairs={{0,6},{1,7},{2,4},{3,5},{4,10},{5,11},{6,8},{7,9},{8,14},{9,15},{1... | collective-permute-start | bytes 614408 | tf_op jit(solution)/shard_map/ppermute | solution.py:433
  65.0 3.9 %collective-permute-start.19 = (bf16[200,512]{1,0:T(8,128)(2,1)S(1)}, bf16[200,512]{1,0:T(8,128)(2,1)S(1)}, u32[]{:S(2)}, u32[]{:S(2)}) collective-permute-start(bf16[200,512]{1,0:T(8,128)(2,1)S(1)} %get-tuple-element.75), channel_id=1, source_target_pairs={{0,14},{1,15},{2,12},{3,13},{4,2},{5,3},{6,0},{7,1},{8,6},{9,7},{1... | collective-permute-start | bytes 614408 | tf_op jit(solution)/shard_map/ppermute | solution.py:433
  69.0 1.8 %collective-permute-start.20 = (bf16[200,512]{1,0:T(8,128)(2,1)S(1)}, bf16[200,512]{1,0:T(8,128)(2,1)S(1)}, u32[]{:S(2)}, u32[]{:S(2)}) collective-permute-start(bf16[200,512]{1,0:T(8,128)(2,1)S(1)} %get-tuple-element.76), channel_id=1, source_target_pairs={{0,11},{1,8},{2,9},{3,10},{4,15},{5,12},{6,13},{7,14},{8,3},{9,0},... | collective-permute-start | bytes 614408 | tf_op jit(solution)/shard_map/ppermute | solution.py:433
  70.8 2.8 %apply_fast.6 = (bf16[200,512]{1,0:T(8,128)(2,1)S(1)}, bf16[200,512]{1,0:T(8,128)(2,1)S(1)}, bf16[200,512]{1,0:T(8,128)(2,1)S(1)}, bf16[200,512]{1,0:T(8,128)(2,1)S(1)}) custom-call(s32[33]{0:T(128)S(1)} %copy-done.3, bf16[16,192,512]{2,1,0:T(8,128)(2,1)S(1)} %bitcast.10, bf16[16,192,512]{2,1,0:T(8,128)(2,1)S(1)} %bitcast.11, ...), custom_call_target="tpu_custom_call" | custom-call | flops 1207959552 | bytes 4194304 | tf_op jit(solution)/shard_map/apply_fast/pallas_call | solution.py:340
  73.6 3.0 %collective-permute-start.21 = (bf16[200,512]{1,0:T(8,128)(2,1)S(1)}, bf16[200,512]{1,0:T(8,128)(2,1)S(1)}, u32[]{:S(2)}, u32[]{:S(2)}) collective-permute-start(bf16[200,512]{1,0:T(8,128)(2,1)S(1)} %get-tuple-element.77), channel_id=1, source_target_pairs={{0,8},{1,9},{2,10},{3,11},{4,12},{5,13},{6,14},{7,15},{8,0},{9,1},... | collective-permute-start | bytes 614408 | tf_op jit(solution)/shard_map/ppermute | solution.py:433
  76.6 0.7 collective-permute-start.14
  77.3 0.6 collective-permute-done.18.refs_6_
  77.9 1.7 %collective-permute-start.15 = (bf16[200,512]{1,0:T(8,128)(2,1)S(1)}, bf16[200,512]{1,0:T(8,128)(2,1)S(1)}, u32[]{:S(2)}, u32[]{:S(2)}) collective-permute-start(bf16[200,512]{1,0:T(8,128)(2,1)S(1)} %get-tuple-element.71), channel_id=1, source_target_pairs={{0,7},{1,4},{2,5},{3,6},{4,11},{5,8},{6,9},{7,10},{8,15},{9,12},{1... | collective-permute-start | bytes 614408 | tf_op jit(solution)/shard_map/ppermute | solution.py:433
  79.6 9.0 %collective-permute-start.16 = (bf16[200,512]{1,0:T(8,128)(2,1)S(1)}, bf16[200,512]{1,0:T(8,128)(2,1)S(1)}, u32[]{:S(2)}, u32[]{:S(2)}) collective-permute-start(bf16[200,512]{1,0:T(8,128)(2,1)S(1)} %get-tuple-element.72), channel_id=1, source_target_pairs={{0,13},{1,14},{2,15},{3,12},{4,1},{5,2},{6,3},{7,0},{8,5},{9,6},{1... | collective-permute-start | bytes 614408 | tf_op jit(solution)/shard_map/ppermute | solution.py:433
  88.6 3.4 %apply_fast.8 = (bf16[200,512]{1,0:T(8,128)(2,1)S(1)}, bf16[200,512]{1,0:T(8,128)(2,1)S(1)}, bf16[200,512]{1,0:T(8,128)(2,1)S(1)}, bf16[200,512]{1,0:T(8,128)(2,1)S(1)}, bf16[200,512]{1,0:T(8,128)(2,1)S(1)}) custom-call(s32[33]{0:T(128)S(1)} %copy-done.3, bf16[16,192,512]{2,1,0:T(8,128)(2,1)S(1)} %bitcast.14, bf16[16,192,512]{2,1,0:T(8,128)(2,1)S(1)} %bitcast.15, ...), custom_call_target="tpu_custom_call" | custom-call | flops 1509949440 | bytes 5242880 | tf_op jit(solution)/shard_map/apply_fast/pallas_call | solution.py:340
  91.9 5.4 %collective-permute-start.22 = (bf16[200,512]{1,0:T(8,128)(2,1)S(1)}, bf16[200,512]{1,0:T(8,128)(2,1)S(1)}, u32[]{:S(2)}, u32[]{:S(2)}) collective-permute-start(bf16[200,512]{1,0:T(8,128)(2,1)S(1)} %get-tuple-element.78), channel_id=1, source_target_pairs={{0,2},{1,3},{2,0},{3,1},{4,6},{5,7},{6,4},{7,5},{8,10},{9,11},{10,... | collective-permute-start | bytes 614408 | tf_op jit(solution)/shard_map/ppermute | solution.py:433
  97.4 2.2 %collective-permute-start.23 = (bf16[200,512]{1,0:T(8,128)(2,1)S(1)}, bf16[200,512]{1,0:T(8,128)(2,1)S(1)}, u32[]{:S(2)}, u32[]{:S(2)}) collective-permute-start(bf16[200,512]{1,0:T(8,128)(2,1)S(1)} %get-tuple-element.79), channel_id=1, source_target_pairs={{0,4},{1,5},{2,6},{3,7},{4,8},{5,9},{6,10},{7,11},{8,12},{9,13},{1... | collective-permute-start | bytes 614408 | tf_op jit(solution)/shard_map/ppermute | solution.py:433
  99.6 4.2 %collective-permute-start.24 = (bf16[200,512]{1,0:T(8,128)(2,1)S(1)}, bf16[200,512]{1,0:T(8,128)(2,1)S(1)}, u32[]{:S(2)}, u32[]{:S(2)}) collective-permute-start(bf16[200,512]{1,0:T(8,128)(2,1)S(1)} %get-tuple-element.80), channel_id=1, source_target_pairs={{0,1},{1,2},{2,3},{3,0},{4,5},{5,6},{6,7},{7,4},{8,9},{9,10},{10,1... | collective-permute-start | bytes 614408 | tf_op jit(solution)/shard_map/ppermute | solution.py:433
  103.8 5.5 %collective-permute-start.25 = (bf16[200,512]{1,0:T(8,128)(2,1)S(1)}, bf16[200,512]{1,0:T(8,128)(2,1)S(1)}, u32[]{:S(2)}, u32[]{:S(2)}) collective-permute-start(bf16[200,512]{1,0:T(8,128)(2,1)S(1)} %get-tuple-element.81), channel_id=1, source_target_pairs={{0,12},{1,13},{2,14},{3,15},{4,0},{5,1},{6,2},{7,3},{8,4},{9,5},{1... | collective-permute-start | bytes 614408 | tf_op jit(solution)/shard_map/ppermute | solution.py:433
  109.3 1.5 %apply_fast.9.refs_15_ = bf16[200,512]{1,0:T(8,128)(2,1)S(1)} custom-call(s32[33]{0:T(128)S(1)} %copy-done.3, bf16[16,192,512]{2,1,0:T(8,128)(2,1)S(1)} %bitcast.19, bf16[16,192,512]{2,1,0:T(8,128)(2,1)S(1)} %bitcast.35, bf16[16,192,512]{2,1,0:T(8,128)(2,1)S(1)} %bitcast.51, f32[1,8192]{1,0:T(1,128)S(1)} %bitcast.56, ...), custom_call_target="tpu_custom_call" | custom-call | flops 301989888 | bytes 1048576 | tf_op jit(solution)/shard_map/apply_fast/pallas_call | solution.py:340
  110.8 0.0 collective-permute-done.23.refs_11_
  110.9 1.7 %collective-permute-done.25.refs_13_ = bf16[200,512]{1,0:T(8,128)(2,1)S(1)} collective-permute-done((bf16[200,512]{1,0:T(8,128)(2,1)S(1)}, bf16[200,512]{1,0:T(8,128)(2,1)S(1)}, u32[]{:S(2)}, u32[]{:S(2)}) %collective-permute-start.25) | collective-permute-done | bytes 204832 | tf_op jit(solution)/shard_map/ppermute | solution.py:433
  112.6 2.5 %collective-permute-done.26.refs_14_ = bf16[200,512]{1,0:T(8,128)(2,1)S(1)} collective-permute-done((bf16[200,512]{1,0:T(8,128)(2,1)S(1)}, bf16[200,512]{1,0:T(8,128)(2,1)S(1)}, u32[]{:S(2)}, u32[]{:S(2)}) %collective-permute-start.26) | collective-permute-done | bytes 204832 | tf_op jit(solution)/shard_map/ppermute | solution.py:433
  115.0 2.5 %scale_rows.1 = bf16[192,8192]{1,0:T(8,128)(2,1)} custom-call(s32[33]{0:T(128)S(1)} %copy-done.3, bf16[200,512]{1,0:T(8,128)(2,1)S(1)} %collective-permute-done.12.refs_0_, bf16[200,512]{1,0:T(8,128)(2,1)S(1)} %collective-permute-done.13.refs_1_, bf16[200,512]{1,0:T(8,128)(2,1)S(1)} %collective-permute-done.14.refs_2_, ...), custom_call_target="tpu_custom_call" | custom-call | tf_op jit(solution)/shard_map/scale_rows/pallas_call | solution.py:379
  (27 shorter events, 0.1 us)
Async XLA Ops:
  2.1 27.6 %copy-start = (bf16[3072,512]{1,0:T(8,128)(2,1)S(1)}, bf16[3072,512]{1,0:T(8,128)(2,1)}, u32[]{:S(2)}) copy-start(bf16[3072,512]{1,0:T(8,128)(2,1)} %q_ref.2) | copy-start | bytes 9437188
  2.1 41.4 %collective-permute-start.4 = (bf16[2,1024,512]{2,1,0:T(8,128)(2,1)S(1)}, bf16[2,1024,512]{2,1,0:T(8,128)(2,1)S(1)}, u32[]{:S(2)}, u32[]{:S(2)}) collective-permute-start(bf16[2,1024,512]{2,1,0:T(8,128)(2,1)S(1)} %get-tuple-element.60), channel_id=1, source_target_pairs={{0,16},{16,32},{32,48},{48,64},{64,80},{80,96},{96,112},{1,17},{17... | collective-permute-start | bytes 6291464 | tf_op jit(solution)/shard_map/ppermute | solution.py:406
  17.9 4.6 %collective-permute-start = (bf16[3,256,512]{2,1,0:T(8,128)(2,1)S(1)}, bf16[3,256,512]{2,1,0:T(8,128)(2,1)S(1)}, u32[]{:S(2)}, u32[]{:S(2)}) collective-permute-start(bf16[3,256,512]{2,1,0:T(8,128)(2,1)S(1)} %get-tuple-element.47), channel_id=1, source_target_pairs={{0,16},{16,0},{32,48},{48,32},{64,80},{80,64},{96,112},{112,96},{1... | collective-permute-start | bytes 2359304 | tf_op jit(solution)/shard_map/ppermute | solution.py:403
  22.7 13.7 %collective-permute-start.1 = (bf16[3,64,512]{2,1,0:T(8,128)(2,1)S(1)}, bf16[3,64,512]{2,1,0:T(8,128)(2,1)S(1)}, u32[]{:S(2)}, u32[]{:S(2)}) collective-permute-start(bf16[3,64,512]{2,1,0:T(8,128)(2,1)S(1)} %get-tuple-element.53), channel_id=1, source_target_pairs={{0,64},{16,80},{32,96},{48,112},{64,0},{80,16},{96,32},{112,48},{1... | collective-permute-start | bytes 589832 | tf_op jit(solution)/shard_map/ppermute | solution.py:400
  26.4 10.0 %collective-permute-start.2 = (bf16[3,64,512]{2,1,0:T(8,128)(2,1)S(1)}, bf16[3,64,512]{2,1,0:T(8,128)(2,1)S(1)}, u32[]{:S(2)}, u32[]{:S(2)}) collective-permute-start(bf16[3,64,512]{2,1,0:T(8,128)(2,1)S(1)} %get-tuple-element.54), channel_id=1, source_target_pairs={{0,32},{16,48},{32,64},{48,80},{64,96},{80,112},{96,0},{112,16},{1... | collective-permute-start | bytes 589832 | tf_op jit(solution)/shard_map/ppermute | solution.py:400
  26.4 10.0 %collective-permute-start.3 = (bf16[3,64,512]{2,1,0:T(8,128)(2,1)S(1)}, bf16[3,64,512]{2,1,0:T(8,128)(2,1)S(1)}, u32[]{:S(2)}, u32[]{:S(2)}) collective-permute-start(bf16[3,64,512]{2,1,0:T(8,128)(2,1)S(1)} %get-tuple-element.55), channel_id=1, source_target_pairs={{0,96},{16,112},{32,0},{48,16},{64,32},{80,48},{96,64},{112,80},{1... | collective-permute-start | bytes 589832 | tf_op jit(solution)/shard_map/ppermute | solution.py:400
  36.7 10.8 %collective-permute-start.7 = (bf16[3,64,512]{2,1,0:T(8,128)(2,1)S(1)}, bf16[3,64,512]{2,1,0:T(8,128)(2,1)S(1)}, u32[]{:S(2)}, u32[]{:S(2)}) collective-permute-start(bf16[3,64,512]{2,1,0:T(8,128)(2,1)S(1)} %shard_map.92.refs_8_), channel_id=1, source_target_pairs={{0,96},{16,112},{32,0},{48,16},{64,32},{80,48},{96,64},{112,80},{1... | collective-permute-start | bytes 589832 | tf_op jit(solution)/shard_map/ppermute | solution.py:400
  38.4 9.1 %collective-permute-start.6 = (bf16[3,64,512]{2,1,0:T(8,128)(2,1)S(1)}, bf16[3,64,512]{2,1,0:T(8,128)(2,1)S(1)}, u32[]{:S(2)}, u32[]{:S(2)}) collective-permute-start(bf16[3,64,512]{2,1,0:T(8,128)(2,1)S(1)} %shard_map.92.refs_8_), channel_id=1, source_target_pairs={{0,32},{16,48},{32,64},{48,80},{64,96},{80,112},{96,0},{112,16},{1... | collective-permute-start | bytes 589832 | tf_op jit(solution)/shard_map/ppermute | solution.py:400
  38.8 9.7 %collective-permute-start.5 = (bf16[3,64,512]{2,1,0:T(8,128)(2,1)S(1)}, bf16[3,64,512]{2,1,0:T(8,128)(2,1)S(1)}, u32[]{:S(2)}, u32[]{:S(2)}) collective-permute-start(bf16[3,64,512]{2,1,0:T(8,128)(2,1)S(1)} %shard_map.92.refs_8_), channel_id=1, source_target_pairs={{0,64},{16,80},{32,96},{48,112},{64,0},{80,16},{96,32},{112,48},{1... | collective-permute-start | bytes 589832 | tf_op jit(solution)/shard_map/ppermute | solution.py:400
  40.8 11.2 %collective-permute-start.8 = (bf16[3,64,512]{2,1,0:T(8,128)(2,1)S(1)}, bf16[3,64,512]{2,1,0:T(8,128)(2,1)S(1)}, u32[]{:S(2)}, u32[]{:S(2)}) collective-permute-start(bf16[3,64,512]{2,1,0:T(8,128)(2,1)S(1)} %shard_map.92.refs_8_), channel_id=1, source_target_pairs={{0,16},{16,0},{32,48},{48,32},{64,80},{80,64},{96,112},{112,96},{1... | collective-permute-start | bytes 589832 | tf_op jit(solution)/shard_map/ppermute | solution.py:403
  45.5 7.7 %copy-start.1 = (bf16[3072,512]{1,0:T(8,128)(2,1)S(1)}, bf16[3072,512]{1,0:T(8,128)(2,1)}, u32[]{:S(2)}) copy-start(bf16[3072,512]{1,0:T(8,128)(2,1)} %param.16) | copy-start | bytes 9437188
  45.5 7.7 %copy-start.2 = (f32[8192]{0:T(1024)S(1)}, f32[8192]{0:T(1024)}, u32[]{:S(2)}) copy-start(f32[8192]{0:T(1024)} %param.17) | copy-start | bytes 98308
  45.5 7.7 %copy-start.3 = (s32[33]{0:T(128)S(1)}, s32[33]{0:T(128)}, u32[]{:S(2)}) copy-start(s32[33]{0:T(128)} %get-tuple-element.44.refs_0_.table) | copy-start | bytes 400
  48.5 4.0 %collective-permute-start.9 = (bf16[3,64,512]{2,1,0:T(8,128)(2,1)S(1)}, bf16[3,64,512]{2,1,0:T(8,128)(2,1)S(1)}, u32[]{:S(2)}, u32[]{:S(2)}) collective-permute-start(bf16[3,64,512]{2,1,0:T(8,128)(2,1)S(1)} %collective-permute-done.5.refs_9_), channel_id=1, source_target_pairs={{0,16},{16,0},{32,48},{48,32},{64,80},{80,64},{96,112},{112,96},{1... | collective-permute-start | bytes 589832 | tf_op jit(solution)/shard_map/ppermute | solution.py:403
  51.5 1.4 %collective-permute-start.10 = (bf16[3,64,512]{2,1,0:T(8,128)(2,1)S(1)}, bf16[3,64,512]{2,1,0:T(8,128)(2,1)S(1)}, u32[]{:S(2)}, u32[]{:S(2)}) collective-permute-start(bf16[3,64,512]{2,1,0:T(8,128)(2,1)S(1)} %collective-permute-done.6.refs_10_), channel_id=1, source_target_pairs={{0,16},{16,0},{32,48},{48,32},{64,80},{80,64},{96,112},{112,96},{1... | collective-permute-start | bytes 589832 | tf_op jit(solution)/shard_map/ppermute | solution.py:403
  51.5 1.7 %collective-permute-start.11 = (bf16[3,64,512]{2,1,0:T(8,128)(2,1)S(1)}, bf16[3,64,512]{2,1,0:T(8,128)(2,1)S(1)}, u32[]{:S(2)}, u32[]{:S(2)}) collective-permute-start(bf16[3,64,512]{2,1,0:T(8,128)(2,1)S(1)} %collective-permute-done.7.refs_11_), channel_id=1, source_target_pairs={{0,16},{16,0},{32,48},{48,32},{64,80},{80,64},{96,112},{112,96},{1... | collective-permute-start | bytes 589832 | tf_op jit(solution)/shard_map/ppermute | solution.py:403
  55.0 18.6 %collective-permute-start.12 = (bf16[200,512]{1,0:T(8,128)(2,1)S(1)}, bf16[200,512]{1,0:T(8,128)(2,1)S(1)}, u32[]{:S(2)}, u32[]{:S(2)}) collective-permute-start(bf16[200,512]{1,0:T(8,128)(2,1)S(1)} %get-tuple-element.67), channel_id=1, source_target_pairs={{0,5},{1,6},{2,7},{3,4},{4,9},{5,10},{6,11},{7,8},{8,13},{9,14},{1... | collective-permute-start | bytes 614408 | tf_op jit(solution)/shard_map/ppermute | solution.py:433
  57.6 19.0 %collective-permute-start.13 = (bf16[200,512]{1,0:T(8,128)(2,1)S(1)}, bf16[200,512]{1,0:T(8,128)(2,1)S(1)}, u32[]{:S(2)}, u32[]{:S(2)}) collective-permute-start(bf16[200,512]{1,0:T(8,128)(2,1)S(1)} %get-tuple-element.68), channel_id=1, source_target_pairs={{0,15},{1,12},{2,13},{3,14},{4,3},{5,0},{6,1},{7,2},{8,7},{9,4},{1... | collective-permute-start | bytes 614408 | tf_op jit(solution)/shard_map/ppermute | solution.py:433
  63.3 14.6 %collective-permute-start.18 = (bf16[200,512]{1,0:T(8,128)(2,1)S(1)}, bf16[200,512]{1,0:T(8,128)(2,1)S(1)}, u32[]{:S(2)}, u32[]{:S(2)}) collective-permute-start(bf16[200,512]{1,0:T(8,128)(2,1)S(1)} %get-tuple-element.74), channel_id=1, source_target_pairs={{0,6},{1,7},{2,4},{3,5},{4,10},{5,11},{6,8},{7,9},{8,14},{9,15},{1... | collective-permute-start | bytes 614408 | tf_op jit(solution)/shard_map/ppermute | solution.py:433
  65.0 14.6 %collective-permute-start.19 = (bf16[200,512]{1,0:T(8,128)(2,1)S(1)}, bf16[200,512]{1,0:T(8,128)(2,1)S(1)}, u32[]{:S(2)}, u32[]{:S(2)}) collective-permute-start(bf16[200,512]{1,0:T(8,128)(2,1)S(1)} %get-tuple-element.75), channel_id=1, source_target_pairs={{0,14},{1,15},{2,12},{3,13},{4,2},{5,3},{6,0},{7,1},{8,6},{9,7},{1... | collective-permute-start | bytes 614408 | tf_op jit(solution)/shard_map/ppermute | solution.py:433
  69.0 19.6 %collective-permute-start.20 = (bf16[200,512]{1,0:T(8,128)(2,1)S(1)}, bf16[200,512]{1,0:T(8,128)(2,1)S(1)}, u32[]{:S(2)}, u32[]{:S(2)}) collective-permute-start(bf16[200,512]{1,0:T(8,128)(2,1)S(1)} %get-tuple-element.76), channel_id=1, source_target_pairs={{0,11},{1,8},{2,9},{3,10},{4,15},{5,12},{6,13},{7,14},{8,3},{9,0},... | collective-permute-start | bytes 614408 | tf_op jit(solution)/shard_map/ppermute | solution.py:433
  73.6 18.3 %collective-permute-start.21 = (bf16[200,512]{1,0:T(8,128)(2,1)S(1)}, bf16[200,512]{1,0:T(8,128)(2,1)S(1)}, u32[]{:S(2)}, u32[]{:S(2)}) collective-permute-start(bf16[200,512]{1,0:T(8,128)(2,1)S(1)} %get-tuple-element.77), channel_id=1, source_target_pairs={{0,8},{1,9},{2,10},{3,11},{4,12},{5,13},{6,14},{7,15},{8,0},{9,1},... | collective-permute-start | bytes 614408 | tf_op jit(solution)/shard_map/ppermute | solution.py:433
  76.6 20.7 %collective-permute-start.14 = (bf16[200,512]{1,0:T(8,128)(2,1)S(1)}, bf16[200,512]{1,0:T(8,128)(2,1)S(1)}, u32[]{:S(2)}, u32[]{:S(2)}) collective-permute-start(bf16[200,512]{1,0:T(8,128)(2,1)S(1)} %get-tuple-element.70), channel_id=1, source_target_pairs={{0,10},{1,11},{2,8},{3,9},{4,14},{5,15},{6,12},{7,13},{8,2},{9,3},... | collective-permute-start | bytes 614408 | tf_op jit(solution)/shard_map/ppermute | solution.py:433
  77.9 21.6 %collective-permute-start.15 = (bf16[200,512]{1,0:T(8,128)(2,1)S(1)}, bf16[200,512]{1,0:T(8,128)(2,1)S(1)}, u32[]{:S(2)}, u32[]{:S(2)}) collective-permute-start(bf16[200,512]{1,0:T(8,128)(2,1)S(1)} %get-tuple-element.71), channel_id=1, source_target_pairs={{0,7},{1,4},{2,5},{3,6},{4,11},{5,8},{6,9},{7,10},{8,15},{9,12},{1... | collective-permute-start | bytes 614408 | tf_op jit(solution)/shard_map/ppermute | solution.py:433
  79.6 24.1 %collective-permute-start.16 = (bf16[200,512]{1,0:T(8,128)(2,1)S(1)}, bf16[200,512]{1,0:T(8,128)(2,1)S(1)}, u32[]{:S(2)}, u32[]{:S(2)}) collective-permute-start(bf16[200,512]{1,0:T(8,128)(2,1)S(1)} %get-tuple-element.72), channel_id=1, source_target_pairs={{0,13},{1,14},{2,15},{3,12},{4,1},{5,2},{6,3},{7,0},{8,5},{9,6},{1... | collective-permute-start | bytes 614408 | tf_op jit(solution)/shard_map/ppermute | solution.py:433
  88.6 20.7 %collective-permute-start.17 = (bf16[200,512]{1,0:T(8,128)(2,1)S(1)}, bf16[200,512]{1,0:T(8,128)(2,1)S(1)}, u32[]{:S(2)}, u32[]{:S(2)}) collective-permute-start(bf16[200,512]{1,0:T(8,128)(2,1)S(1)} %get-tuple-element.73), channel_id=1, source_target_pairs={{0,9},{1,10},{2,11},{3,8},{4,13},{5,14},{6,15},{7,12},{8,1},{9,2},... | collective-permute-start | bytes 614408 | tf_op jit(solution)/shard_map/ppermute | solution.py:433
  91.9 18.9 %collective-permute-start.22 = (bf16[200,512]{1,0:T(8,128)(2,1)S(1)}, bf16[200,512]{1,0:T(8,128)(2,1)S(1)}, u32[]{:S(2)}, u32[]{:S(2)}) collective-permute-start(bf16[200,512]{1,0:T(8,128)(2,1)S(1)} %get-tuple-element.78), channel_id=1, source_target_pairs={{0,2},{1,3},{2,0},{3,1},{4,6},{5,7},{6,4},{7,5},{8,10},{9,11},{10,... | collective-permute-start | bytes 614408 | tf_op jit(solution)/shard_map/ppermute | solution.py:433
  97.4 13.5 %collective-permute-start.23 = (bf16[200,512]{1,0:T(8,128)(2,1)S(1)}, bf16[200,512]{1,0:T(8,128)(2,1)S(1)}, u32[]{:S(2)}, u32[]{:S(2)}) collective-permute-start(bf16[200,512]{1,0:T(8,128)(2,1)S(1)} %get-tuple-element.79), channel_id=1, source_target_pairs={{0,4},{1,5},{2,6},{3,7},{4,8},{5,9},{6,10},{7,11},{8,12},{9,13},{1... | collective-permute-start | bytes 614408 | tf_op jit(solution)/shard_map/ppermute | solution.py:433
  99.6 11.3 %collective-permute-start.24 = (bf16[200,512]{1,0:T(8,128)(2,1)S(1)}, bf16[200,512]{1,0:T(8,128)(2,1)S(1)}, u32[]{:S(2)}, u32[]{:S(2)}) collective-permute-start(bf16[200,512]{1,0:T(8,128)(2,1)S(1)} %get-tuple-element.80), channel_id=1, source_target_pairs={{0,1},{1,2},{2,3},{3,0},{4,5},{5,6},{6,7},{7,4},{8,9},{9,10},{10,1... | collective-permute-start | bytes 614408 | tf_op jit(solution)/shard_map/ppermute | solution.py:433
  103.8 8.8 %collective-permute-start.25 = (bf16[200,512]{1,0:T(8,128)(2,1)S(1)}, bf16[200,512]{1,0:T(8,128)(2,1)S(1)}, u32[]{:S(2)}, u32[]{:S(2)}) collective-permute-start(bf16[200,512]{1,0:T(8,128)(2,1)S(1)} %get-tuple-element.81), channel_id=1, source_target_pairs={{0,12},{1,13},{2,14},{3,15},{4,0},{5,1},{6,2},{7,3},{8,4},{9,5},{1... | collective-permute-start | bytes 614408 | tf_op jit(solution)/shard_map/ppermute | solution.py:433
  109.3 5.8 %collective-permute-start.26 = (bf16[200,512]{1,0:T(8,128)(2,1)S(1)}, bf16[200,512]{1,0:T(8,128)(2,1)S(1)}, u32[]{:S(2)}, u32[]{:S(2)}) collective-permute-start(bf16[200,512]{1,0:T(8,128)(2,1)S(1)} %get-tuple-element.82), channel_id=1, source_target_pairs={{0,3},{1,0},{2,1},{3,2},{4,7},{5,4},{6,5},{7,6},{8,11},{9,8},{10,9... | collective-permute-start | bytes 614408 | tf_op jit(solution)/shard_map/ppermute | solution.py:433

commit v3 on v2

--- a/solution.py
+++ b/solution.py
@@ -35,10 +35,6 @@
     return jnp.dot(a, b, preferred_element_type=F32)
 
 
-def whole(shape):
-    return pl.BlockSpec(shape, lambda *_: (0,) * len(shape))
-
-
 def position():
     ctx = lax.axis_index("ctx")
     return ctx // 2, ctx % 2
@@ -50,25 +46,21 @@
 STEP = 1024
 
 
-def increments_kernel(k_hbm, v_hbm, rate_ref, wi_hbm, wu_hbm, wo_hbm,
-                      keep_ref, send_ref, slice_ref, k_ref, v_ref, w, wt, acc, w_sems, sems):
+def increments_kernel(k_hbm, v_hbm, rate_ref, wi_ref, wu_ref, wo_ref,
+                      keep_ref, send_ref, slice_ref, k_ref, v_ref, wt, acc, sems):
     rows = k_ref.shape[0]
-    loads = [pltpu.make_async_copy(src.at[0], w.at[n], w_sems.at[n]) for n, src in enumerate((wi_hbm, wu_hbm, wo_hbm))]
 
     def tile_loads(t):
         at = pl.ds(pl.multiple_of(t * TILE, TILE), TILE)
         return (pltpu.make_async_copy(k_hbm.at[at], k_ref.at[at], sems.at[2 * t]),
                 pltpu.make_async_copy(v_hbm.at[at], v_ref.at[at], sems.at[2 * t + 1]))
 
-    ahead = 2
-    for c in loads:
-        c.start()
+    ahead = STEP // TILE
     for t in range(ahead):
         for c in tile_loads(t):
             c.start()
-    for n, c in enumerate(loads):
-        c.wait()
-        wt[n] = w[n].T
+    for n, w in enumerate((wi_ref, wu_ref, wo_ref)):
+        wt[n] = w[0].T
     for t in range(ahead, rows // TILE):
         for c in tile_loads(t):
             c.start()
@@ -113,15 +105,15 @@
     anywhere, inside = pl.BlockSpec(memory_space=pl.ANY), pl.BlockSpec(memory_space=pltpu.VMEM)
     return pl.pallas_call(
         increments_kernel,
-        in_specs=[anywhere, anywhere, inside, anywhere, anywhere, anywhere],
+        in_specs=[anywhere, anywhere, inside, inside, inside, inside],
         out_specs=[inside] * 5,
         out_shape=[pltpu.VMEM((3, half, hd), BF16), pltpu.VMEM((3, half, hd), BF16), pltpu.VMEM((3, part, hd), BF16),
                    pltpu.VMEM((rows, hd), BF16), pltpu.VMEM((rows, hd), BF16)],
-        scratch_shapes=[pltpu.VMEM((3, hd, fh), BF16), pltpu.VMEM((3, fh, hd), BF16), pltpu.VMEM((3, fh, hd), F32),
-                        pltpu.SemaphoreType.DMA((3,)), pltpu.SemaphoreType.DMA((2 * rows // TILE,))],
+        scratch_shapes=[pltpu.VMEM((3, fh, hd), BF16), pltpu.VMEM((3, fh, hd), F32),
+                        pltpu.SemaphoreType.DMA((2 * rows // TILE,))],
         cost_estimate=pl.CostEstimate(flops=12 * rows * hd * fh, bytes_accessed=9 << 20,
                                       transcendentals=rows * fh),
-        compiler_params=pltpu.CompilerParams(vmem_limit_bytes=48 << 20),
+        compiler_params=pltpu.CompilerParams(vmem_limit_bytes=45 << 20),
         name="increments",
     )(k, v, rate, w_in, w_up, w_out)
 
@@ -143,6 +135,10 @@
     three, half, hd = keep.shape
     return small_call(pair_sum_kernel, [jax.ShapeDtypeStruct((three, half // z_size, hd), BF16)] * z_size,
                       keep, got)
+
+
+def add_kernel(a_ref, b_ref, o_ref):
+    o_ref[...] = (a_ref[...].astype(F32) + b_ref[...].astype(F32)).astype(BF16)
 
 
 def renorm_kernel(w_ref, *refs):
@@ -210,87 +206,78 @@
     return p.astype(BF16), 1.0 / jnp.sum(p, axis=1, keepdims=True)
 
 
-def attend(q_ref, o_ref, key_rows, value_rows, lo, tq, scale):
-    count = q_ref.shape[0] // tq
-
-    def rows(n):
-        return slice(n * tq, (n + 1) * tq)
-
-    scores = dot_nt(q_ref[rows(0), :], key_rows(0))
+def attend(q_rows, o_store, key_rows, value_rows, lo, count, scale):
+    scores = dot_nt(q_rows(0), key_rows(0))
     for n in range(count):
-        ahead = dot_nt(q_ref[rows(n + 1), :], key_rows(n + 1)) if n + 1 < count else None
-        p, inverse = softmax_parts(scores, None if lo is None else lo - n * tq, scale)
-        o_ref[rows(n), :] = (dot_nn(p, value_rows(n)) * inverse).astype(BF16)
+        ahead = dot_nt(q_rows(n + 1), key_rows(n + 1)) if n + 1 < count else None
+        p, inverse = softmax_parts(scores, None if lo is None else lo(n), scale)
+        o_store(n, (dot_nn(p, value_rows(n)) * inverse).astype(BF16))
         scores = ahead
 
 
-def attention_own_kernel(q_ref, k_ref, v_ref, *refs, tq, skip, scale):
-    def window(ref):
-        def rows(n):
-            base = (pl.program_id(0) + skip) * q_ref.shape[0] + n * tq - WINDOW
-            return ref[pl.ds(pl.multiple_of(base, tq), WINDOW + tq), :]
-
-        return rows
-
-    attend(q_ref, refs[-1], window(k_ref), window(v_ref), None, tq, scale)
-
-
-def attention_first_kernel(q_ref, b_ref, k_ref, v_ref, *refs, at, tq, scale):
-    o_ref, ek, ev, sems = refs[-4:]
-    old, new = WINDOW - at, ek.shape[0] - WINDOW + at
-    copies = []
-    for n, (keys, held) in enumerate(((k_ref, ek), (v_ref, ev))):
-        copies.append(pltpu.make_async_copy(b_ref.at[n, pl.ds(at, old)], held.at[pl.ds(0, old)], sems.at[2 * n]))
-        copies.append(pltpu.make_async_copy(keys.at[pl.ds(0, new)], held.at[pl.ds(old, new)], sems.at[2 * n + 1]))
-    for c in copies:
-        c.start()
-    for c in copies:
-        c.wait()
+def attention_own_kernel(q_ref, k_ref, v_ref, *refs, tq, per, start, stop, scale):
+    o_ref = refs[-1]
+
+    def one(t, carry):
+        first = start + t * per * tq
+
+        def rows(ref, size, back):
+            return lambda n: ref[pl.ds(pl.multiple_of(first + n * tq - back, tq), size), :]
+
+        def store(n, x):
+            o_ref[pl.ds(pl.multiple_of(first + n * tq, tq), tq), :] = x
+
+        attend(rows(q_ref, tq, 0), store, rows(k_ref, WINDOW + tq, WINDOW), rows(v_ref, WINDOW + tq, WINDOW),
+               None, per, scale)
+        return carry
+
+    lax.fori_loop(0, (stop - start) // (per * tq), one, 0)
+
+
+def attention_first_kernel(q_ref, b_ref, k_ref, v_ref, _, o_ref, *, tq, scale):
     z, core = position()
-    lo = jnp.where(z + core == 0, WINDOW, 0) - at
-
-    def window(ref):
-        return lambda n: ref[n * tq:n * tq + WINDOW + tq, :]
-
-    attend(q_ref, o_ref, window(ek), window(ev), lo, tq, scale)
-
-
-def attention_own(q, k, v, start, stop, attended=None, tq=256, tile=512):
+    limit = jnp.where(z + core == 0, WINDOW, 0)
+
+    def window(which, ref):
+        return lambda n: jnp.concatenate([b_ref[which, n * tq:, :], ref[:(n + 1) * tq, :]], axis=0)
+
+    def store(n, x):
+        o_ref[n * tq:(n + 1) * tq, :] = x
+
+    attend(lambda n: q_ref[n * tq:(n + 1) * tq, :], store, window(0, k_ref), window(1, v_ref),
+           lambda n: limit - n * tq, WINDOW // tq, scale)
+
+
+INSIDE = pl.BlockSpec(memory_space=pltpu.VMEM)
+
+
+def attention_own(q, k, v, start, stop, attended=None, tq=256, per=2):
     rows, hd = q.shape
-    skip = start // tile
-    scale = hd ** -0.5 * LOG2E
-    count = (stop - start) // tile
-    tile_spec = pl.BlockSpec((tile, hd), lambda i: (i + skip, 0))
     into = [] if attended is None else [attended]
     return pl.pallas_call(
-        functools.partial(attention_own_kernel, tq=tq, skip=skip, scale=scale),
-        grid=(count,),
-        in_specs=[tile_spec, whole((rows, hd)), whole((rows, hd))] + [pl.BlockSpec(memory_space=pl.ANY)] * len(into),
-        out_specs=tile_spec,
-        out_shape=jax.ShapeDtypeStruct((rows, hd), BF16),
+        functools.partial(attention_own_kernel, tq=tq, per=per, start=start, stop=stop, scale=hd ** -0.5 * LOG2E),
+        in_specs=[INSIDE] * (3 + len(into)),
+        out_specs=INSIDE,
+        out_shape=pltpu.VMEM((rows, hd), BF16),
         input_output_aliases={3: 0} if into else {},
-        cost_estimate=pl.CostEstimate(flops=4 * count * tile * (WINDOW + tq) * hd,
-                                      bytes_accessed=10 << 20, transcendentals=count * tile * WINDOW),
-        compiler_params=pltpu.CompilerParams(vmem_limit_bytes=24 << 20),
+        cost_estimate=pl.CostEstimate(flops=4 * (stop - start) * (WINDOW + tq) * hd,
+                                      bytes_accessed=8 << 20, transcendentals=(stop - start) * WINDOW),
+        compiler_params=pltpu.CompilerParams(vmem_limit_bytes=14 << 20),
         name="attention_own",
     )(q, k, v, *into)
 
 
-def attention_first(q, before, k, v, attended, at, tq=256, tile=512):
+def attention_first(q, before, k, v, attended, tq=256):
     hd = q.shape[1]
-    scale = hd ** -0.5 * LOG2E
-    tile_spec = pl.BlockSpec((tile, hd), lambda i: (at // tile, 0))
-    return pl.pallas_call(
-        functools.partial(attention_first_kernel, at=at, tq=tq, scale=scale),
-        grid=(1,),
-        in_specs=[tile_spec] + [pl.BlockSpec(memory_space=pl.ANY)] * 4,
-        out_specs=tile_spec,
-        scratch_shapes=[pltpu.VMEM((WINDOW + tile, hd), BF16)] * 2 + [pltpu.SemaphoreType.DMA((4,))],
-        out_shape=jax.ShapeDtypeStruct(attended.shape, BF16),
+    return pl.pallas_call(
+        functools.partial(attention_first_kernel, tq=tq, scale=hd ** -0.5 * LOG2E),
+        in_specs=[INSIDE] * 5,
+        out_specs=INSIDE,
+        out_shape=pltpu.VMEM(attended.shape, BF16),
         input_output_aliases={4: 0},
-        cost_estimate=pl.CostEstimate(flops=4 * tile * (WINDOW + tq) * hd,
-                                      bytes_accessed=4 << 20, transcendentals=tile * WINDOW),
-        compiler_params=pltpu.CompilerParams(vmem_limit_bytes=20 << 20),
+        cost_estimate=pl.CostEstimate(flops=4 * WINDOW * (WINDOW + tq) * hd,
+                                      bytes_accessed=6 << 20, transcendentals=WINDOW * WINDOW),
+        compiler_params=pltpu.CompilerParams(vmem_limit_bytes=18 << 20),
         name="attention_first",
     )(q, before, k, v, attended)
 
@@ -299,10 +286,8 @@
 LANES = 256
 
 
-def apply_kernel(*refs, count, n_pieces, at):
-    refs = refs[1:]
-    q_refs, attended_refs, gate_refs = refs[:count], refs[count:2 * count], refs[2 * count:3 * count]
-    gain_ref, weights, outs = refs[3 * count], refs[3 * count + 1:3 * count + 1 + n_pieces], refs[3 * count + 1 + n_pieces:]
+def apply_kernel(table, q_ref, attended_ref, gate_ref, gain_ref, *refs, count, n_pieces, at):
+    weights, outs = refs[:n_pieces], refs[n_pieces:]
     if n_pieces > 1:
         wt, start = outs[-1], 0
         for p in weights:
@@ -310,16 +295,18 @@
             start += p.shape[1]
     else:
         wt = weights[0]
-    share = q_refs[0].shape[1]
-    q = jnp.concatenate([r[0] for r in q_refs], axis=0)
+    share, hd = q_ref.shape[1:]
+    targets = [table[TARGET_AT + at + n] for n in range(count)]
+    gain = gain_ref[:, pl.ds(pl.multiple_of(table[HEAD_AT] * hd, hd), hd)]
+    q = jnp.concatenate([q_ref[t] for t in targets], axis=0)
     hidden = (silu(dot_nt(q, wt[0])) * dot_nt(q, wt[1])).astype(BF16)
     fast = dot_nn(hidden, wt[2])
-    for n in range(count):
+    for n, t in enumerate(targets):
         rows = slice(n * share, (n + 1) * share)
-        head = (attended_refs[n][0].astype(F32) + fast[rows]).astype(BF16).astype(F32)
+        head = (attended_ref[t].astype(F32) + fast[rows]).astype(BF16).astype(F32)
         squares = jnp.sum(head * head, axis=1, keepdims=True)
         y = outs[n]
-        y[:share, :] = (head * (gain_ref[...] * silu(gate_refs[n][0].astype(F32)))).astype(BF16)
+        y[:share, :] = (head * (gain * silu(gate_ref[t].astype(F32)))).astype(BF16)
         column = jnp.concatenate([squares, jnp.zeros((LANES - share, 1), F32)], axis=0)
         line = jnp.broadcast_to(column, (LANES, 128)).T[:EXTRA, :]
         high = line.astype(BF16)
@@ -333,23 +320,20 @@
     share = rows // n_head
     fh = sum(p.shape[1] for p in weights)
     blocks = [a.reshape(n_head, share, hd) for a in (q, attended, out_gate)]
-    specs = [pl.BlockSpec((1, share, hd), lambda i, t, j=TARGET_AT + at + j: (t[j], 0, 0)) for j in range(count)]
-    first = len(weights) > 1
-    outs = [jax.ShapeDtypeStruct((share + EXTRA, hd), BF16)] * count
-    outs += [jax.ShapeDtypeStruct((3, fh, hd), BF16)] * first
+    inside = pl.BlockSpec(memory_space=pltpu.VMEM)
+    outs = [pltpu.VMEM((share + EXTRA, hd), BF16)] * count
+    if len(weights) > 1:
+        outs.append(pltpu.VMEM((3, fh, hd), BF16))
     return pl.pallas_call(
         functools.partial(apply_kernel, count=count, n_pieces=len(weights), at=at),
-        grid_spec=pltpu.PrefetchScalarGridSpec(
-            num_scalar_prefetch=1, grid=(1,),
-            in_specs=specs * 3 + [pl.BlockSpec((1, hd), lambda i, t: (0, t[HEAD_AT]))] + [whole(p.shape) for p in weights],
-            out_specs=[whole(o.shape) for o in outs],
-        ),
+        in_specs=[pl.BlockSpec(memory_space=pltpu.SMEM)] + [inside] * (4 + len(weights)),
+        out_specs=[inside] * len(outs),
         out_shape=outs,
         cost_estimate=pl.CostEstimate(flops=6 * count * share * hd * fh, bytes_accessed=count << 20,
                                       transcendentals=2 * count * share * fh),
         compiler_params=pltpu.CompilerParams(vmem_limit_bytes=18 << 20),
         name="apply_fast",
-    )(table, *[b for b in blocks for _ in range(count)], gain, *weights)
+    )(table, *blocks, gain, *weights)
 
 
 def scale_kernel(table, *refs):
@@ -378,14 +362,11 @@
     share, count = rows - EXTRA, len(parts)
     return pl.pallas_call(
         scale_kernel,
-        grid_spec=pltpu.PrefetchScalarGridSpec(
-            num_scalar_prefetch=1, grid=(1,),
-            in_specs=[whole((rows, hd))] * count,
-            out_specs=pl.BlockSpec(memory_space=pl.ANY),
-            scratch_shapes=[pltpu.VMEM((count, share, hd), BF16), pltpu.SemaphoreType.DMA((count,))],
-        ),
+        in_specs=[pl.BlockSpec(memory_space=pltpu.SMEM)] + [pl.BlockSpec(memory_space=pltpu.VMEM)] * count,
+        out_specs=pl.BlockSpec(memory_space=pl.ANY),
         out_shape=jax.ShapeDtypeStruct((share, count * hd), BF16),
-        compiler_params=pltpu.CompilerParams(vmem_limit_bytes=16 << 20),
+        scratch_shapes=[pltpu.VMEM((count, share, hd), BF16), pltpu.SemaphoreType.DMA((count,))],
+        compiler_params=pltpu.CompilerParams(vmem_limit_bytes=12 << 20),
         name="scale_rows",
     )(table, *parts)
 
@@ -404,20 +385,27 @@
 
     tail, table = tails(key_vectors, value_vectors)
     before = lax.ppermute(tail, "ctx", [(i, i + 1) for i in range(n_ctx - 1)])
-    keep, send, w_slice, keys, values = increments(
-        key_vectors, value_vectors, step_sizes, w_in, w_up, w_out, z_size)
+    early = [pltpu.with_memory_space_constraint(x, pltpu.VMEM) for x in (step_sizes, w_in, w_up, w_out)]
+    keep, send, w_slice, keys, values = increments(key_vectors, value_vectors, *early, z_size)
 
     order = sorted(range(1, z_size), key=lambda d: -min(d, z_size - d))
     parts = pair_sum(keep, swapped(send), z_size)
-    arrived = [along_z(parts[d], d) for d in order]
+    below = z_size - 1
+    from_far, from_below = along_z(parts[2], below), along_z(parts[1], 1)
     q, own = tied((queries, parts[0]))
-    attended = attention_own(q, keys, values, WINDOW, rows)
-    attended, arrived = tied((attended, arrived))
-    piece = small_call(renorm_kernel, jax.ShapeDtypeStruct(own.shape, BF16), w_slice, own, *arrived)
+    half = rows - WINDOW
+    attended = attention_own(q, keys, values, WINDOW, half)
+    attended, from_far = tied((attended, from_far))
+    both = small_call(add_kernel, jax.ShapeDtypeStruct(own.shape, BF16), parts[below], from_far)
+    from_above = along_z(both, below)
+    q, own, _ = tied((queries, own, both))
+    attended = attention_own(q, keys, values, half, rows, attended)
+    attended, from_below, from_above = tied((attended, from_below, from_above))
+    piece = small_call(renorm_kernel, jax.ShapeDtypeStruct(own.shape, BF16),
+                       w_slice, own, from_below, from_above)
     rest = [along_z(piece, d) for d in order]
     q, piece = tied((queries, piece))
-    attended = attention_first(q, before, keys, values, attended, 0)
-    attended = attention_first(q, before, keys, values, attended, TILE)
+    attended = attention_first(q, before, keys, values, attended)
     attended, rest = tied((attended, rest))
     chip = [piece] + rest
     other = [swapped(p) for p in chip]

time: 118 us -> 115 us (0.975)
  the two profiles are of different devices: /device:TPU:0 before, /device:TPU:6 now
where the time goes in v3:
time: 115 us
  starting transfers between devices  50.5 us (44%)
  Pallas kernels  42.2 us (37%)
  waiting for transfers between devices  21.4 us (19%)
    ppermute x15, starting transfers between devices, layer(): lax.ppermute(y, 'head', [(h, shifted(h, dx, dy)) for h in range(n_head)])  34.1 us
    ppermute x15, waiting for transfers between devices, layer(): lax.ppermute(y, 'head', [(h, shifted(h, dx, dy)) for h in range(n_head)])  14.7 us
    pallas_call x1, Pallas kernels, increments(): pl.pallas_call(increments_kernel, in_specs=[anywhere, anywhere, inside, i...  13.5 us
    pallas_call x5, Pallas kernels, applied(): pl.pallas_call(functools.partial(apply_kernel, count=count, n_pieces=len(...  12.4 us
    ppermute x6, starting transfers between devices, along_z(): lax.ppermute(x, 'ctx', [(i, (i // 2 + d) % z_size * 2 + i % 2) for i in r...  11.9 us
    pallas_call x2, Pallas kernels, attention_own(): pl.pallas_call(functools.partial(attention_own_kernel, tq=tq, per=per, st...  7.3 us
    pallas_call x1, Pallas kernels, attention_first(): pl.pallas_call(functools.partial(attention_first_kernel, tq=tq, scale=hd...  3.77 us
    ppermute x5, waiting for transfers between devices, swapped(): return lax.ppermute(x, 'ctx', [(i, i ^ 1) for i in range(n_ctx)])  3.4 us
  transfers between devices with their start and end apart: 27, of which 13 were waited for; matrix products, arithmetic and copies ran while one was open for 0% of the time, Pallas kernels for 28%

profile of v3, /device:TPU:6, one launch (start us, length us, event | category | flops | bytes accessed | tf_op | source)
XLA Modules:
  0.0 114.5 jit_solution(2323243238657929228)
XLA Ops:
  0.0 2.2 %tails.1 = (bf16[2,1024,512]{2,1,0:T(8,128)(2,1)S(1)}, s32[33]{0:T(128)}) custom-call(bf16[3072,512]{1,0:T(8,128)(2,1)} %k_hbm.1, bf16[3072,512]{1,0:T(8,128)(2,1)} %v_hbm.1), custom_call_target="tpu_custom_call" | custom-call | tf_op jit(solution)/shard_map/tails/pallas_call | solution.py:185
  2.2 1.9 %collective-permute-start.4 = (bf16[2,1024,512]{2,1,0:T(8,128)(2,1)S(1)}, bf16[2,1024,512]{2,1,0:T(8,128)(2,1)S(1)}, u32[]{:S(2)}, u32[]{:S(2)}) collective-permute-start(bf16[2,1024,512]{2,1,0:T(8,128)(2,1)S(1)} %get-tuple-element.66), channel_id=1, source_target_pairs={{0,16},{16,32},{32,48},{48,64},{64,80},{80,96},{96,112},{1,17},{17... | collective-permute-start | bytes 6291464 | tf_op jit(solution)/shard_map/ppermute | solution.py:387
  4.2 13.5 %increments.1 = (bf16[3,256,512]{2,1,0:T(8,128)(2,1)S(1)}, bf16[3,256,512]{2,1,0:T(8,128)(2,1)S(1)}, bf16[3,64,512]{2,1,0:T(8,128)(2,1)S(1)}, bf16[3072,512]{1,0:T(8,128)(2,1)S(1)}, bf16[3072,512]{1,0:T(8,128)(2,1)S(1)}) custom-call(bf16[3072,512]{1,0:T(8,128)(2,1)} %k_hbm.1, bf16[3072,512]{1,0:T(8,128)(2,1)} %v_hbm.1, f32[1,3072]{1,0:T(1,128)S(1)} %copy-done.7, ...), custom_call_target="tpu_custom_call" | custom-call | flops 9663676416 | bytes 9437184 | tf_op jit(solution)/shard_map/increments/pallas_call | solution.py:106
  17.7 2.1 %collective-permute-start = (bf16[3,256,512]{2,1,0:T(8,128)(2,1)S(1)}, bf16[3,256,512]{2,1,0:T(8,128)(2,1)S(1)}, u32[]{:S(2)}, u32[]{:S(2)}) collective-permute-start(bf16[3,256,512]{2,1,0:T(8,128)(2,1)S(1)} %get-tuple-element.50), channel_id=1, source_target_pairs={{0,16},{16,0},{32,48},{48,32},{64,80},{80,64},{96,112},{112,96},{1... | collective-permute-start | bytes 2359304 | tf_op jit(solution)/shard_map/ppermute | solution.py:384
  19.8 1.9 %collective-permute-done.got_ref = bf16[3,256,512]{2,1,0:T(8,128)(2,1)S(1)} collective-permute-done((bf16[3,256,512]{2,1,0:T(8,128)(2,1)S(1)}, bf16[3,256,512]{2,1,0:T(8,128)(2,1)S(1)}, u32[]{:S(2)}, u32[]{:S(2)}) %collective-permute-start) | collective-permute-done | bytes 786464 | tf_op jit(solution)/shard_map/ppermute | solution.py:384
  21.7 0.2 shard_map.91
  21.9 2.5 %collective-permute-start.1 = (bf16[3,64,512]{2,1,0:T(8,128)(2,1)S(1)}, bf16[3,64,512]{2,1,0:T(8,128)(2,1)S(1)}, u32[]{:S(2)}, u32[]{:S(2)}) collective-permute-start(bf16[3,64,512]{2,1,0:T(8,128)(2,1)S(1)} %get-tuple-element.57), channel_id=1, source_target_pairs={{0,96},{16,112},{32,0},{48,16},{64,32},{80,48},{96,64},{112,80},{1... | collective-permute-start | bytes 589832 | tf_op jit(solution)/shard_map/ppermute | solution.py:381
  24.4 3.7 %attention_own.2.refs_0_ = bf16[3072,512]{1,0:T(8,128)(2,1)S(1)} custom-call(bf16[3072,512]{1,0:T(8,128)(2,1)S(1)} %copy-done, bf16[3072,512]{1,0:T(8,128)(2,1)S(1)} %get-tuple-element.55.k_ref, bf16[3072,512]{1,0:T(8,128)(2,1)S(1)} %get-tuple-element.56.v_ref), custom_call_target="tpu_custom_call" | custom-call | flops 2684354560 | bytes 8388608 | tf_op jit(solution)/shard_map/attention_own/pallas_call | solution.py:257
  28.1 1.3 %collective-permute-done.1.b_ref = bf16[3,64,512]{2,1,0:T(8,128)(2,1)S(1)} collective-permute-done((bf16[3,64,512]{2,1,0:T(8,128)(2,1)S(1)}, bf16[3,64,512]{2,1,0:T(8,128)(2,1)S(1)}, u32[]{:S(2)}, u32[]{:S(2)}) %collective-permute-start.1) | collective-permute-done | bytes 196640 | tf_op jit(solution)/shard_map/ppermute | solution.py:381
  29.4 3.3 %collective-permute-start.3 = (bf16[3,64,512]{2,1,0:T(8,128)(2,1)S(1)}, bf16[3,64,512]{2,1,0:T(8,128)(2,1)S(1)}, u32[]{:S(2)}, u32[]{:S(2)}) collective-permute-start(bf16[3,64,512]{2,1,0:T(8,128)(2,1)S(1)} %shard_map.92), channel_id=1, source_target_pairs={{0,96},{16,112},{32,0},{48,16},{64,32},{80,48},{96,64},{112,80},{1... | collective-permute-start | bytes 589832 | tf_op jit(solution)/shard_map/ppermute | solution.py:381
  32.7 3.7 %attention_own.3._ = bf16[3072,512]{1,0:T(8,128)(2,1)S(1)} custom-call(bf16[3072,512]{1,0:T(8,128)(2,1)S(1)} %copy-done, bf16[3072,512]{1,0:T(8,128)(2,1)S(1)} %get-tuple-element.55.k_ref, bf16[3072,512]{1,0:T(8,128)(2,1)S(1)} %get-tuple-element.56.v_ref, bf16[3072,512]{1,0:T(8,128)(2,1)S(1)} %attention_own.2.refs_0_), custom_call_target="tpu_custom_call", output_to_operand_aliasing={{}: (3, {})} | custom-call | flops 2684354560 | bytes 8388608 | tf_op jit(solution)/shard_map/attention_own/pallas_call | solution.py:257
  36.3 0.3 shard_map.93.refs_0_
  36.6 2.9 %collective-permute-start.5 = (bf16[3,64,512]{2,1,0:T(8,128)(2,1)S(1)}, bf16[3,64,512]{2,1,0:T(8,128)(2,1)S(1)}, u32[]{:S(2)}, u32[]{:S(2)}) collective-permute-start(bf16[3,64,512]{2,1,0:T(8,128)(2,1)S(1)} %shard_map.93.refs_0_), channel_id=1, source_target_pairs={{0,64},{16,80},{32,96},{48,112},{64,0},{80,16},{96,32},{112,48},{1... | collective-permute-start | bytes 589832 | tf_op jit(solution)/shard_map/ppermute | solution.py:381
  39.6 1.6 %collective-permute-start.6 = (bf16[3,64,512]{2,1,0:T(8,128)(2,1)S(1)}, bf16[3,64,512]{2,1,0:T(8,128)(2,1)S(1)}, u32[]{:S(2)}, u32[]{:S(2)}) collective-permute-start(bf16[3,64,512]{2,1,0:T(8,128)(2,1)S(1)} %shard_map.93.refs_0_), channel_id=1, source_target_pairs={{0,32},{16,48},{32,64},{48,80},{64,96},{80,112},{96,0},{112,16},{1... | collective-permute-start | bytes 589832 | tf_op jit(solution)/shard_map/ppermute | solution.py:381
  41.2 1.6 %collective-permute-start.7 = (bf16[3,64,512]{2,1,0:T(8,128)(2,1)S(1)}, bf16[3,64,512]{2,1,0:T(8,128)(2,1)S(1)}, u32[]{:S(2)}, u32[]{:S(2)}) collective-permute-start(bf16[3,64,512]{2,1,0:T(8,128)(2,1)S(1)} %shard_map.93.refs_0_), channel_id=1, source_target_pairs={{0,96},{16,112},{32,0},{48,16},{64,32},{80,48},{96,64},{112,80},{1... | collective-permute-start | bytes 589832 | tf_op jit(solution)/shard_map/ppermute | solution.py:381
  42.8 3.8 %attention_first.1 = bf16[3072,512]{1,0:T(8,128)(2,1)S(1)} custom-call(bf16[3072,512]{1,0:T(8,128)(2,1)S(1)} %copy-done, bf16[2,1024,512]{2,1,0:T(8,128)(2,1)S(1)} %collective-permute-done.4.b_ref, bf16[3072,512]{1,0:T(8,128)(2,1)S(1)} %get-tuple-element.55.k_ref, bf16[3072,512]{1,0:T(8,128)(2,1)S(1)} %get-tuple-element.56.v_ref, ...), custom_call_target="tpu_custom_call", output_to_operand_aliasing={{}: (4, {})} | custom-call | flops 2684354560 | bytes 6291456 | tf_op jit(solution)/shard_map/attention_first/pallas_call | solution.py:272
  46.6 1.6 %collective-permute-done.6.refs_2_ = bf16[3,64,512]{2,1,0:T(8,128)(2,1)S(1)} collective-permute-done((bf16[3,64,512]{2,1,0:T(8,128)(2,1)S(1)}, bf16[3,64,512]{2,1,0:T(8,128)(2,1)S(1)}, u32[]{:S(2)}, u32[]{:S(2)}) %collective-permute-start.6) | collective-permute-done | bytes 196640 | tf_op jit(solution)/shard_map/ppermute | solution.py:381
  48.2 0.4 collective-permute-done.7.refs_3_
  48.6 0.5 collective-permute-start.11
  49.1 0.9 collective-permute-done.10.refs_6_
  50.0 0.3 collective-permute-done.11.refs_7_
  50.3 0.3 collective-permute-done.9.refs_5_
  50.6 1.8 %apply_fast.5 = (bf16[200,512]{1,0:T(8,128)(2,1)S(1)}, bf16[200,512]{1,0:T(8,128)(2,1)S(1)}, bf16[3,512,512]{2,1,0:T(8,128)(2,1)S(1)}) custom-call(s32[33]{0:T(128)S(1)} %copy-done.3, bf16[16,192,512]{2,1,0:T(8,128)(2,1)S(1)} %bitcast.4, bf16[16,192,512]{2,1,0:T(8,128)(2,1)S(1)} %bitcast.9, bf16[16,192,512]{2,1,0:T(8,128)(2,1)S(1)} %bitcast.14, ...), custom_call_target="tpu_custom_call" | custom-call | flops 603979776 | bytes 2097152 | tf_op jit(solution)/shard_map/apply_fast/pallas_call | solution.py:327
  52.5 3.4 %apply_fast.8 = (bf16[200,512]{1,0:T(8,128)(2,1)S(1)}, bf16[200,512]{1,0:T(8,128)(2,1)S(1)}, bf16[200,512]{1,0:T(8,128)(2,1)S(1)}, bf16[200,512]{1,0:T(8,128)(2,1)S(1)}, bf16[200,512]{1,0:T(8,128)(2,1)S(1)}) custom-call(s32[33]{0:T(128)S(1)} %copy-done.3, bf16[16,192,512]{2,1,0:T(8,128)(2,1)S(1)} %bitcast.5, bf16[16,192,512]{2,1,0:T(8,128)(2,1)S(1)} %bitcast.10, ...), custom_call_target="tpu_custom_call" | custom-call | flops 1509949440 | bytes 5242880 | tf_op jit(solution)/shard_map/apply_fast/pallas_call | solution.py:327
  55.8 3.3 %collective-permute-start.22 = (bf16[200,512]{1,0:T(8,128)(2,1)S(1)}, bf16[200,512]{1,0:T(8,128)(2,1)S(1)}, u32[]{:S(2)}, u32[]{:S(2)}) collective-permute-start(bf16[200,512]{1,0:T(8,128)(2,1)S(1)} %get-tuple-element.84), channel_id=1, source_target_pairs={{0,2},{1,3},{2,0},{3,1},{4,6},{5,7},{6,4},{7,5},{8,10},{9,11},{10,... | collective-permute-start | bytes 614408 | tf_op jit(solution)/shard_map/ppermute | solution.py:421
  59.1 0.5 collective-permute-start.23
  59.6 0.7 collective-permute-start.24
  60.2 1.6 %collective-permute-start.25 = (bf16[200,512]{1,0:T(8,128)(2,1)S(1)}, bf16[200,512]{1,0:T(8,128)(2,1)S(1)}, u32[]{:S(2)}, u32[]{:S(2)}) collective-permute-start(bf16[200,512]{1,0:T(8,128)(2,1)S(1)} %get-tuple-element.87), channel_id=1, source_target_pairs={{0,12},{1,13},{2,14},{3,15},{4,0},{5,1},{6,2},{7,3},{8,4},{9,5},{1... | collective-permute-start | bytes 614408 | tf_op jit(solution)/shard_map/ppermute | solution.py:421
  61.8 2.6 %collective-permute-start.26 = (bf16[200,512]{1,0:T(8,128)(2,1)S(1)}, bf16[200,512]{1,0:T(8,128)(2,1)S(1)}, u32[]{:S(2)}, u32[]{:S(2)}) collective-permute-start(bf16[200,512]{1,0:T(8,128)(2,1)S(1)} %get-tuple-element.88), channel_id=1, source_target_pairs={{0,3},{1,0},{2,1},{3,2},{4,7},{5,4},{6,5},{7,6},{8,11},{9,8},{10,9... | collective-permute-start | bytes 614408 | tf_op jit(solution)/shard_map/ppermute | solution.py:421
  64.4 2.8 %apply_fast.7 = (bf16[200,512]{1,0:T(8,128)(2,1)S(1)}, bf16[200,512]{1,0:T(8,128)(2,1)S(1)}, bf16[200,512]{1,0:T(8,128)(2,1)S(1)}, bf16[200,512]{1,0:T(8,128)(2,1)S(1)}) custom-call(s32[33]{0:T(128)S(1)} %copy-done.3, bf16[16,192,512]{2,1,0:T(8,128)(2,1)S(1)} %bitcast.6, bf16[16,192,512]{2,1,0:T(8,128)(2,1)S(1)} %bitcast.11, ...), custom_call_target="tpu_custom_call" | custom-call | flops 1207959552 | bytes 4194304 | tf_op jit(solution)/shard_map/apply_fast/pallas_call | solution.py:327
  67.2 2.8 %apply_fast.6 = (bf16[200,512]{1,0:T(8,128)(2,1)S(1)}, bf16[200,512]{1,0:T(8,128)(2,1)S(1)}, bf16[200,512]{1,0:T(8,128)(2,1)S(1)}, bf16[200,512]{1,0:T(8,128)(2,1)S(1)}) custom-call(s32[33]{0:T(128)S(1)} %copy-done.3, bf16[16,192,512]{2,1,0:T(8,128)(2,1)S(1)} %bitcast.7, bf16[16,192,512]{2,1,0:T(8,128)(2,1)S(1)} %bitcast.12, ...), custom_call_target="tpu_custom_call" | custom-call | flops 1207959552 | bytes 4194304 | tf_op jit(solution)/shard_map/apply_fast/pallas_call | solution.py:327
  70.1 0.7 collective-permute-start.18
  70.7 3.8 %collective-permute-start.19 = (bf16[200,512]{1,0:T(8,128)(2,1)S(1)}, bf16[200,512]{1,0:T(8,128)(2,1)S(1)}, u32[]{:S(2)}, u32[]{:S(2)}) collective-permute-start(bf16[200,512]{1,0:T(8,128)(2,1)S(1)} %get-tuple-element.81), channel_id=1, source_target_pairs={{0,14},{1,15},{2,12},{3,13},{4,2},{5,3},{6,0},{7,1},{8,6},{9,7},{1... | collective-permute-start | bytes 614408 | tf_op jit(solution)/shard_map/ppermute | solution.py:421
  74.6 0.8 collective-permute-start.20
  75.4 2.1 %collective-permute-start.21 = (bf16[200,512]{1,0:T(8,128)(2,1)S(1)}, bf16[200,512]{1,0:T(8,128)(2,1)S(1)}, u32[]{:S(2)}, u32[]{:S(2)}) collective-permute-start(bf16[200,512]{1,0:T(8,128)(2,1)S(1)} %get-tuple-element.83), channel_id=1, source_target_pairs={{0,8},{1,9},{2,10},{3,11},{4,12},{5,13},{6,14},{7,15},{8,0},{9,1},... | collective-permute-start | bytes 614408 | tf_op jit(solution)/shard_map/ppermute | solution.py:421
  77.5 2.4 %collective-permute-start.14 = (bf16[200,512]{1,0:T(8,128)(2,1)S(1)}, bf16[200,512]{1,0:T(8,128)(2,1)S(1)}, u32[]{:S(2)}, u32[]{:S(2)}) collective-permute-start(bf16[200,512]{1,0:T(8,128)(2,1)S(1)} %get-tuple-element.76), channel_id=1, source_target_pairs={{0,10},{1,11},{2,8},{3,9},{4,14},{5,15},{6,12},{7,13},{8,2},{9,3},... | collective-permute-start | bytes 614408 | tf_op jit(solution)/shard_map/ppermute | solution.py:421
  79.9 1.7 %collective-permute-done.18.refs_6_ = bf16[200,512]{1,0:T(8,128)(2,1)S(1)} collective-permute-done((bf16[200,512]{1,0:T(8,128)(2,1)S(1)}, bf16[200,512]{1,0:T(8,128)(2,1)S(1)}, u32[]{:S(2)}, u32[]{:S(2)}) %collective-permute-start.18) | collective-permute-done | bytes 204832 | tf_op jit(solution)/shard_map/ppermute | solution.py:421
  81.6 4.3 %collective-permute-start.15 = (bf16[200,512]{1,0:T(8,128)(2,1)S(1)}, bf16[200,512]{1,0:T(8,128)(2,1)S(1)}, u32[]{:S(2)}, u32[]{:S(2)}) collective-permute-start(bf16[200,512]{1,0:T(8,128)(2,1)S(1)} %get-tuple-element.77), channel_id=1, source_target_pairs={{0,7},{1,4},{2,5},{3,6},{4,11},{5,8},{6,9},{7,10},{8,15},{9,12},{1... | collective-permute-start | bytes 614408 | tf_op jit(solution)/shard_map/ppermute | solution.py:421
  85.9 0.6 collective-permute-start.16
  86.5 1.7 %collective-permute-done.20.refs_8_ = bf16[200,512]{1,0:T(8,128)(2,1)S(1)} collective-permute-done((bf16[200,512]{1,0:T(8,128)(2,1)S(1)}, bf16[200,512]{1,0:T(8,128)(2,1)S(1)}, u32[]{:S(2)}, u32[]{:S(2)}) %collective-permute-start.20) | collective-permute-done | bytes 204832 | tf_op jit(solution)/shard_map/ppermute | solution.py:421
  88.3 0.8 collective-permute-start.17
  89.0 3.3 %collective-permute-done.21.refs_9_ = bf16[200,512]{1,0:T(8,128)(2,1)S(1)} collective-permute-done((bf16[200,512]{1,0:T(8,128)(2,1)S(1)}, bf16[200,512]{1,0:T(8,128)(2,1)S(1)}, u32[]{:S(2)}, u32[]{:S(2)}) %collective-permute-start.21) | collective-permute-done | bytes 204832 | tf_op jit(solution)/shard_map/ppermute | solution.py:421
  92.3 10.0 %collective-permute-start.12 = (bf16[200,512]{1,0:T(8,128)(2,1)S(1)}, bf16[200,512]{1,0:T(8,128)(2,1)S(1)}, u32[]{:S(2)}, u32[]{:S(2)}) collective-permute-start(bf16[200,512]{1,0:T(8,128)(2,1)S(1)} %get-tuple-element.73), channel_id=1, source_target_pairs={{0,5},{1,6},{2,7},{3,4},{4,9},{5,10},{6,11},{7,8},{8,13},{9,14},{1... | collective-permute-start | bytes 614408 | tf_op jit(solution)/shard_map/ppermute | solution.py:421
  102.4 1.5 %apply_fast.9.refs_15_ = bf16[200,512]{1,0:T(8,128)(2,1)S(1)} custom-call(s32[33]{0:T(128)S(1)} %copy-done.3, bf16[16,192,512]{2,1,0:T(8,128)(2,1)S(1)} %bitcast.8, bf16[16,192,512]{2,1,0:T(8,128)(2,1)S(1)} %bitcast.13, bf16[16,192,512]{2,1,0:T(8,128)(2,1)S(1)} %bitcast.18, f32[1,8192]{1,0:T(1,128)S(1)} %bitcast.23, ...), custom_call_target="tpu_custom_call" | custom-call | flops 301989888 | bytes 1048576 | tf_op jit(solution)/shard_map/apply_fast/pallas_call | solution.py:327
  103.9 4.3 %collective-permute-done.17.refs_5_ = bf16[200,512]{1,0:T(8,128)(2,1)S(1)} collective-permute-done((bf16[200,512]{1,0:T(8,128)(2,1)S(1)}, bf16[200,512]{1,0:T(8,128)(2,1)S(1)}, u32[]{:S(2)}, u32[]{:S(2)}) %collective-permute-start.17) | collective-permute-done | bytes 204832 | tf_op jit(solution)/shard_map/ppermute | solution.py:421
  108.2 0.5 collective-permute-done.12.refs_0_
  108.7 3.2 %collective-permute-done.13.refs_1_ = bf16[200,512]{1,0:T(8,128)(2,1)S(1)} collective-permute-done((bf16[200,512]{1,0:T(8,128)(2,1)S(1)}, bf16[200,512]{1,0:T(8,128)(2,1)S(1)}, u32[]{:S(2)}, u32[]{:S(2)}) %collective-permute-start.13) | collective-permute-done | bytes 204832 | tf_op jit(solution)/shard_map/ppermute | solution.py:421
  111.9 2.5 %scale_rows.1 = bf16[192,8192]{1,0:T(8,128)(2,1)} custom-call(s32[33]{0:T(128)S(1)} %copy-done.3, bf16[200,512]{1,0:T(8,128)(2,1)S(1)} %collective-permute-done.12.refs_0_, bf16[200,512]{1,0:T(8,128)(2,1)S(1)} %collective-permute-done.13.refs_1_, bf16[200,512]{1,0:T(8,128)(2,1)S(1)} %collective-permute-done.14.refs_2_, ...), custom_call_target="tpu_custom_call" | custom-call | tf_op jit(solution)/shard_map/scale_rows/pallas_call | solution.py:363
  (36 shorter events, 0.2 us)
Async XLA Ops:
  0.0 4.1 %copy-start.7 = (f32[1,3072]{1,0:T(1,128)S(1)}, f32[1,3072]{1,0:T(1,128)}, u32[]{:S(2)}) copy-start(f32[1,3072]{1,0:T(1,128)} %rate_ref.1) | copy-start | bytes 36868
  0.0 4.1 %copy-start.4 = (bf16[1,512,512]{2,1,0:T(8,128)(2,1)S(1)}, bf16[1,512,512]{2,1,0:T(8,128)(2,1)}, u32[]{:S(2)}) copy-start(bf16[1,512,512]{2,1,0:T(8,128)(2,1)} %wi_ref.1) | copy-start | bytes 1572868
  0.0 4.1 %copy-start.5 = (bf16[1,512,512]{2,1,0:T(8,128)(2,1)S(1)}, bf16[1,512,512]{2,1,0:T(8,128)(2,1)}, u32[]{:S(2)}) copy-start(bf16[1,512,512]{2,1,0:T(8,128)(2,1)} %wu_ref.1) | copy-start | bytes 1572868
  0.0 4.1 %copy-start.6 = (bf16[1,512,512]{2,1,0:T(8,128)(2,1)S(1)}, bf16[1,512,512]{2,1,0:T(8,128)(2,1)}, u32[]{:S(2)}) copy-start(bf16[1,512,512]{2,1,0:T(8,128)(2,1)} %wo_ref.1) | copy-start | bytes 1572868
  2.2 40.6 %collective-permute-start.4 = (bf16[2,1024,512]{2,1,0:T(8,128)(2,1)S(1)}, bf16[2,1024,512]{2,1,0:T(8,128)(2,1)S(1)}, u32[]{:S(2)}, u32[]{:S(2)}) collective-permute-start(bf16[2,1024,512]{2,1,0:T(8,128)(2,1)S(1)} %get-tuple-element.66), channel_id=1, source_target_pairs={{0,16},{16,32},{32,48},{48,64},{64,80},{80,96},{96,112},{1,17},{17... | collective-permute-start | bytes 6291464 | tf_op jit(solution)/shard_map/ppermute | solution.py:387
  4.1 20.2 %copy-start = (bf16[3072,512]{1,0:T(8,128)(2,1)S(1)}, bf16[3072,512]{1,0:T(8,128)(2,1)}, u32[]{:S(2)}) copy-start(bf16[3072,512]{1,0:T(8,128)(2,1)} %q_ref.2) | copy-start | bytes 9437188
  17.7 4.1 %collective-permute-start = (bf16[3,256,512]{2,1,0:T(8,128)(2,1)S(1)}, bf16[3,256,512]{2,1,0:T(8,128)(2,1)S(1)}, u32[]{:S(2)}, u32[]{:S(2)}) collective-permute-start(bf16[3,256,512]{2,1,0:T(8,128)(2,1)S(1)} %get-tuple-element.50), channel_id=1, source_target_pairs={{0,16},{16,0},{32,48},{48,32},{64,80},{80,64},{96,112},{112,96},{1... | collective-permute-start | bytes 2359304 | tf_op jit(solution)/shard_map/ppermute | solution.py:384
  21.9 7.4 %collective-permute-start.1 = (bf16[3,64,512]{2,1,0:T(8,128)(2,1)S(1)}, bf16[3,64,512]{2,1,0:T(8,128)(2,1)S(1)}, u32[]{:S(2)}, u32[]{:S(2)}) collective-permute-start(bf16[3,64,512]{2,1,0:T(8,128)(2,1)S(1)} %get-tuple-element.57), channel_id=1, source_target_pairs={{0,96},{16,112},{32,0},{48,16},{64,32},{80,48},{96,64},{112,80},{1... | collective-permute-start | bytes 589832 | tf_op jit(solution)/shard_map/ppermute | solution.py:381
  24.4 11.9 %collective-permute-start.2 = (bf16[3,64,512]{2,1,0:T(8,128)(2,1)S(1)}, bf16[3,64,512]{2,1,0:T(8,128)(2,1)S(1)}, u32[]{:S(2)}, u32[]{:S(2)}) collective-permute-start(bf16[3,64,512]{2,1,0:T(8,128)(2,1)S(1)} %get-tuple-element.62), channel_id=1, source_target_pairs={{0,32},{16,48},{32,64},{48,80},{64,96},{80,112},{96,0},{112,16},{1... | collective-permute-start | bytes 589832 | tf_op jit(solution)/shard_map/ppermute | solution.py:381
  29.4 6.9 %collective-permute-start.3 = (bf16[3,64,512]{2,1,0:T(8,128)(2,1)S(1)}, bf16[3,64,512]{2,1,0:T(8,128)(2,1)S(1)}, u32[]{:S(2)}, u32[]{:S(2)}) collective-permute-start(bf16[3,64,512]{2,1,0:T(8,128)(2,1)S(1)} %shard_map.92), channel_id=1, source_target_pairs={{0,96},{16,112},{32,0},{48,16},{64,32},{80,48},{96,64},{112,80},{1... | collective-permute-start | bytes 589832 | tf_op jit(solution)/shard_map/ppermute | solution.py:381
  36.6 14.0 %copy-start.1 = (bf16[3072,512]{1,0:T(8,128)(2,1)S(1)}, bf16[3072,512]{1,0:T(8,128)(2,1)}, u32[]{:S(2)}) copy-start(bf16[3072,512]{1,0:T(8,128)(2,1)} %param.16) | copy-start | bytes 9437188
  36.6 14.0 %copy-start.2 = (f32[8192]{0:T(1024)S(1)}, f32[8192]{0:T(1024)}, u32[]{:S(2)}) copy-start(f32[8192]{0:T(1024)} %param.17) | copy-start | bytes 98308
  36.6 14.0 %copy-start.3 = (s32[33]{0:T(128)S(1)}, s32[33]{0:T(128)}, u32[]{:S(2)}) copy-start(s32[33]{0:T(128)} %get-tuple-element.47.table) | copy-start | bytes 400
  36.6 10.0 %collective-permute-start.5 = (bf16[3,64,512]{2,1,0:T(8,128)(2,1)S(1)}, bf16[3,64,512]{2,1,0:T(8,128)(2,1)S(1)}, u32[]{:S(2)}, u32[]{:S(2)}) collective-permute-start(bf16[3,64,512]{2,1,0:T(8,128)(2,1)S(1)} %shard_map.93.refs_0_), channel_id=1, source_target_pairs={{0,64},{16,80},{32,96},{48,112},{64,0},{80,16},{96,32},{112,48},{1... | collective-permute-start | bytes 589832 | tf_op jit(solution)/shard_map/ppermute | solution.py:381
  39.6 8.7 %collective-permute-start.6 = (bf16[3,64,512]{2,1,0:T(8,128)(2,1)S(1)}, bf16[3,64,512]{2,1,0:T(8,128)(2,1)S(1)}, u32[]{:S(2)}, u32[]{:S(2)}) collective-permute-start(bf16[3,64,512]{2,1,0:T(8,128)(2,1)S(1)} %shard_map.93.refs_0_), channel_id=1, source_target_pairs={{0,32},{16,48},{32,64},{48,80},{64,96},{80,112},{96,0},{112,16},{1... | collective-permute-start | bytes 589832 | tf_op jit(solution)/shard_map/ppermute | solution.py:381
  41.2 7.4 %collective-permute-start.7 = (bf16[3,64,512]{2,1,0:T(8,128)(2,1)S(1)}, bf16[3,64,512]{2,1,0:T(8,128)(2,1)S(1)}, u32[]{:S(2)}, u32[]{:S(2)}) collective-permute-start(bf16[3,64,512]{2,1,0:T(8,128)(2,1)S(1)} %shard_map.93.refs_0_), channel_id=1, source_target_pairs={{0,96},{16,112},{32,0},{48,16},{64,32},{80,48},{96,64},{112,80},{1... | collective-permute-start | bytes 589832 | tf_op jit(solution)/shard_map/ppermute | solution.py:381
  42.8 6.3 %collective-permute-start.8 = (bf16[3,64,512]{2,1,0:T(8,128)(2,1)S(1)}, bf16[3,64,512]{2,1,0:T(8,128)(2,1)S(1)}, u32[]{:S(2)}, u32[]{:S(2)}) collective-permute-start(bf16[3,64,512]{2,1,0:T(8,128)(2,1)S(1)} %shard_map.93.refs_0_), channel_id=1, source_target_pairs={{0,16},{16,0},{32,48},{48,32},{64,80},{80,64},{96,112},{112,96},{1... | collective-permute-start | bytes 589832 | tf_op jit(solution)/shard_map/ppermute | solution.py:384
  48.6 1.4 %collective-permute-start.10 = (bf16[3,64,512]{2,1,0:T(8,128)(2,1)S(1)}, bf16[3,64,512]{2,1,0:T(8,128)(2,1)S(1)}, u32[]{:S(2)}, u32[]{:S(2)}) collective-permute-start(bf16[3,64,512]{2,1,0:T(8,128)(2,1)S(1)} %collective-permute-done.6.refs_2_), channel_id=1, source_target_pairs={{0,16},{16,0},{32,48},{48,32},{64,80},{80,64},{96,112},{112,96},{1... | collective-permute-start | bytes 589832 | tf_op jit(solution)/shard_map/ppermute | solution.py:384
  48.6 1.7 %collective-permute-start.11 = (bf16[3,64,512]{2,1,0:T(8,128)(2,1)S(1)}, bf16[3,64,512]{2,1,0:T(8,128)(2,1)S(1)}, u32[]{:S(2)}, u32[]{:S(2)}) collective-permute-start(bf16[3,64,512]{2,1,0:T(8,128)(2,1)S(1)} %collective-permute-done.7.refs_3_), channel_id=1, source_target_pairs={{0,16},{16,0},{32,48},{48,32},{64,80},{80,64},{96,112},{112,96},{1... | collective-permute-start | bytes 589832 | tf_op jit(solution)/shard_map/ppermute | solution.py:384
  49.1 1.5 %collective-permute-start.9 = (bf16[3,64,512]{2,1,0:T(8,128)(2,1)S(1)}, bf16[3,64,512]{2,1,0:T(8,128)(2,1)S(1)}, u32[]{:S(2)}, u32[]{:S(2)}) collective-permute-start(bf16[3,64,512]{2,1,0:T(8,128)(2,1)S(1)} %collective-permute-done.5.refs_1_), channel_id=1, source_target_pairs={{0,16},{16,0},{32,48},{48,32},{64,80},{80,64},{96,112},{112,96},{1... | collective-permute-start | bytes 589832 | tf_op jit(solution)/shard_map/ppermute | solution.py:384
  55.8 14.2 %collective-permute-start.22 = (bf16[200,512]{1,0:T(8,128)(2,1)S(1)}, bf16[200,512]{1,0:T(8,128)(2,1)S(1)}, u32[]{:S(2)}, u32[]{:S(2)}) collective-permute-start(bf16[200,512]{1,0:T(8,128)(2,1)S(1)} %get-tuple-element.84), channel_id=1, source_target_pairs={{0,2},{1,3},{2,0},{3,1},{4,6},{5,7},{6,4},{7,5},{8,10},{9,11},{10,... | collective-permute-start | bytes 614408 | tf_op jit(solution)/shard_map/ppermute | solution.py:421
  59.1 11.6 %collective-permute-start.23 = (bf16[200,512]{1,0:T(8,128)(2,1)S(1)}, bf16[200,512]{1,0:T(8,128)(2,1)S(1)}, u32[]{:S(2)}, u32[]{:S(2)}) collective-permute-start(bf16[200,512]{1,0:T(8,128)(2,1)S(1)} %get-tuple-element.85), channel_id=1, source_target_pairs={{0,4},{1,5},{2,6},{3,7},{4,8},{5,9},{6,10},{7,11},{8,12},{9,13},{1... | collective-permute-start | bytes 614408 | tf_op jit(solution)/shard_map/ppermute | solution.py:421
  59.6 15.0 %collective-permute-start.24 = (bf16[200,512]{1,0:T(8,128)(2,1)S(1)}, bf16[200,512]{1,0:T(8,128)(2,1)S(1)}, u32[]{:S(2)}, u32[]{:S(2)}) collective-permute-start(bf16[200,512]{1,0:T(8,128)(2,1)S(1)} %get-tuple-element.86), channel_id=1, source_target_pairs={{0,1},{1,2},{2,3},{3,0},{4,5},{5,6},{6,7},{7,4},{8,9},{9,10},{10,1... | collective-permute-start | bytes 614408 | tf_op jit(solution)/shard_map/ppermute | solution.py:421
  60.2 15.1 %collective-permute-start.25 = (bf16[200,512]{1,0:T(8,128)(2,1)S(1)}, bf16[200,512]{1,0:T(8,128)(2,1)S(1)}, u32[]{:S(2)}, u32[]{:S(2)}) collective-permute-start(bf16[200,512]{1,0:T(8,128)(2,1)S(1)} %get-tuple-element.87), channel_id=1, source_target_pairs={{0,12},{1,13},{2,14},{3,15},{4,0},{5,1},{6,2},{7,3},{8,4},{9,5},{1... | collective-permute-start | bytes 614408 | tf_op jit(solution)/shard_map/ppermute | solution.py:421
  61.8 15.7 %collective-permute-start.26 = (bf16[200,512]{1,0:T(8,128)(2,1)S(1)}, bf16[200,512]{1,0:T(8,128)(2,1)S(1)}, u32[]{:S(2)}, u32[]{:S(2)}) collective-permute-start(bf16[200,512]{1,0:T(8,128)(2,1)S(1)} %get-tuple-element.88), channel_id=1, source_target_pairs={{0,3},{1,0},{2,1},{3,2},{4,7},{5,4},{6,5},{7,6},{8,11},{9,8},{10,9... | collective-permute-start | bytes 614408 | tf_op jit(solution)/shard_map/ppermute | solution.py:421
  70.1 11.6 %collective-permute-start.18 = (bf16[200,512]{1,0:T(8,128)(2,1)S(1)}, bf16[200,512]{1,0:T(8,128)(2,1)S(1)}, u32[]{:S(2)}, u32[]{:S(2)}) collective-permute-start(bf16[200,512]{1,0:T(8,128)(2,1)S(1)} %get-tuple-element.80), channel_id=1, source_target_pairs={{0,6},{1,7},{2,4},{3,5},{4,10},{5,11},{6,8},{7,9},{8,14},{9,15},{1... | collective-permute-start | bytes 614408 | tf_op jit(solution)/shard_map/ppermute | solution.py:421
  70.7 15.2 %collective-permute-start.19 = (bf16[200,512]{1,0:T(8,128)(2,1)S(1)}, bf16[200,512]{1,0:T(8,128)(2,1)S(1)}, u32[]{:S(2)}, u32[]{:S(2)}) collective-permute-start(bf16[200,512]{1,0:T(8,128)(2,1)S(1)} %get-tuple-element.81), channel_id=1, source_target_pairs={{0,14},{1,15},{2,12},{3,13},{4,2},{5,3},{6,0},{7,1},{8,6},{9,7},{1... | collective-permute-start | bytes 614408 | tf_op jit(solution)/shard_map/ppermute | solution.py:421
  74.6 13.7 %collective-permute-start.20 = (bf16[200,512]{1,0:T(8,128)(2,1)S(1)}, bf16[200,512]{1,0:T(8,128)(2,1)S(1)}, u32[]{:S(2)}, u32[]{:S(2)}) collective-permute-start(bf16[200,512]{1,0:T(8,128)(2,1)S(1)} %get-tuple-element.82), channel_id=1, source_target_pairs={{0,11},{1,8},{2,9},{3,10},{4,15},{5,12},{6,13},{7,14},{8,3},{9,0},... | collective-permute-start | bytes 614408 | tf_op jit(solution)/shard_map/ppermute | solution.py:421
  75.4 16.9 %collective-permute-start.21 = (bf16[200,512]{1,0:T(8,128)(2,1)S(1)}, bf16[200,512]{1,0:T(8,128)(2,1)S(1)}, u32[]{:S(2)}, u32[]{:S(2)}) collective-permute-start(bf16[200,512]{1,0:T(8,128)(2,1)S(1)} %get-tuple-element.83), channel_id=1, source_target_pairs={{0,8},{1,9},{2,10},{3,11},{4,12},{5,13},{6,14},{7,15},{8,0},{9,1},... | collective-permute-start | bytes 614408 | tf_op jit(solution)/shard_map/ppermute | solution.py:421
  77.5 24.8 %collective-permute-start.14 = (bf16[200,512]{1,0:T(8,128)(2,1)S(1)}, bf16[200,512]{1,0:T(8,128)(2,1)S(1)}, u32[]{:S(2)}, u32[]{:S(2)}) collective-permute-start(bf16[200,512]{1,0:T(8,128)(2,1)S(1)} %get-tuple-element.76), channel_id=1, source_target_pairs={{0,10},{1,11},{2,8},{3,9},{4,14},{5,15},{6,12},{7,13},{8,2},{9,3},... | collective-permute-start | bytes 614408 | tf_op jit(solution)/shard_map/ppermute | solution.py:421
  81.6 22.3 %collective-permute-start.15 = (bf16[200,512]{1,0:T(8,128)(2,1)S(1)}, bf16[200,512]{1,0:T(8,128)(2,1)S(1)}, u32[]{:S(2)}, u32[]{:S(2)}) collective-permute-start(bf16[200,512]{1,0:T(8,128)(2,1)S(1)} %get-tuple-element.77), channel_id=1, source_target_pairs={{0,7},{1,4},{2,5},{3,6},{4,11},{5,8},{6,9},{7,10},{8,15},{9,12},{1... | collective-permute-start | bytes 614408 | tf_op jit(solution)/shard_map/ppermute | solution.py:421
  85.9 18.0 %collective-permute-start.16 = (bf16[200,512]{1,0:T(8,128)(2,1)S(1)}, bf16[200,512]{1,0:T(8,128)(2,1)S(1)}, u32[]{:S(2)}, u32[]{:S(2)}) collective-permute-start(bf16[200,512]{1,0:T(8,128)(2,1)S(1)} %get-tuple-element.78), channel_id=1, source_target_pairs={{0,13},{1,14},{2,15},{3,12},{4,1},{5,2},{6,3},{7,0},{8,5},{9,6},{1... | collective-permute-start | bytes 614408 | tf_op jit(solution)/shard_map/ppermute | solution.py:421
  88.3 20.0 %collective-permute-start.17 = (bf16[200,512]{1,0:T(8,128)(2,1)S(1)}, bf16[200,512]{1,0:T(8,128)(2,1)S(1)}, u32[]{:S(2)}, u32[]{:S(2)}) collective-permute-start(bf16[200,512]{1,0:T(8,128)(2,1)S(1)} %get-tuple-element.79), channel_id=1, source_target_pairs={{0,9},{1,10},{2,11},{3,8},{4,13},{5,14},{6,15},{7,12},{8,1},{9,2},... | collective-permute-start | bytes 614408 | tf_op jit(solution)/shard_map/ppermute | solution.py:421
  92.3 16.4 %collective-permute-start.12 = (bf16[200,512]{1,0:T(8,128)(2,1)S(1)}, bf16[200,512]{1,0:T(8,128)(2,1)S(1)}, u32[]{:S(2)}, u32[]{:S(2)}) collective-permute-start(bf16[200,512]{1,0:T(8,128)(2,1)S(1)} %get-tuple-element.73), channel_id=1, source_target_pairs={{0,5},{1,6},{2,7},{3,4},{4,9},{5,10},{6,11},{7,8},{8,13},{9,14},{1... | collective-permute-start | bytes 614408 | tf_op jit(solution)/shard_map/ppermute | solution.py:421
  102.4 9.5 %collective-permute-start.13 = (bf16[200,512]{1,0:T(8,128)(2,1)S(1)}, bf16[200,512]{1,0:T(8,128)(2,1)S(1)}, u32[]{:S(2)}, u32[]{:S(2)}) collective-permute-start(bf16[200,512]{1,0:T(8,128)(2,1)S(1)} %get-tuple-element.74), channel_id=1, source_target_pairs={{0,15},{1,12},{2,13},{3,14},{4,3},{5,0},{6,1},{7,2},{8,7},{9,4},{1... | collective-permute-start | bytes 614408 | tf_op jit(solution)/shard_map/ppermute | solution.py:421

commit v4 on v3

--- a/solution.py
+++ b/solution.py
@@ -172,10 +172,12 @@
     for c in copies:
         c.start()
     head = lax.axis_index("head")
+    _, core = position()
     table[HEAD_AT] = head
     for n, (dx, dy) in enumerate(SHIFTS):
-        table[TARGET_AT + n] = shifted(head, dx, dy)
-        table[SOURCE_AT + n] = shifted(head, SIDE - dx, SIDE - dy)
+        forth, back = shifted(head, dx, dy), shifted(head, SIDE - dx, SIDE - dy)
+        table[TARGET_AT + n] = jnp.where(core == 0, forth, back)
+        table[SOURCE_AT + n] = jnp.where(core == 0, back, forth)
     for c in copies:
         c.wait()
 
@@ -418,7 +420,9 @@
             weights = outs[count:]
         for y, (dx, dy) in zip(outs, SHIFTS[at:at + count]):
             if dx or dy:
-                y = lax.ppermute(y, "head", [(h, shifted(h, dx, dy)) for h in range(n_head)])
+                ways = ((dx, dy), (SIDE - dx, SIDE - dy))
+                y = lax.ppermute(y, ("ctx", "head"), [
+                    (c * n_head + h, c * n_head + shifted(h, *ways[c % 2])) for c in range(n_ctx) for h in range(n_head)])
             parts.append(y)
         at += count
     return scaled_rows(table, parts)

time: 115 us -> 119 us (1.035)
  the two profiles are of different devices: /device:TPU:6 before, /device:TPU:1 now
where the time goes in v4:
time: 119 us; the launch traced here: 118 us
  starting transfers between devices  42.3 us (36%)
  Pallas kernels  42.2 us (35%)
  waiting for transfers between devices  32.8 us (28%)
    ppermute x15, waiting for transfers between devices, layer(): lax.ppermute(y, ('ctx', 'head'), [(c * n_head + h, c * n_head + shifted(h...  28.1 us
    ppermute x15, starting transfers between devices, layer(): lax.ppermute(y, ('ctx', 'head'), [(c * n_head + h, c * n_head + shifted(h...  22.6 us
    pallas_call x1, Pallas kernels, increments(): pl.pallas_call(increments_kernel, in_specs=[anywhere, anywhere, inside, i...  13.5 us
    pallas_call x5, Pallas kernels, applied(): pl.pallas_call(functools.partial(apply_kernel, count=count, n_pieces=len(...  12.4 us
    ppermute x6, starting transfers between devices, along_z(): lax.ppermute(x, 'ctx', [(i, (i // 2 + d) % z_size * 2 + i % 2) for i in r...  9.55 us
    pallas_call x2, Pallas kernels, attention_own(): pl.pallas_call(functools.partial(attention_own_kernel, tq=tq, per=per, st...  7.31 us
    ppermute x5, starting transfers between devices, swapped(): return lax.ppermute(x, 'ctx', [(i, i ^ 1) for i in range(n_ctx)])  5.19 us
    ppermute x1, starting transfers between devices, layer(): before = lax.ppermute(tail, 'ctx', [(i, i + 1) for i in range(n_ctx - 1)])  4.92 us
  transfers between devices with their start and end apart: 27, of which 9 were waited for; matrix products, arithmetic and copies ran while one was open for 0% of the time, Pallas kernels for 27%

profile of v4, /device:TPU:1, one launch (start us, length us, event | category | flops | bytes accessed | tf_op | source)
XLA Modules:
  0.0 117.7 jit_solution(15805179199566939983)
XLA Ops:
  0.0 2.2 %tails.1 = (bf16[2,1024,512]{2,1,0:T(8,128)(2,1)S(1)}, s32[33]{0:T(128)}) custom-call(bf16[3072,512]{1,0:T(8,128)(2,1)} %k_hbm.1, bf16[3072,512]{1,0:T(8,128)(2,1)} %v_hbm.1), custom_call_target="tpu_custom_call" | custom-call | tf_op jit(solution)/shard_map/tails/pallas_call | solution.py:187
  2.2 4.9 %collective-permute-start.4 = (bf16[2,1024,512]{2,1,0:T(8,128)(2,1)S(1)}, bf16[2,1024,512]{2,1,0:T(8,128)(2,1)S(1)}, u32[]{:S(2)}, u32[]{:S(2)}) collective-permute-start(bf16[2,1024,512]{2,1,0:T(8,128)(2,1)S(1)} %get-tuple-element.66), channel_id=1, source_target_pairs={{0,16},{16,32},{32,48},{48,64},{64,80},{80,96},{96,112},{1,17},{17... | collective-permute-start | bytes 6291464 | tf_op jit(solution)/shard_map/ppermute | solution.py:389
  7.2 0.0 copy-start
  7.2 13.5 %increments.1 = (bf16[3,256,512]{2,1,0:T(8,128)(2,1)S(1)}, bf16[3,256,512]{2,1,0:T(8,128)(2,1)S(1)}, bf16[3,64,512]{2,1,0:T(8,128)(2,1)S(1)}, bf16[3072,512]{1,0:T(8,128)(2,1)S(1)}, bf16[3072,512]{1,0:T(8,128)(2,1)S(1)}) custom-call(bf16[3072,512]{1,0:T(8,128)(2,1)} %k_hbm.1, bf16[3072,512]{1,0:T(8,128)(2,1)} %v_hbm.1, f32[1,3072]{1,0:T(1,128)S(1)} %copy-done.7, ...), custom_call_target="tpu_custom_call" | custom-call | flops 9663676416 | bytes 9437184 | tf_op jit(solution)/shard_map/increments/pallas_call | solution.py:106
  20.7 0.1 collective-permute-start
  20.8 2.3 %collective-permute-done.got_ref = bf16[3,256,512]{2,1,0:T(8,128)(2,1)S(1)} collective-permute-done((bf16[3,256,512]{2,1,0:T(8,128)(2,1)S(1)}, bf16[3,256,512]{2,1,0:T(8,128)(2,1)S(1)}, u32[]{:S(2)}, u32[]{:S(2)}) %collective-permute-start) | collective-permute-done | bytes 786464 | tf_op jit(solution)/shard_map/ppermute | solution.py:386
  23.1 0.2 shard_map.91
  23.3 2.0 %collective-permute-start.1 = (bf16[3,64,512]{2,1,0:T(8,128)(2,1)S(1)}, bf16[3,64,512]{2,1,0:T(8,128)(2,1)S(1)}, u32[]{:S(2)}, u32[]{:S(2)}) collective-permute-start(bf16[3,64,512]{2,1,0:T(8,128)(2,1)S(1)} %get-tuple-element.57), channel_id=1, source_target_pairs={{0,96},{16,112},{32,0},{48,16},{64,32},{80,48},{96,64},{112,80},{1... | collective-permute-start | bytes 589832 | tf_op jit(solution)/shard_map/ppermute | solution.py:383
  25.2 3.7 %attention_own.2.refs_0_ = bf16[3072,512]{1,0:T(8,128)(2,1)S(1)} custom-call(bf16[3072,512]{1,0:T(8,128)(2,1)S(1)} %copy-done, bf16[3072,512]{1,0:T(8,128)(2,1)S(1)} %get-tuple-element.55.k_ref, bf16[3072,512]{1,0:T(8,128)(2,1)S(1)} %get-tuple-element.56.v_ref), custom_call_target="tpu_custom_call" | custom-call | flops 2684354560 | bytes 8388608 | tf_op jit(solution)/shard_map/attention_own/pallas_call | solution.py:259
  28.9 1.1 collective-permute-done.1.b_ref
  30.1 2.6 %collective-permute-start.3 = (bf16[3,64,512]{2,1,0:T(8,128)(2,1)S(1)}, bf16[3,64,512]{2,1,0:T(8,128)(2,1)S(1)}, u32[]{:S(2)}, u32[]{:S(2)}) collective-permute-start(bf16[3,64,512]{2,1,0:T(8,128)(2,1)S(1)} %shard_map.92), channel_id=1, source_target_pairs={{0,96},{16,112},{32,0},{48,16},{64,32},{80,48},{96,64},{112,80},{1... | collective-permute-start | bytes 589832 | tf_op jit(solution)/shard_map/ppermute | solution.py:383
  32.6 3.7 %attention_own.3._ = bf16[3072,512]{1,0:T(8,128)(2,1)S(1)} custom-call(bf16[3072,512]{1,0:T(8,128)(2,1)S(1)} %copy-done, bf16[3072,512]{1,0:T(8,128)(2,1)S(1)} %get-tuple-element.55.k_ref, bf16[3072,512]{1,0:T(8,128)(2,1)S(1)} %get-tuple-element.56.v_ref, bf16[3072,512]{1,0:T(8,128)(2,1)S(1)} %attention_own.2.refs_0_), custom_call_target="tpu_custom_call", output_to_operand_aliasing={{}: (3, {})} | custom-call | flops 2684354560 | bytes 8388608 | tf_op jit(solution)/shard_map/attention_own/pallas_call | solution.py:259
  36.3 0.3 shard_map.93.refs_0_
  36.6 0.0 copy-start.1
  36.6 0.0 copy-start.2
  36.6 0.0 copy-start.3
  36.6 2.3 %collective-permute-start.5 = (bf16[3,64,512]{2,1,0:T(8,128)(2,1)S(1)}, bf16[3,64,512]{2,1,0:T(8,128)(2,1)S(1)}, u32[]{:S(2)}, u32[]{:S(2)}) collective-permute-start(bf16[3,64,512]{2,1,0:T(8,128)(2,1)S(1)} %shard_map.93.refs_0_), channel_id=1, source_target_pairs={{0,64},{16,80},{32,96},{48,112},{64,0},{80,16},{96,32},{112,48},{1... | collective-permute-start | bytes 589832 | tf_op jit(solution)/shard_map/ppermute | solution.py:383
  38.9 1.1 collective-permute-start.6
  40.0 1.6 %collective-permute-start.7 = (bf16[3,64,512]{2,1,0:T(8,128)(2,1)S(1)}, bf16[3,64,512]{2,1,0:T(8,128)(2,1)S(1)}, u32[]{:S(2)}, u32[]{:S(2)}) collective-permute-start(bf16[3,64,512]{2,1,0:T(8,128)(2,1)S(1)} %shard_map.93.refs_0_), channel_id=1, source_target_pairs={{0,96},{16,112},{32,0},{48,16},{64,32},{80,48},{96,64},{112,80},{1... | collective-permute-start | bytes 589832 | tf_op jit(solution)/shard_map/ppermute | solution.py:383
  41.6 2.7 %collective-permute-start.8 = (bf16[3,64,512]{2,1,0:T(8,128)(2,1)S(1)}, bf16[3,64,512]{2,1,0:T(8,128)(2,1)S(1)}, u32[]{:S(2)}, u32[]{:S(2)}) collective-permute-start(bf16[3,64,512]{2,1,0:T(8,128)(2,1)S(1)} %shard_map.93.refs_0_), channel_id=1, source_target_pairs={{0,16},{16,0},{32,48},{48,32},{64,80},{80,64},{96,112},{112,96},{1... | collective-permute-start | bytes 589832 | tf_op jit(solution)/shard_map/ppermute | solution.py:386
  44.3 3.8 %attention_first.1 = bf16[3072,512]{1,0:T(8,128)(2,1)S(1)} custom-call(bf16[3072,512]{1,0:T(8,128)(2,1)S(1)} %copy-done, bf16[2,1024,512]{2,1,0:T(8,128)(2,1)S(1)} %collective-permute-done.4.b_ref, bf16[3072,512]{1,0:T(8,128)(2,1)S(1)} %get-tuple-element.55.k_ref, bf16[3072,512]{1,0:T(8,128)(2,1)S(1)} %get-tuple-element.56.v_ref, ...), custom_call_target="tpu_custom_call", output_to_operand_aliasing={{}: (4, {})} | custom-call | flops 2684354560 | bytes 6291456 | tf_op jit(solution)/shard_map/attention_first/pallas_call | solution.py:274
  48.1 0.1 collective-permute-done.6.refs_2_
  48.2 1.9 %collective-permute-start.10 = (bf16[3,64,512]{2,1,0:T(8,128)(2,1)S(1)}, bf16[3,64,512]{2,1,0:T(8,128)(2,1)S(1)}, u32[]{:S(2)}, u32[]{:S(2)}) collective-permute-start(bf16[3,64,512]{2,1,0:T(8,128)(2,1)S(1)} %collective-permute-done.6.refs_2_), channel_id=1, source_target_pairs={{0,16},{16,0},{32,48},{48,32},{64,80},{80,64},{96,112},{112,96},{1... | collective-permute-start | bytes 589832 | tf_op jit(solution)/shard_map/ppermute | solution.py:386
  50.1 0.5 collective-permute-start.9
  50.6 0.6 collective-permute-done.10.refs_6_
  51.2 0.4 collective-permute-done.11.refs_7_
  51.5 0.3 collective-permute-done.9.refs_5_
  51.8 1.8 %apply_fast.5 = (bf16[200,512]{1,0:T(8,128)(2,1)S(1)}, bf16[200,512]{1,0:T(8,128)(2,1)S(1)}, bf16[3,512,512]{2,1,0:T(8,128)(2,1)S(1)}) custom-call(s32[33]{0:T(128)S(1)} %copy-done.3, bf16[16,192,512]{2,1,0:T(8,128)(2,1)S(1)} %bitcast.4, bf16[16,192,512]{2,1,0:T(8,128)(2,1)S(1)} %bitcast.9, bf16[16,192,512]{2,1,0:T(8,128)(2,1)S(1)} %bitcast.14, ...), custom_call_target="tpu_custom_call" | custom-call | flops 603979776 | bytes 2097152 | tf_op jit(solution)/shard_map/apply_fast/pallas_call | solution.py:329
  53.7 3.4 %apply_fast.8 = (bf16[200,512]{1,0:T(8,128)(2,1)S(1)}, bf16[200,512]{1,0:T(8,128)(2,1)S(1)}, bf16[200,512]{1,0:T(8,128)(2,1)S(1)}, bf16[200,512]{1,0:T(8,128)(2,1)S(1)}, bf16[200,512]{1,0:T(8,128)(2,1)S(1)}) custom-call(s32[33]{0:T(128)S(1)} %copy-done.3, bf16[16,192,512]{2,1,0:T(8,128)(2,1)S(1)} %bitcast.5, bf16[16,192,512]{2,1,0:T(8,128)(2,1)S(1)} %bitcast.10, ...), custom_call_target="tpu_custom_call" | custom-call | flops 1509949440 | bytes 5242880 | tf_op jit(solution)/shard_map/apply_fast/pallas_call | solution.py:329
  57.1 3.0 %collective-permute-start.22 = (bf16[200,512]{1,0:T(8,128)(2,1)S(1)}, bf16[200,512]{1,0:T(8,128)(2,1)S(1)}, u32[]{:S(2)}, u32[]{:S(2)}) collective-permute-start(bf16[200,512]{1,0:T(8,128)(2,1)S(1)} %get-tuple-element.84), channel_id=1, source_target_pairs={{0,2},{1,3},{2,0},{3,1},{4,6},{5,7},{6,4},{7,5},{8,10},{9,11},{10,... | collective-permute-start | bytes 614408 | tf_op jit(solution)/shard_map/ppermute | solution.py:424
  60.0 2.5 %collective-permute-start.23 = (bf16[200,512]{1,0:T(8,128)(2,1)S(1)}, bf16[200,512]{1,0:T(8,128)(2,1)S(1)}, u32[]{:S(2)}, u32[]{:S(2)}) collective-permute-start(bf16[200,512]{1,0:T(8,128)(2,1)S(1)} %get-tuple-element.85), channel_id=1, source_target_pairs={{0,4},{1,5},{2,6},{3,7},{4,8},{5,9},{6,10},{7,11},{8,12},{9,13},{1... | collective-permute-start | bytes 614408 | tf_op jit(solution)/shard_map/ppermute | solution.py:424
  62.5 0.8 collective-permute-start.24
  63.3 0.7 collective-permute-start.26
  64.0 2.8 %apply_fast.7 = (bf16[200,512]{1,0:T(8,128)(2,1)S(1)}, bf16[200,512]{1,0:T(8,128)(2,1)S(1)}, bf16[200,512]{1,0:T(8,128)(2,1)S(1)}, bf16[200,512]{1,0:T(8,128)(2,1)S(1)}) custom-call(s32[33]{0:T(128)S(1)} %copy-done.3, bf16[16,192,512]{2,1,0:T(8,128)(2,1)S(1)} %bitcast.6, bf16[16,192,512]{2,1,0:T(8,128)(2,1)S(1)} %bitcast.11, ...), custom_call_target="tpu_custom_call" | custom-call | flops 1207959552 | bytes 4194304 | tf_op jit(solution)/shard_map/apply_fast/pallas_call | solution.py:329
  66.8 2.8 %apply_fast.6 = (bf16[200,512]{1,0:T(8,128)(2,1)S(1)}, bf16[200,512]{1,0:T(8,128)(2,1)S(1)}, bf16[200,512]{1,0:T(8,128)(2,1)S(1)}, bf16[200,512]{1,0:T(8,128)(2,1)S(1)}) custom-call(s32[33]{0:T(128)S(1)} %copy-done.3, bf16[16,192,512]{2,1,0:T(8,128)(2,1)S(1)} %bitcast.7, bf16[16,192,512]{2,1,0:T(8,128)(2,1)S(1)} %bitcast.12, ...), custom_call_target="tpu_custom_call" | custom-call | flops 1207959552 | bytes 4194304 | tf_op jit(solution)/shard_map/apply_fast/pallas_call | solution.py:329
  69.7 3.2 %collective-permute-start.18 = (bf16[200,512]{1,0:T(8,128)(2,1)S(1)}, bf16[200,512]{1,0:T(8,128)(2,1)S(1)}, u32[]{:S(2)}, u32[]{:S(2)}) collective-permute-start(bf16[200,512]{1,0:T(8,128)(2,1)S(1)} %get-tuple-element.80), channel_id=1, source_target_pairs={{0,6},{1,7},{2,4},{3,5},{4,10},{5,11},{6,8},{7,9},{8,14},{9,15},{1... | collective-permute-start | bytes 614408 | tf_op jit(solution)/shard_map/ppermute | solution.py:424
  72.8 0.8 collective-permute-start.19
  73.6 2.0 %collective-permute-start.20 = (bf16[200,512]{1,0:T(8,128)(2,1)S(1)}, bf16[200,512]{1,0:T(8,128)(2,1)S(1)}, u32[]{:S(2)}, u32[]{:S(2)}) collective-permute-start(bf16[200,512]{1,0:T(8,128)(2,1)S(1)} %get-tuple-element.82), channel_id=1, source_target_pairs={{0,11},{1,8},{2,9},{3,10},{4,15},{5,12},{6,13},{7,14},{8,3},{9,0},... | collective-permute-start | bytes 614408 | tf_op jit(solution)/shard_map/ppermute | solution.py:424
  75.7 1.8 %collective-permute-start.21 = (bf16[200,512]{1,0:T(8,128)(2,1)S(1)}, bf16[200,512]{1,0:T(8,128)(2,1)S(1)}, u32[]{:S(2)}, u32[]{:S(2)}) collective-permute-start(bf16[200,512]{1,0:T(8,128)(2,1)S(1)} %get-tuple-element.83), channel_id=1, source_target_pairs={{0,8},{1,9},{2,10},{3,11},{4,12},{5,13},{6,14},{7,15},{8,0},{9,1},... | collective-permute-start | bytes 614408 | tf_op jit(solution)/shard_map/ppermute | solution.py:424
  77.4 3.5 %collective-permute-start.14 = (bf16[200,512]{1,0:T(8,128)(2,1)S(1)}, bf16[200,512]{1,0:T(8,128)(2,1)S(1)}, u32[]{:S(2)}, u32[]{:S(2)}) collective-permute-start(bf16[200,512]{1,0:T(8,128)(2,1)S(1)} %get-tuple-element.76), channel_id=1, source_target_pairs={{0,10},{1,11},{2,8},{3,9},{4,14},{5,15},{6,12},{7,13},{8,2},{9,3},... | collective-permute-start | bytes 614408 | tf_op jit(solution)/shard_map/ppermute | solution.py:424
  80.9 2.0 %collective-permute-start.15 = (bf16[200,512]{1,0:T(8,128)(2,1)S(1)}, bf16[200,512]{1,0:T(8,128)(2,1)S(1)}, u32[]{:S(2)}, u32[]{:S(2)}) collective-permute-start(bf16[200,512]{1,0:T(8,128)(2,1)S(1)} %get-tuple-element.77), channel_id=1, source_target_pairs={{0,7},{1,4},{2,5},{3,6},{4,11},{5,8},{6,9},{7,10},{8,15},{9,12},{1... | collective-permute-start | bytes 614408 | tf_op jit(solution)/shard_map/ppermute | solution.py:424
  83.0 17.1 %collective-permute-done.19.refs_7_ = bf16[200,512]{1,0:T(8,128)(2,1)S(1)} collective-permute-done((bf16[200,512]{1,0:T(8,128)(2,1)S(1)}, bf16[200,512]{1,0:T(8,128)(2,1)S(1)}, u32[]{:S(2)}, u32[]{:S(2)}) %collective-permute-start.19) | collective-permute-done | bytes 204832 | tf_op jit(solution)/shard_map/ppermute | solution.py:424
  100.1 0.1 collective-permute-start.12
  100.2 2.3 %collective-permute-start.13 = (bf16[200,512]{1,0:T(8,128)(2,1)S(1)}, bf16[200,512]{1,0:T(8,128)(2,1)S(1)}, u32[]{:S(2)}, u32[]{:S(2)}) collective-permute-start(bf16[200,512]{1,0:T(8,128)(2,1)S(1)} %get-tuple-element.74), channel_id=1, source_target_pairs={{0,15},{1,12},{2,13},{3,14},{4,3},{5,0},{6,1},{7,2},{8,7},{9,4},{1... | collective-permute-start | bytes 614408 | tf_op jit(solution)/shard_map/ppermute | solution.py:424
  102.5 1.5 %apply_fast.9.refs_15_ = bf16[200,512]{1,0:T(8,128)(2,1)S(1)} custom-call(s32[33]{0:T(128)S(1)} %copy-done.3, bf16[16,192,512]{2,1,0:T(8,128)(2,1)S(1)} %bitcast.8, bf16[16,192,512]{2,1,0:T(8,128)(2,1)S(1)} %bitcast.13, bf16[16,192,512]{2,1,0:T(8,128)(2,1)S(1)} %bitcast.18, f32[1,8192]{1,0:T(1,128)S(1)} %bitcast.23, ...), custom_call_target="tpu_custom_call" | custom-call | flops 301989888 | bytes 1048576 | tf_op jit(solution)/shard_map/apply_fast/pallas_call | solution.py:329
  104.1 10.5 %collective-permute-done.16.refs_4_ = bf16[200,512]{1,0:T(8,128)(2,1)S(1)} collective-permute-done((bf16[200,512]{1,0:T(8,128)(2,1)S(1)}, bf16[200,512]{1,0:T(8,128)(2,1)S(1)}, u32[]{:S(2)}, u32[]{:S(2)}) %collective-permute-start.16) | collective-permute-done | bytes 204832 | tf_op jit(solution)/shard_map/ppermute | solution.py:424
  114.5 0.5 collective-permute-done.13.refs_1_
  115.0 2.5 %scale_rows.1 = bf16[192,8192]{1,0:T(8,128)(2,1)} custom-call(s32[33]{0:T(128)S(1)} %copy-done.3, bf16[200,512]{1,0:T(8,128)(2,1)S(1)} %collective-permute-done.12.refs_0_, bf16[200,512]{1,0:T(8,128)(2,1)S(1)} %collective-permute-done.13.refs_1_, bf16[200,512]{1,0:T(8,128)(2,1)S(1)} %collective-permute-done.14.refs_2_, ...), custom_call_target="tpu_custom_call" | custom-call | tf_op jit(solution)/shard_map/scale_rows/pallas_call | solution.py:365
  (36 shorter events, 0.1 us)
Async XLA Ops:
  0.0 7.2 %copy-start.7 = (f32[1,3072]{1,0:T(1,128)S(1)}, f32[1,3072]{1,0:T(1,128)}, u32[]{:S(2)}) copy-start(f32[1,3072]{1,0:T(1,128)} %rate_ref.1) | copy-start | bytes 36868
  0.0 7.2 %copy-start.4 = (bf16[1,512,512]{2,1,0:T(8,128)(2,1)S(1)}, bf16[1,512,512]{2,1,0:T(8,128)(2,1)}, u32[]{:S(2)}) copy-start(bf16[1,512,512]{2,1,0:T(8,128)(2,1)} %wi_ref.1) | copy-start | bytes 1572868
  0.0 7.2 %copy-start.5 = (bf16[1,512,512]{2,1,0:T(8,128)(2,1)S(1)}, bf16[1,512,512]{2,1,0:T(8,128)(2,1)}, u32[]{:S(2)}) copy-start(bf16[1,512,512]{2,1,0:T(8,128)(2,1)} %wu_ref.1) | copy-start | bytes 1572868
  0.0 7.2 %copy-start.6 = (bf16[1,512,512]{2,1,0:T(8,128)(2,1)S(1)}, bf16[1,512,512]{2,1,0:T(8,128)(2,1)}, u32[]{:S(2)}) copy-start(bf16[1,512,512]{2,1,0:T(8,128)(2,1)} %wo_ref.1) | copy-start | bytes 1572868
  2.2 42.1 %collective-permute-start.4 = (bf16[2,1024,512]{2,1,0:T(8,128)(2,1)S(1)}, bf16[2,1024,512]{2,1,0:T(8,128)(2,1)S(1)}, u32[]{:S(2)}, u32[]{:S(2)}) collective-permute-start(bf16[2,1024,512]{2,1,0:T(8,128)(2,1)S(1)} %get-tuple-element.66), channel_id=1, source_target_pairs={{0,16},{16,32},{32,48},{48,64},{64,80},{80,96},{96,112},{1,17},{17... | collective-permute-start | bytes 6291464 | tf_op jit(solution)/shard_map/ppermute | solution.py:389
  7.2 18.0 %copy-start = (bf16[3072,512]{1,0:T(8,128)(2,1)S(1)}, bf16[3072,512]{1,0:T(8,128)(2,1)}, u32[]{:S(2)}) copy-start(bf16[3072,512]{1,0:T(8,128)(2,1)} %q_ref.2) | copy-start | bytes 9437188
  20.7 2.4 %collective-permute-start = (bf16[3,256,512]{2,1,0:T(8,128)(2,1)S(1)}, bf16[3,256,512]{2,1,0:T(8,128)(2,1)S(1)}, u32[]{:S(2)}, u32[]{:S(2)}) collective-permute-start(bf16[3,256,512]{2,1,0:T(8,128)(2,1)S(1)} %get-tuple-element.50), channel_id=1, source_target_pairs={{0,16},{16,0},{32,48},{48,32},{64,80},{80,64},{96,112},{112,96},{1... | collective-permute-start | bytes 2359304 | tf_op jit(solution)/shard_map/ppermute | solution.py:386
  23.3 6.7 %collective-permute-start.1 = (bf16[3,64,512]{2,1,0:T(8,128)(2,1)S(1)}, bf16[3,64,512]{2,1,0:T(8,128)(2,1)S(1)}, u32[]{:S(2)}, u32[]{:S(2)}) collective-permute-start(bf16[3,64,512]{2,1,0:T(8,128)(2,1)S(1)} %get-tuple-element.57), channel_id=1, source_target_pairs={{0,96},{16,112},{32,0},{48,16},{64,32},{80,48},{96,64},{112,80},{1... | collective-permute-start | bytes 589832 | tf_op jit(solution)/shard_map/ppermute | solution.py:383
  25.2 11.1 %collective-permute-start.2 = (bf16[3,64,512]{2,1,0:T(8,128)(2,1)S(1)}, bf16[3,64,512]{2,1,0:T(8,128)(2,1)S(1)}, u32[]{:S(2)}, u32[]{:S(2)}) collective-permute-start(bf16[3,64,512]{2,1,0:T(8,128)(2,1)S(1)} %get-tuple-element.62), channel_id=1, source_target_pairs={{0,32},{16,48},{32,64},{48,80},{64,96},{80,112},{96,0},{112,16},{1... | collective-permute-start | bytes 589832 | tf_op jit(solution)/shard_map/ppermute | solution.py:383
  30.1 6.3 %collective-permute-start.3 = (bf16[3,64,512]{2,1,0:T(8,128)(2,1)S(1)}, bf16[3,64,512]{2,1,0:T(8,128)(2,1)S(1)}, u32[]{:S(2)}, u32[]{:S(2)}) collective-permute-start(bf16[3,64,512]{2,1,0:T(8,128)(2,1)S(1)} %shard_map.92), channel_id=1, source_target_pairs={{0,96},{16,112},{32,0},{48,16},{64,32},{80,48},{96,64},{112,80},{1... | collective-permute-start | bytes 589832 | tf_op jit(solution)/shard_map/ppermute | solution.py:383
  36.6 15.2 %copy-start.1 = (bf16[3072,512]{1,0:T(8,128)(2,1)S(1)}, bf16[3072,512]{1,0:T(8,128)(2,1)}, u32[]{:S(2)}) copy-start(bf16[3072,512]{1,0:T(8,128)(2,1)} %param.16) | copy-start | bytes 9437188
  36.6 15.2 %copy-start.2 = (f32[8192]{0:T(1024)S(1)}, f32[8192]{0:T(1024)}, u32[]{:S(2)}) copy-start(f32[8192]{0:T(1024)} %param.17) | copy-start | bytes 98308
  36.6 15.2 %copy-start.3 = (s32[33]{0:T(128)S(1)}, s32[33]{0:T(128)}, u32[]{:S(2)}) copy-start(s32[33]{0:T(128)} %get-tuple-element.47.table) | copy-start | bytes 400
  36.6 11.5 %collective-permute-start.5 = (bf16[3,64,512]{2,1,0:T(8,128)(2,1)S(1)}, bf16[3,64,512]{2,1,0:T(8,128)(2,1)S(1)}, u32[]{:S(2)}, u32[]{:S(2)}) collective-permute-start(bf16[3,64,512]{2,1,0:T(8,128)(2,1)S(1)} %shard_map.93.refs_0_), channel_id=1, source_target_pairs={{0,64},{16,80},{32,96},{48,112},{64,0},{80,16},{96,32},{112,48},{1... | collective-permute-start | bytes 589832 | tf_op jit(solution)/shard_map/ppermute | solution.py:383
  38.9 9.2 %collective-permute-start.6 = (bf16[3,64,512]{2,1,0:T(8,128)(2,1)S(1)}, bf16[3,64,512]{2,1,0:T(8,128)(2,1)S(1)}, u32[]{:S(2)}, u32[]{:S(2)}) collective-permute-start(bf16[3,64,512]{2,1,0:T(8,128)(2,1)S(1)} %shard_map.93.refs_0_), channel_id=1, source_target_pairs={{0,32},{16,48},{32,64},{48,80},{64,96},{80,112},{96,0},{112,16},{1... | collective-permute-start | bytes 589832 | tf_op jit(solution)/shard_map/ppermute | solution.py:383
  40.0 8.2 %collective-permute-start.7 = (bf16[3,64,512]{2,1,0:T(8,128)(2,1)S(1)}, bf16[3,64,512]{2,1,0:T(8,128)(2,1)S(1)}, u32[]{:S(2)}, u32[]{:S(2)}) collective-permute-start(bf16[3,64,512]{2,1,0:T(8,128)(2,1)S(1)} %shard_map.93.refs_0_), channel_id=1, source_target_pairs={{0,96},{16,112},{32,0},{48,16},{64,32},{80,48},{96,64},{112,80},{1... | collective-permute-start | bytes 589832 | tf_op jit(solution)/shard_map/ppermute | solution.py:383
  41.6 9.0 %collective-permute-start.8 = (bf16[3,64,512]{2,1,0:T(8,128)(2,1)S(1)}, bf16[3,64,512]{2,1,0:T(8,128)(2,1)S(1)}, u32[]{:S(2)}, u32[]{:S(2)}) collective-permute-start(bf16[3,64,512]{2,1,0:T(8,128)(2,1)S(1)} %shard_map.93.refs_0_), channel_id=1, source_target_pairs={{0,16},{16,0},{32,48},{48,32},{64,80},{80,64},{96,112},{112,96},{1... | collective-permute-start | bytes 589832 | tf_op jit(solution)/shard_map/ppermute | solution.py:386
  48.2 3.0 %collective-permute-start.10 = (bf16[3,64,512]{2,1,0:T(8,128)(2,1)S(1)}, bf16[3,64,512]{2,1,0:T(8,128)(2,1)S(1)}, u32[]{:S(2)}, u32[]{:S(2)}) collective-permute-start(bf16[3,64,512]{2,1,0:T(8,128)(2,1)S(1)} %collective-permute-done.6.refs_2_), channel_id=1, source_target_pairs={{0,16},{16,0},{32,48},{48,32},{64,80},{80,64},{96,112},{112,96},{1... | collective-permute-start | bytes 589832 | tf_op jit(solution)/shard_map/ppermute | solution.py:386
  50.1 1.4 %collective-permute-start.11 = (bf16[3,64,512]{2,1,0:T(8,128)(2,1)S(1)}, bf16[3,64,512]{2,1,0:T(8,128)(2,1)S(1)}, u32[]{:S(2)}, u32[]{:S(2)}) collective-permute-start(bf16[3,64,512]{2,1,0:T(8,128)(2,1)S(1)} %collective-permute-done.7.refs_3_), channel_id=1, source_target_pairs={{0,16},{16,0},{32,48},{48,32},{64,80},{80,64},{96,112},{112,96},{1... | collective-permute-start | bytes 589832 | tf_op jit(solution)/shard_map/ppermute | solution.py:386
  50.1 1.7 %collective-permute-start.9 = (bf16[3,64,512]{2,1,0:T(8,128)(2,1)S(1)}, bf16[3,64,512]{2,1,0:T(8,128)(2,1)S(1)}, u32[]{:S(2)}, u32[]{:S(2)}) collective-permute-start(bf16[3,64,512]{2,1,0:T(8,128)(2,1)S(1)} %collective-permute-done.5.refs_1_), channel_id=1, source_target_pairs={{0,16},{16,0},{32,48},{48,32},{64,80},{80,64},{96,112},{112,96},{1... | collective-permute-start | bytes 589832 | tf_op jit(solution)/shard_map/ppermute | solution.py:386
  57.1 12.6 %collective-permute-start.22 = (bf16[200,512]{1,0:T(8,128)(2,1)S(1)}, bf16[200,512]{1,0:T(8,128)(2,1)S(1)}, u32[]{:S(2)}, u32[]{:S(2)}) collective-permute-start(bf16[200,512]{1,0:T(8,128)(2,1)S(1)} %get-tuple-element.84), channel_id=1, source_target_pairs={{0,2},{1,3},{2,0},{3,1},{4,6},{5,7},{6,4},{7,5},{8,10},{9,11},{10,... | collective-permute-start | bytes 614408 | tf_op jit(solution)/shard_map/ppermute | solution.py:424
  60.0 12.8 %collective-permute-start.23 = (bf16[200,512]{1,0:T(8,128)(2,1)S(1)}, bf16[200,512]{1,0:T(8,128)(2,1)S(1)}, u32[]{:S(2)}, u32[]{:S(2)}) collective-permute-start(bf16[200,512]{1,0:T(8,128)(2,1)S(1)} %get-tuple-element.85), channel_id=1, source_target_pairs={{0,4},{1,5},{2,6},{3,7},{4,8},{5,9},{6,10},{7,11},{8,12},{9,13},{1... | collective-permute-start | bytes 614408 | tf_op jit(solution)/shard_map/ppermute | solution.py:424
  62.5 11.1 %collective-permute-start.24 = (bf16[200,512]{1,0:T(8,128)(2,1)S(1)}, bf16[200,512]{1,0:T(8,128)(2,1)S(1)}, u32[]{:S(2)}, u32[]{:S(2)}) collective-permute-start(bf16[200,512]{1,0:T(8,128)(2,1)S(1)} %get-tuple-element.86), channel_id=1, source_target_pairs={{0,1},{1,2},{2,3},{3,0},{4,5},{5,6},{6,7},{7,4},{8,9},{9,10},{10,1... | collective-permute-start | bytes 614408 | tf_op jit(solution)/shard_map/ppermute | solution.py:424
  63.3 12.4 %collective-permute-start.25 = (bf16[200,512]{1,0:T(8,128)(2,1)S(1)}, bf16[200,512]{1,0:T(8,128)(2,1)S(1)}, u32[]{:S(2)}, u32[]{:S(2)}) collective-permute-start(bf16[200,512]{1,0:T(8,128)(2,1)S(1)} %get-tuple-element.87), channel_id=1, source_target_pairs={{0,12},{1,13},{2,14},{3,15},{4,0},{5,1},{6,2},{7,3},{8,4},{9,5},{1... | collective-permute-start | bytes 614408 | tf_op jit(solution)/shard_map/ppermute | solution.py:424
  63.3 14.2 %collective-permute-start.26 = (bf16[200,512]{1,0:T(8,128)(2,1)S(1)}, bf16[200,512]{1,0:T(8,128)(2,1)S(1)}, u32[]{:S(2)}, u32[]{:S(2)}) collective-permute-start(bf16[200,512]{1,0:T(8,128)(2,1)S(1)} %get-tuple-element.88), channel_id=1, source_target_pairs={{0,3},{1,0},{2,1},{3,2},{4,7},{5,4},{6,5},{7,6},{8,11},{9,8},{10,9... | collective-permute-start | bytes 614408 | tf_op jit(solution)/shard_map/ppermute | solution.py:424
  69.7 11.3 %collective-permute-start.18 = (bf16[200,512]{1,0:T(8,128)(2,1)S(1)}, bf16[200,512]{1,0:T(8,128)(2,1)S(1)}, u32[]{:S(2)}, u32[]{:S(2)}) collective-permute-start(bf16[200,512]{1,0:T(8,128)(2,1)S(1)} %get-tuple-element.80), channel_id=1, source_target_pairs={{0,6},{1,7},{2,4},{3,5},{4,10},{5,11},{6,8},{7,9},{8,14},{9,15},{1... | collective-permute-start | bytes 614408 | tf_op jit(solution)/shard_map/ppermute | solution.py:424
  72.8 27.2 %collective-permute-start.19 = (bf16[200,512]{1,0:T(8,128)(2,1)S(1)}, bf16[200,512]{1,0:T(8,128)(2,1)S(1)}, u32[]{:S(2)}, u32[]{:S(2)}) collective-permute-start(bf16[200,512]{1,0:T(8,128)(2,1)S(1)} %get-tuple-element.81), channel_id=1, source_target_pairs={{0,14},{1,15},{2,12},{3,13},{4,2},{5,3},{6,0},{7,1},{8,6},{9,7},{1... | collective-permute-start | bytes 614408 | tf_op jit(solution)/shard_map/ppermute | solution.py:424
  73.6 26.5 %collective-permute-start.20 = (bf16[200,512]{1,0:T(8,128)(2,1)S(1)}, bf16[200,512]{1,0:T(8,128)(2,1)S(1)}, u32[]{:S(2)}, u32[]{:S(2)}) collective-permute-start(bf16[200,512]{1,0:T(8,128)(2,1)S(1)} %get-tuple-element.82), channel_id=1, source_target_pairs={{0,11},{1,8},{2,9},{3,10},{4,15},{5,12},{6,13},{7,14},{8,3},{9,0},... | collective-permute-start | bytes 614408 | tf_op jit(solution)/shard_map/ppermute | solution.py:424
  75.7 24.4 %collective-permute-start.21 = (bf16[200,512]{1,0:T(8,128)(2,1)S(1)}, bf16[200,512]{1,0:T(8,128)(2,1)S(1)}, u32[]{:S(2)}, u32[]{:S(2)}) collective-permute-start(bf16[200,512]{1,0:T(8,128)(2,1)S(1)} %get-tuple-element.83), channel_id=1, source_target_pairs={{0,8},{1,9},{2,10},{3,11},{4,12},{5,13},{6,14},{7,15},{8,0},{9,1},... | collective-permute-start | bytes 614408 | tf_op jit(solution)/shard_map/ppermute | solution.py:424
  77.4 22.8 %collective-permute-start.14 = (bf16[200,512]{1,0:T(8,128)(2,1)S(1)}, bf16[200,512]{1,0:T(8,128)(2,1)S(1)}, u32[]{:S(2)}, u32[]{:S(2)}) collective-permute-start(bf16[200,512]{1,0:T(8,128)(2,1)S(1)} %get-tuple-element.76), channel_id=1, source_target_pairs={{0,10},{1,11},{2,8},{3,9},{4,14},{5,15},{6,12},{7,13},{8,2},{9,3},... | collective-permute-start | bytes 614408 | tf_op jit(solution)/shard_map/ppermute | solution.py:424
  80.9 23.2 %collective-permute-start.15 = (bf16[200,512]{1,0:T(8,128)(2,1)S(1)}, bf16[200,512]{1,0:T(8,128)(2,1)S(1)}, u32[]{:S(2)}, u32[]{:S(2)}) collective-permute-start(bf16[200,512]{1,0:T(8,128)(2,1)S(1)} %get-tuple-element.77), channel_id=1, source_target_pairs={{0,7},{1,4},{2,5},{3,6},{4,11},{5,8},{6,9},{7,10},{8,15},{9,12},{1... | collective-permute-start | bytes 614408 | tf_op jit(solution)/shard_map/ppermute | solution.py:424
  100.1 14.5 %collective-permute-start.16 = (bf16[200,512]{1,0:T(8,128)(2,1)S(1)}, bf16[200,512]{1,0:T(8,128)(2,1)S(1)}, u32[]{:S(2)}, u32[]{:S(2)}) collective-permute-start(bf16[200,512]{1,0:T(8,128)(2,1)S(1)} %get-tuple-element.78), channel_id=1, source_target_pairs={{0,13},{1,14},{2,15},{3,12},{4,1},{5,2},{6,3},{7,0},{8,5},{9,6},{1... | collective-permute-start | bytes 614408 | tf_op jit(solution)/shard_map/ppermute | solution.py:424
  100.1 14.4 %collective-permute-start.17 = (bf16[200,512]{1,0:T(8,128)(2,1)S(1)}, bf16[200,512]{1,0:T(8,128)(2,1)S(1)}, u32[]{:S(2)}, u32[]{:S(2)}) collective-permute-start(bf16[200,512]{1,0:T(8,128)(2,1)S(1)} %get-tuple-element.79), channel_id=1, source_target_pairs={{0,9},{1,10},{2,11},{3,8},{4,13},{5,14},{6,15},{7,12},{8,1},{9,2},... | collective-permute-start | bytes 614408 | tf_op jit(solution)/shard_map/ppermute | solution.py:424
  100.1 14.4 %collective-permute-start.12 = (bf16[200,512]{1,0:T(8,128)(2,1)S(1)}, bf16[200,512]{1,0:T(8,128)(2,1)S(1)}, u32[]{:S(2)}, u32[]{:S(2)}) collective-permute-start(bf16[200,512]{1,0:T(8,128)(2,1)S(1)} %get-tuple-element.73), channel_id=1, source_target_pairs={{0,5},{1,6},{2,7},{3,4},{4,9},{5,10},{6,11},{7,8},{8,13},{9,14},{1... | collective-permute-start | bytes 614408 | tf_op jit(solution)/shard_map/ppermute | solution.py:424
  100.2 14.8 %collective-permute-start.13 = (bf16[200,512]{1,0:T(8,128)(2,1)S(1)}, bf16[200,512]{1,0:T(8,128)(2,1)S(1)}, u32[]{:S(2)}, u32[]{:S(2)}) collective-permute-start(bf16[200,512]{1,0:T(8,128)(2,1)S(1)} %get-tuple-element.74), channel_id=1, source_target_pairs={{0,15},{1,12},{2,13},{3,14},{4,3},{5,0},{6,1},{7,2},{8,7},{9,4},{1... | collective-permute-start | bytes 614408 | tf_op jit(solution)/shard_map/ppermute | solution.py:424

commit v5 on v3

--- a/solution.py
+++ b/solution.py
@@ -155,9 +155,9 @@
 
 
 SIDE = 4
-SHIFTS = ((1, 1), (3, 3), (2, 2), (1, 3), (3, 1), (2, 1), (1, 2), (3, 2),
-          (2, 3), (2, 0), (0, 2), (1, 0), (0, 1), (3, 0), (0, 3), (0, 0))
-GROUPS = (2, 4, 4, 5, 1)
+SHIFTS = ((1, 1), (3, 3), (1, 3), (3, 1), (2, 2), (2, 1), (1, 2), (3, 2),
+          (2, 3), (0, 2), (2, 0), (0, 1), (1, 0), (0, 3), (3, 0), (0, 0))
+GROUPS = (2, 6, 7, 1)
 HEAD_AT, TARGET_AT = 0, 1
 SOURCE_AT = TARGET_AT + len(SHIFTS)
 

time: 115 us -> 113 us (0.983)
  the two profiles are of different devices: /device:TPU:6 before, /device:TPU:1 now
where the time goes in v5:
time: 113 us; the launch traced here: 112 us
  starting transfers between devices  53 us (47%)
  Pallas kernels  41.6 us (37%)
  waiting for transfers between devices  17.2 us (15%)
    ppermute x15, starting transfers between devices, layer(): lax.ppermute(y, 'head', [(h, shifted(h, dx, dy)) for h in range(n_head)])  33.3 us
    pallas_call x1, Pallas kernels, increments(): pl.pallas_call(increments_kernel, in_specs=[anywhere, anywhere, inside, i...  13.5 us
    ppermute x15, waiting for transfers between devices, layer(): lax.ppermute(y, 'head', [(h, shifted(h, dx, dy)) for h in range(n_head)])  12.5 us
    pallas_call x4, Pallas kernels, applied(): pl.pallas_call(functools.partial(apply_kernel, count=count, n_pieces=len(...  11.8 us
    ppermute x6, starting transfers between devices, along_z(): lax.ppermute(x, 'ctx', [(i, (i // 2 + d) % z_size * 2 + i % 2) for i in r...  9.55 us
    pallas_call x2, Pallas kernels, attention_own(): pl.pallas_call(functools.partial(attention_own_kernel, tq=tq, per=per, st...  7.31 us
    ppermute x5, starting transfers between devices, swapped(): return lax.ppermute(x, 'ctx', [(i, i ^ 1) for i in range(n_ctx)])  5.19 us
    ppermute x1, starting transfers between devices, layer(): before = lax.ppermute(tail, 'ctx', [(i, i + 1) for i in range(n_ctx - 1)])  4.92 us
  transfers between devices with their start and end apart: 27, of which 10 were waited for; matrix products, arithmetic and copies ran while one was open for 0% of the time, Pallas kernels for 27%

profile of v5, /device:TPU:1, one launch (start us, length us, event | category | flops | bytes accessed | tf_op | source)
XLA Modules:
  0.0 112.2 jit_solution(16830320090471623329)
XLA Ops:
  0.0 2.2 %tails.1 = (bf16[2,1024,512]{2,1,0:T(8,128)(2,1)S(1)}, s32[33]{0:T(128)}) custom-call(bf16[3072,512]{1,0:T(8,128)(2,1)} %k_hbm.1, bf16[3072,512]{1,0:T(8,128)(2,1)} %v_hbm.1), custom_call_target="tpu_custom_call" | custom-call | tf_op jit(solution)/shard_map/tails/pallas_call | solution.py:185
  2.2 4.9 %collective-permute-start.4 = (bf16[2,1024,512]{2,1,0:T(8,128)(2,1)S(1)}, bf16[2,1024,512]{2,1,0:T(8,128)(2,1)S(1)}, u32[]{:S(2)}, u32[]{:S(2)}) collective-permute-start(bf16[2,1024,512]{2,1,0:T(8,128)(2,1)S(1)} %get-tuple-element.66), channel_id=1, source_target_pairs={{0,16},{16,32},{32,48},{48,64},{64,80},{80,96},{96,112},{1,17},{17... | collective-permute-start | bytes 6291464 | tf_op jit(solution)/shard_map/ppermute | solution.py:387
  7.2 0.0 copy-start
  7.2 13.5 %increments.1 = (bf16[3,256,512]{2,1,0:T(8,128)(2,1)S(1)}, bf16[3,256,512]{2,1,0:T(8,128)(2,1)S(1)}, bf16[3,64,512]{2,1,0:T(8,128)(2,1)S(1)}, bf16[3072,512]{1,0:T(8,128)(2,1)S(1)}, bf16[3072,512]{1,0:T(8,128)(2,1)S(1)}) custom-call(bf16[3072,512]{1,0:T(8,128)(2,1)} %k_hbm.1, bf16[3072,512]{1,0:T(8,128)(2,1)} %v_hbm.1, f32[1,3072]{1,0:T(1,128)S(1)} %copy-done.7, ...), custom_call_target="tpu_custom_call" | custom-call | flops 9663676416 | bytes 9437184 | tf_op jit(solution)/shard_map/increments/pallas_call | solution.py:106
  20.7 0.1 collective-permute-start
  20.8 2.3 %collective-permute-done.got_ref = bf16[3,256,512]{2,1,0:T(8,128)(2,1)S(1)} collective-permute-done((bf16[3,256,512]{2,1,0:T(8,128)(2,1)S(1)}, bf16[3,256,512]{2,1,0:T(8,128)(2,1)S(1)}, u32[]{:S(2)}, u32[]{:S(2)}) %collective-permute-start) | collective-permute-done | bytes 786464 | tf_op jit(solution)/shard_map/ppermute | solution.py:384
  23.1 0.2 shard_map.91
  23.3 2.0 %collective-permute-start.1 = (bf16[3,64,512]{2,1,0:T(8,128)(2,1)S(1)}, bf16[3,64,512]{2,1,0:T(8,128)(2,1)S(1)}, u32[]{:S(2)}, u32[]{:S(2)}) collective-permute-start(bf16[3,64,512]{2,1,0:T(8,128)(2,1)S(1)} %get-tuple-element.57), channel_id=1, source_target_pairs={{0,96},{16,112},{32,0},{48,16},{64,32},{80,48},{96,64},{112,80},{1... | collective-permute-start | bytes 589832 | tf_op jit(solution)/shard_map/ppermute | solution.py:381
  25.2 3.7 %attention_own.2.refs_0_ = bf16[3072,512]{1,0:T(8,128)(2,1)S(1)} custom-call(bf16[3072,512]{1,0:T(8,128)(2,1)S(1)} %copy-done, bf16[3072,512]{1,0:T(8,128)(2,1)S(1)} %get-tuple-element.55.k_ref, bf16[3072,512]{1,0:T(8,128)(2,1)S(1)} %get-tuple-element.56.v_ref), custom_call_target="tpu_custom_call" | custom-call | flops 2684354560 | bytes 8388608 | tf_op jit(solution)/shard_map/attention_own/pallas_call | solution.py:257
  28.9 1.1 collective-permute-done.1.b_ref
  30.1 2.6 %collective-permute-start.3 = (bf16[3,64,512]{2,1,0:T(8,128)(2,1)S(1)}, bf16[3,64,512]{2,1,0:T(8,128)(2,1)S(1)}, u32[]{:S(2)}, u32[]{:S(2)}) collective-permute-start(bf16[3,64,512]{2,1,0:T(8,128)(2,1)S(1)} %shard_map.92), channel_id=1, source_target_pairs={{0,96},{16,112},{32,0},{48,16},{64,32},{80,48},{96,64},{112,80},{1... | collective-permute-start | bytes 589832 | tf_op jit(solution)/shard_map/ppermute | solution.py:381
  32.6 3.7 %attention_own.3._ = bf16[3072,512]{1,0:T(8,128)(2,1)S(1)} custom-call(bf16[3072,512]{1,0:T(8,128)(2,1)S(1)} %copy-done, bf16[3072,512]{1,0:T(8,128)(2,1)S(1)} %get-tuple-element.55.k_ref, bf16[3072,512]{1,0:T(8,128)(2,1)S(1)} %get-tuple-element.56.v_ref, bf16[3072,512]{1,0:T(8,128)(2,1)S(1)} %attention_own.2.refs_0_), custom_call_target="tpu_custom_call", output_to_operand_aliasing={{}: (3, {})} | custom-call | flops 2684354560 | bytes 8388608 | tf_op jit(solution)/shard_map/attention_own/pallas_call | solution.py:257
  36.3 0.3 shard_map.93.refs_0_
  36.6 0.0 copy-start.1
  36.6 0.0 copy-start.2
  36.6 2.3 %collective-permute-start.5 = (bf16[3,64,512]{2,1,0:T(8,128)(2,1)S(1)}, bf16[3,64,512]{2,1,0:T(8,128)(2,1)S(1)}, u32[]{:S(2)}, u32[]{:S(2)}) collective-permute-start(bf16[3,64,512]{2,1,0:T(8,128)(2,1)S(1)} %shard_map.93.refs_0_), channel_id=1, source_target_pairs={{0,64},{16,80},{32,96},{48,112},{64,0},{80,16},{96,32},{112,48},{1... | collective-permute-start | bytes 589832 | tf_op jit(solution)/shard_map/ppermute | solution.py:381
  38.9 1.1 collective-permute-start.6
  40.0 1.6 %collective-permute-start.7 = (bf16[3,64,512]{2,1,0:T(8,128)(2,1)S(1)}, bf16[3,64,512]{2,1,0:T(8,128)(2,1)S(1)}, u32[]{:S(2)}, u32[]{:S(2)}) collective-permute-start(bf16[3,64,512]{2,1,0:T(8,128)(2,1)S(1)} %shard_map.93.refs_0_), channel_id=1, source_target_pairs={{0,96},{16,112},{32,0},{48,16},{64,32},{80,48},{96,64},{112,80},{1... | collective-permute-start | bytes 589832 | tf_op jit(solution)/shard_map/ppermute | solution.py:381
  41.6 2.7 %collective-permute-start.8 = (bf16[3,64,512]{2,1,0:T(8,128)(2,1)S(1)}, bf16[3,64,512]{2,1,0:T(8,128)(2,1)S(1)}, u32[]{:S(2)}, u32[]{:S(2)}) collective-permute-start(bf16[3,64,512]{2,1,0:T(8,128)(2,1)S(1)} %shard_map.93.refs_0_), channel_id=1, source_target_pairs={{0,16},{16,0},{32,48},{48,32},{64,80},{80,64},{96,112},{112,96},{1... | collective-permute-start | bytes 589832 | tf_op jit(solution)/shard_map/ppermute | solution.py:384
  44.3 3.8 %attention_first.1 = bf16[3072,512]{1,0:T(8,128)(2,1)S(1)} custom-call(bf16[3072,512]{1,0:T(8,128)(2,1)S(1)} %copy-done, bf16[2,1024,512]{2,1,0:T(8,128)(2,1)S(1)} %collective-permute-done.4.b_ref, bf16[3072,512]{1,0:T(8,128)(2,1)S(1)} %get-tuple-element.55.k_ref, bf16[3072,512]{1,0:T(8,128)(2,1)S(1)} %get-tuple-element.56.v_ref, ...), custom_call_target="tpu_custom_call", output_to_operand_aliasing={{}: (4, {})} | custom-call | flops 2684354560 | bytes 6291456 | tf_op jit(solution)/shard_map/attention_first/pallas_call | solution.py:272
  48.1 0.1 collective-permute-done.6.refs_2_
  48.2 1.9 %collective-permute-start.10 = (bf16[3,64,512]{2,1,0:T(8,128)(2,1)S(1)}, bf16[3,64,512]{2,1,0:T(8,128)(2,1)S(1)}, u32[]{:S(2)}, u32[]{:S(2)}) collective-permute-start(bf16[3,64,512]{2,1,0:T(8,128)(2,1)S(1)} %collective-permute-done.6.refs_2_), channel_id=1, source_target_pairs={{0,16},{16,0},{32,48},{48,32},{64,80},{80,64},{96,112},{112,96},{1... | collective-permute-start | bytes 589832 | tf_op jit(solution)/shard_map/ppermute | solution.py:384
  50.1 0.5 collective-permute-start.9
  50.6 0.6 collective-permute-done.10.refs_6_
  51.2 0.4 collective-permute-done.11.refs_7_
  51.5 0.3 collective-permute-done.9.refs_5_
  51.8 1.8 %apply_fast.4 = (bf16[200,512]{1,0:T(8,128)(2,1)S(1)}, bf16[200,512]{1,0:T(8,128)(2,1)S(1)}, bf16[3,512,512]{2,1,0:T(8,128)(2,1)S(1)}) custom-call(s32[33]{0:T(128)S(1)} %copy-done.3, bf16[16,192,512]{2,1,0:T(8,128)(2,1)S(1)} %bitcast.4, bf16[16,192,512]{2,1,0:T(8,128)(2,1)S(1)} %bitcast.8, bf16[16,192,512]{2,1,0:T(8,128)(2,1)S(1)} %bitcast.12, ...), custom_call_target="tpu_custom_call" | custom-call | flops 603979776 | bytes 2097152 | tf_op jit(solution)/shard_map/apply_fast/pallas_call | solution.py:327
  53.7 4.5 %apply_fast.6 = (bf16[200,512]{1,0:T(8,128)(2,1)S(1)}, bf16[200,512]{1,0:T(8,128)(2,1)S(1)}, bf16[200,512]{1,0:T(8,128)(2,1)S(1)}, bf16[200,512]{1,0:T(8,128)(2,...) custom-call(s32[33]{0:T(128)S(1)} %copy-done.3, ...), custom_call_target="tpu_custom_call" | custom-call | flops 2113929216 | bytes 7340032 | tf_op jit(solution)/shard_map/apply_fast/pallas_call | solution.py:327
  58.2 5.2 %collective-permute-start.20 = (bf16[200,512]{1,0:T(8,128)(2,1)S(1)}, bf16[200,512]{1,0:T(8,128)(2,1)S(1)}, u32[]{:S(2)}, u32[]{:S(2)}) collective-permute-start(bf16[200,512]{1,0:T(8,128)(2,1)S(1)} %get-tuple-element.82), channel_id=1, source_target_pairs={{0,11},{1,8},{2,9},{3,10},{4,15},{5,12},{6,13},{7,14},{8,3},{9,0},... | collective-permute-start | bytes 614408 | tf_op jit(solution)/shard_map/ppermute | solution.py:421
  63.4 0.4 collective-permute-start.21
  63.8 0.2 collective-permute-start.22
  64.0 0.7 collective-permute-start.23
  64.7 1.2 %collective-permute-start.24 = (bf16[200,512]{1,0:T(8,128)(2,1)S(1)}, bf16[200,512]{1,0:T(8,128)(2,1)S(1)}, u32[]{:S(2)}, u32[]{:S(2)}) collective-permute-start(bf16[200,512]{1,0:T(8,128)(2,1)S(1)} %get-tuple-element.86), channel_id=1, source_target_pairs={{0,4},{1,5},{2,6},{3,7},{4,8},{5,9},{6,10},{7,11},{8,12},{9,13},{1... | collective-permute-start | bytes 614408 | tf_op jit(solution)/shard_map/ppermute | solution.py:421
  65.9 3.9 %apply_fast.5 = (bf16[200,512]{1,0:T(8,128)(2,1)S(1)}, bf16[200,512]{1,0:T(8,128)(2,1)S(1)}, bf16[200,512]{1,0:T(8,128)(2,1)S(1)}, bf16[200,512]{1,0:T(8,128)(2,...) custom-call(s32[33]{0:T(128)S(1)} %copy-done.3, bf16[16,192,512]{2,1,0:T(8,128)(2,1)S(1)} %bitcast.6, ...), custom_call_target="tpu_custom_call" | custom-call | flops 1811939328 | bytes 6291456 | tf_op jit(solution)/shard_map/apply_fast/pallas_call | solution.py:327
  69.8 2.1 %collective-permute-start.25 = (bf16[200,512]{1,0:T(8,128)(2,1)S(1)}, bf16[200,512]{1,0:T(8,128)(2,1)S(1)}, u32[]{:S(2)}, u32[]{:S(2)}) collective-permute-start(bf16[200,512]{1,0:T(8,128)(2,1)S(1)} %get-tuple-element.87), channel_id=1, source_target_pairs={{0,3},{1,0},{2,1},{3,2},{4,7},{5,4},{6,5},{7,6},{8,11},{9,8},{10,9... | collective-permute-start | bytes 614408 | tf_op jit(solution)/shard_map/ppermute | solution.py:421
  71.9 2.0 %collective-permute-start.26 = (bf16[200,512]{1,0:T(8,128)(2,1)S(1)}, bf16[200,512]{1,0:T(8,128)(2,1)S(1)}, u32[]{:S(2)}, u32[]{:S(2)}) collective-permute-start(bf16[200,512]{1,0:T(8,128)(2,1)S(1)} %get-tuple-element.88), channel_id=1, source_target_pairs={{0,12},{1,13},{2,14},{3,15},{4,0},{5,1},{6,2},{7,3},{8,4},{9,5},{1... | collective-permute-start | bytes 614408 | tf_op jit(solution)/shard_map/ppermute | solution.py:421
  73.9 3.2 %collective-permute-start.14 = (bf16[200,512]{1,0:T(8,128)(2,1)S(1)}, bf16[200,512]{1,0:T(8,128)(2,1)S(1)}, u32[]{:S(2)}, u32[]{:S(2)}) collective-permute-start(bf16[200,512]{1,0:T(8,128)(2,1)S(1)} %get-tuple-element.76), channel_id=1, source_target_pairs={{0,7},{1,4},{2,5},{3,6},{4,11},{5,8},{6,9},{7,10},{8,15},{9,12},{1... | collective-permute-start | bytes 614408 | tf_op jit(solution)/shard_map/ppermute | solution.py:421
  77.1 0.4 collective-permute-start.15
  77.5 0.5 collective-permute-done.24.refs_12_
  78.0 3.9 %collective-permute-start.16 = (bf16[200,512]{1,0:T(8,128)(2,1)S(1)}, bf16[200,512]{1,0:T(8,128)(2,1)S(1)}, u32[]{:S(2)}, u32[]{:S(2)}) collective-permute-start(bf16[200,512]{1,0:T(8,128)(2,1)S(1)} %get-tuple-element.78), channel_id=1, source_target_pairs={{0,10},{1,11},{2,8},{3,9},{4,14},{5,15},{6,12},{7,13},{8,2},{9,3},... | collective-permute-start | bytes 614408 | tf_op jit(solution)/shard_map/ppermute | solution.py:421
  81.8 4.3 %collective-permute-start.17 = (bf16[200,512]{1,0:T(8,128)(2,1)S(1)}, bf16[200,512]{1,0:T(8,128)(2,1)S(1)}, u32[]{:S(2)}, u32[]{:S(2)}) collective-permute-start(bf16[200,512]{1,0:T(8,128)(2,1)S(1)} %get-tuple-element.79), channel_id=1, source_target_pairs={{0,9},{1,10},{2,11},{3,8},{4,13},{5,14},{6,15},{7,12},{8,1},{9,2},... | collective-permute-start | bytes 614408 | tf_op jit(solution)/shard_map/ppermute | solution.py:421
  86.1 5.1 %collective-permute-start.19 = (bf16[200,512]{1,0:T(8,128)(2,1)S(1)}, bf16[200,512]{1,0:T(8,128)(2,1)S(1)}, u32[]{:S(2)}, u32[]{:S(2)}) collective-permute-start(bf16[200,512]{1,0:T(8,128)(2,1)S(1)} %get-tuple-element.81), channel_id=1, source_target_pairs={{0,14},{1,15},{2,12},{3,13},{4,2},{5,3},{6,0},{7,1},{8,6},{9,7},{1... | collective-permute-start | bytes 614408 | tf_op jit(solution)/shard_map/ppermute | solution.py:421
  91.2 4.8 %collective-permute-start.13 = (bf16[200,512]{1,0:T(8,128)(2,1)S(1)}, bf16[200,512]{1,0:T(8,128)(2,1)S(1)}, u32[]{:S(2)}, u32[]{:S(2)}) collective-permute-start(bf16[200,512]{1,0:T(8,128)(2,1)S(1)} %get-tuple-element.74), channel_id=1, source_target_pairs={{0,15},{1,12},{2,13},{3,14},{4,3},{5,0},{6,1},{7,2},{8,7},{9,4},{1... | collective-permute-start | bytes 614408 | tf_op jit(solution)/shard_map/ppermute | solution.py:421
  96.0 1.5 %apply_fast.7.refs_15_ = bf16[200,512]{1,0:T(8,128)(2,1)S(1)} custom-call(s32[33]{0:T(128)S(1)} %copy-done.3, bf16[16,192,512]{2,1,0:T(8,128)(2,1)S(1)} %bitcast.7, bf16[16,192,512]{2,1,0:T(8,128)(2,1)S(1)} %bitcast.11, bf16[16,192,512]{2,1,0:T(8,128)(2,1)S(1)} %bitcast.15, f32[1,8192]{1,0:T(1,128)S(1)} %bitcast.19, ...), custom_call_target="tpu_custom_call" | custom-call | flops 301989888 | bytes 1048576 | tf_op jit(solution)/shard_map/apply_fast/pallas_call | solution.py:327
  97.5 6.9 %collective-permute-done.18.refs_6_ = bf16[200,512]{1,0:T(8,128)(2,1)S(1)} collective-permute-done((bf16[200,512]{1,0:T(8,128)(2,1)S(1)}, bf16[200,512]{1,0:T(8,128)(2,1)S(1)}, u32[]{:S(2)}, u32[]{:S(2)}) %collective-permute-start.18) | collective-permute-done | bytes 204832 | tf_op jit(solution)/shard_map/ppermute | solution.py:421
  104.5 3.2 %collective-permute-done.19.refs_7_ = bf16[200,512]{1,0:T(8,128)(2,1)S(1)} collective-permute-done((bf16[200,512]{1,0:T(8,128)(2,1)S(1)}, bf16[200,512]{1,0:T(8,128)(2,1)S(1)}, u32[]{:S(2)}, u32[]{:S(2)}) %collective-permute-start.19) | collective-permute-done | bytes 204832 | tf_op jit(solution)/shard_map/ppermute | solution.py:421
  107.7 1.8 %collective-permute-done.12.refs_0_ = bf16[200,512]{1,0:T(8,128)(2,1)S(1)} collective-permute-done((bf16[200,512]{1,0:T(8,128)(2,1)S(1)}, bf16[200,512]{1,0:T(8,128)(2,1)S(1)}, u32[]{:S(2)}, u32[]{:S(2)}) %collective-permute-start.12) | collective-permute-done | bytes 204832 | tf_op jit(solution)/shard_map/ppermute | solution.py:421
  109.5 2.5 %scale_rows.1 = bf16[192,8192]{1,0:T(8,128)(2,1)} custom-call(s32[33]{0:T(128)S(1)} %copy-done.3, bf16[200,512]{1,0:T(8,128)(2,1)S(1)} %collective-permute-done.12.refs_0_, bf16[200,512]{1,0:T(8,128)(2,1)S(1)} %collective-permute-done.13.refs_1_, bf16[200,512]{1,0:T(8,128)(2,1)S(1)} %collective-permute-done.14.refs_2_, ...), custom_call_target="tpu_custom_call" | custom-call | tf_op jit(solution)/shard_map/scale_rows/pallas_call | solution.py:363
  (35 shorter events, 0.1 us)
Async XLA Ops:
  0.0 7.2 %copy-start.7 = (f32[1,3072]{1,0:T(1,128)S(1)}, f32[1,3072]{1,0:T(1,128)}, u32[]{:S(2)}) copy-start(f32[1,3072]{1,0:T(1,128)} %rate_ref.1) | copy-start | bytes 36868
  0.0 7.2 %copy-start.4 = (bf16[1,512,512]{2,1,0:T(8,128)(2,1)S(1)}, bf16[1,512,512]{2,1,0:T(8,128)(2,1)}, u32[]{:S(2)}) copy-start(bf16[1,512,512]{2,1,0:T(8,128)(2,1)} %wi_ref.1) | copy-start | bytes 1572868
  0.0 7.2 %copy-start.5 = (bf16[1,512,512]{2,1,0:T(8,128)(2,1)S(1)}, bf16[1,512,512]{2,1,0:T(8,128)(2,1)}, u32[]{:S(2)}) copy-start(bf16[1,512,512]{2,1,0:T(8,128)(2,1)} %wu_ref.1) | copy-start | bytes 1572868
  0.0 7.2 %copy-start.6 = (bf16[1,512,512]{2,1,0:T(8,128)(2,1)S(1)}, bf16[1,512,512]{2,1,0:T(8,128)(2,1)}, u32[]{:S(2)}) copy-start(bf16[1,512,512]{2,1,0:T(8,128)(2,1)} %wo_ref.1) | copy-start | bytes 1572868
  2.2 42.1 %collective-permute-start.4 = (bf16[2,1024,512]{2,1,0:T(8,128)(2,1)S(1)}, bf16[2,1024,512]{2,1,0:T(8,128)(2,1)S(1)}, u32[]{:S(2)}, u32[]{:S(2)}) collective-permute-start(bf16[2,1024,512]{2,1,0:T(8,128)(2,1)S(1)} %get-tuple-element.66), channel_id=1, source_target_pairs={{0,16},{16,32},{32,48},{48,64},{64,80},{80,96},{96,112},{1,17},{17... | collective-permute-start | bytes 6291464 | tf_op jit(solution)/shard_map/ppermute | solution.py:387
  7.2 18.0 %copy-start = (bf16[3072,512]{1,0:T(8,128)(2,1)S(1)}, bf16[3072,512]{1,0:T(8,128)(2,1)}, u32[]{:S(2)}) copy-start(bf16[3072,512]{1,0:T(8,128)(2,1)} %q_ref.2) | copy-start | bytes 9437188
  20.7 2.4 %collective-permute-start = (bf16[3,256,512]{2,1,0:T(8,128)(2,1)S(1)}, bf16[3,256,512]{2,1,0:T(8,128)(2,1)S(1)}, u32[]{:S(2)}, u32[]{:S(2)}) collective-permute-start(bf16[3,256,512]{2,1,0:T(8,128)(2,1)S(1)} %get-tuple-element.50), channel_id=1, source_target_pairs={{0,16},{16,0},{32,48},{48,32},{64,80},{80,64},{96,112},{112,96},{1... | collective-permute-start | bytes 2359304 | tf_op jit(solution)/shard_map/ppermute | solution.py:384
  23.3 6.7 %collective-permute-start.1 = (bf16[3,64,512]{2,1,0:T(8,128)(2,1)S(1)}, bf16[3,64,512]{2,1,0:T(8,128)(2,1)S(1)}, u32[]{:S(2)}, u32[]{:S(2)}) collective-permute-start(bf16[3,64,512]{2,1,0:T(8,128)(2,1)S(1)} %get-tuple-element.57), channel_id=1, source_target_pairs={{0,96},{16,112},{32,0},{48,16},{64,32},{80,48},{96,64},{112,80},{1... | collective-permute-start | bytes 589832 | tf_op jit(solution)/shard_map/ppermute | solution.py:381
  25.2 11.1 %collective-permute-start.2 = (bf16[3,64,512]{2,1,0:T(8,128)(2,1)S(1)}, bf16[3,64,512]{2,1,0:T(8,128)(2,1)S(1)}, u32[]{:S(2)}, u32[]{:S(2)}) collective-permute-start(bf16[3,64,512]{2,1,0:T(8,128)(2,1)S(1)} %get-tuple-element.62), channel_id=1, source_target_pairs={{0,32},{16,48},{32,64},{48,80},{64,96},{80,112},{96,0},{112,16},{1... | collective-permute-start | bytes 589832 | tf_op jit(solution)/shard_map/ppermute | solution.py:381
  30.1 6.3 %collective-permute-start.3 = (bf16[3,64,512]{2,1,0:T(8,128)(2,1)S(1)}, bf16[3,64,512]{2,1,0:T(8,128)(2,1)S(1)}, u32[]{:S(2)}, u32[]{:S(2)}) collective-permute-start(bf16[3,64,512]{2,1,0:T(8,128)(2,1)S(1)} %shard_map.92), channel_id=1, source_target_pairs={{0,96},{16,112},{32,0},{48,16},{64,32},{80,48},{96,64},{112,80},{1... | collective-permute-start | bytes 589832 | tf_op jit(solution)/shard_map/ppermute | solution.py:381
  36.6 15.2 %copy-start.1 = (bf16[3072,512]{1,0:T(8,128)(2,1)S(1)}, bf16[3072,512]{1,0:T(8,128)(2,1)}, u32[]{:S(2)}) copy-start(bf16[3072,512]{1,0:T(8,128)(2,1)} %param.16) | copy-start | bytes 9437188
  36.6 15.2 %copy-start.2 = (f32[8192]{0:T(1024)S(1)}, f32[8192]{0:T(1024)}, u32[]{:S(2)}) copy-start(f32[8192]{0:T(1024)} %param.17) | copy-start | bytes 98308
  36.6 15.2 %copy-start.3 = (s32[33]{0:T(128)S(1)}, s32[33]{0:T(128)}, u32[]{:S(2)}) copy-start(s32[33]{0:T(128)} %get-tuple-element.47.table) | copy-start | bytes 400
  36.6 11.5 %collective-permute-start.5 = (bf16[3,64,512]{2,1,0:T(8,128)(2,1)S(1)}, bf16[3,64,512]{2,1,0:T(8,128)(2,1)S(1)}, u32[]{:S(2)}, u32[]{:S(2)}) collective-permute-start(bf16[3,64,512]{2,1,0:T(8,128)(2,1)S(1)} %shard_map.93.refs_0_), channel_id=1, source_target_pairs={{0,64},{16,80},{32,96},{48,112},{64,0},{80,16},{96,32},{112,48},{1... | collective-permute-start | bytes 589832 | tf_op jit(solution)/shard_map/ppermute | solution.py:381
  38.9 9.2 %collective-permute-start.6 = (bf16[3,64,512]{2,1,0:T(8,128)(2,1)S(1)}, bf16[3,64,512]{2,1,0:T(8,128)(2,1)S(1)}, u32[]{:S(2)}, u32[]{:S(2)}) collective-permute-start(bf16[3,64,512]{2,1,0:T(8,128)(2,1)S(1)} %shard_map.93.refs_0_), channel_id=1, source_target_pairs={{0,32},{16,48},{32,64},{48,80},{64,96},{80,112},{96,0},{112,16},{1... | collective-permute-start | bytes 589832 | tf_op jit(solution)/shard_map/ppermute | solution.py:381
  40.0 8.2 %collective-permute-start.7 = (bf16[3,64,512]{2,1,0:T(8,128)(2,1)S(1)}, bf16[3,64,512]{2,1,0:T(8,128)(2,1)S(1)}, u32[]{:S(2)}, u32[]{:S(2)}) collective-permute-start(bf16[3,64,512]{2,1,0:T(8,128)(2,1)S(1)} %shard_map.93.refs_0_), channel_id=1, source_target_pairs={{0,96},{16,112},{32,0},{48,16},{64,32},{80,48},{96,64},{112,80},{1... | collective-permute-start | bytes 589832 | tf_op jit(solution)/shard_map/ppermute | solution.py:381
  41.6 9.0 %collective-permute-start.8 = (bf16[3,64,512]{2,1,0:T(8,128)(2,1)S(1)}, bf16[3,64,512]{2,1,0:T(8,128)(2,1)S(1)}, u32[]{:S(2)}, u32[]{:S(2)}) collective-permute-start(bf16[3,64,512]{2,1,0:T(8,128)(2,1)S(1)} %shard_map.93.refs_0_), channel_id=1, source_target_pairs={{0,16},{16,0},{32,48},{48,32},{64,80},{80,64},{96,112},{112,96},{1... | collective-permute-start | bytes 589832 | tf_op jit(solution)/shard_map/ppermute | solution.py:384
  48.2 3.0 %collective-permute-start.10 = (bf16[3,64,512]{2,1,0:T(8,128)(2,1)S(1)}, bf16[3,64,512]{2,1,0:T(8,128)(2,1)S(1)}, u32[]{:S(2)}, u32[]{:S(2)}) collective-permute-start(bf16[3,64,512]{2,1,0:T(8,128)(2,1)S(1)} %collective-permute-done.6.refs_2_), channel_id=1, source_target_pairs={{0,16},{16,0},{32,48},{48,32},{64,80},{80,64},{96,112},{112,96},{1... | collective-permute-start | bytes 589832 | tf_op jit(solution)/shard_map/ppermute | solution.py:384
  50.1 1.4 %collective-permute-start.11 = (bf16[3,64,512]{2,1,0:T(8,128)(2,1)S(1)}, bf16[3,64,512]{2,1,0:T(8,128)(2,1)S(1)}, u32[]{:S(2)}, u32[]{:S(2)}) collective-permute-start(bf16[3,64,512]{2,1,0:T(8,128)(2,1)S(1)} %collective-permute-done.7.refs_3_), channel_id=1, source_target_pairs={{0,16},{16,0},{32,48},{48,32},{64,80},{80,64},{96,112},{112,96},{1... | collective-permute-start | bytes 589832 | tf_op jit(solution)/shard_map/ppermute | solution.py:384
  50.1 1.7 %collective-permute-start.9 = (bf16[3,64,512]{2,1,0:T(8,128)(2,1)S(1)}, bf16[3,64,512]{2,1,0:T(8,128)(2,1)S(1)}, u32[]{:S(2)}, u32[]{:S(2)}) collective-permute-start(bf16[3,64,512]{2,1,0:T(8,128)(2,1)S(1)} %collective-permute-done.5.refs_1_), channel_id=1, source_target_pairs={{0,16},{16,0},{32,48},{48,32},{64,80},{80,64},{96,112},{112,96},{1... | collective-permute-start | bytes 589832 | tf_op jit(solution)/shard_map/ppermute | solution.py:384
  58.2 11.6 %collective-permute-start.20 = (bf16[200,512]{1,0:T(8,128)(2,1)S(1)}, bf16[200,512]{1,0:T(8,128)(2,1)S(1)}, u32[]{:S(2)}, u32[]{:S(2)}) collective-permute-start(bf16[200,512]{1,0:T(8,128)(2,1)S(1)} %get-tuple-element.82), channel_id=1, source_target_pairs={{0,11},{1,8},{2,9},{3,10},{4,15},{5,12},{6,13},{7,14},{8,3},{9,0},... | collective-permute-start | bytes 614408 | tf_op jit(solution)/shard_map/ppermute | solution.py:421
  63.4 8.5 %collective-permute-start.21 = (bf16[200,512]{1,0:T(8,128)(2,1)S(1)}, bf16[200,512]{1,0:T(8,128)(2,1)S(1)}, u32[]{:S(2)}, u32[]{:S(2)}) collective-permute-start(bf16[200,512]{1,0:T(8,128)(2,1)S(1)} %get-tuple-element.83), channel_id=1, source_target_pairs={{0,2},{1,3},{2,0},{3,1},{4,6},{5,7},{6,4},{7,5},{8,10},{9,11},{10,... | collective-permute-start | bytes 614408 | tf_op jit(solution)/shard_map/ppermute | solution.py:421
  63.8 10.1 %collective-permute-start.22 = (bf16[200,512]{1,0:T(8,128)(2,1)S(1)}, bf16[200,512]{1,0:T(8,128)(2,1)S(1)}, u32[]{:S(2)}, u32[]{:S(2)}) collective-permute-start(bf16[200,512]{1,0:T(8,128)(2,1)S(1)} %get-tuple-element.84), channel_id=1, source_target_pairs={{0,8},{1,9},{2,10},{3,11},{4,12},{5,13},{6,14},{7,15},{8,0},{9,1},... | collective-permute-start | bytes 614408 | tf_op jit(solution)/shard_map/ppermute | solution.py:421
  64.0 13.1 %collective-permute-start.23 = (bf16[200,512]{1,0:T(8,128)(2,1)S(1)}, bf16[200,512]{1,0:T(8,128)(2,1)S(1)}, u32[]{:S(2)}, u32[]{:S(2)}) collective-permute-start(bf16[200,512]{1,0:T(8,128)(2,1)S(1)} %get-tuple-element.85), channel_id=1, source_target_pairs={{0,1},{1,2},{2,3},{3,0},{4,5},{5,6},{6,7},{7,4},{8,9},{9,10},{10,1... | collective-permute-start | bytes 614408 | tf_op jit(solution)/shard_map/ppermute | solution.py:421
  64.7 13.3 %collective-permute-start.24 = (bf16[200,512]{1,0:T(8,128)(2,1)S(1)}, bf16[200,512]{1,0:T(8,128)(2,1)S(1)}, u32[]{:S(2)}, u32[]{:S(2)}) collective-permute-start(bf16[200,512]{1,0:T(8,128)(2,1)S(1)} %get-tuple-element.86), channel_id=1, source_target_pairs={{0,4},{1,5},{2,6},{3,7},{4,8},{5,9},{6,10},{7,11},{8,12},{9,13},{1... | collective-permute-start | bytes 614408 | tf_op jit(solution)/shard_map/ppermute | solution.py:421
  69.8 12.0 %collective-permute-start.25 = (bf16[200,512]{1,0:T(8,128)(2,1)S(1)}, bf16[200,512]{1,0:T(8,128)(2,1)S(1)}, u32[]{:S(2)}, u32[]{:S(2)}) collective-permute-start(bf16[200,512]{1,0:T(8,128)(2,1)S(1)} %get-tuple-element.87), channel_id=1, source_target_pairs={{0,3},{1,0},{2,1},{3,2},{4,7},{5,4},{6,5},{7,6},{8,11},{9,8},{10,9... | collective-permute-start | bytes 614408 | tf_op jit(solution)/shard_map/ppermute | solution.py:421
  71.9 14.2 %collective-permute-start.26 = (bf16[200,512]{1,0:T(8,128)(2,1)S(1)}, bf16[200,512]{1,0:T(8,128)(2,1)S(1)}, u32[]{:S(2)}, u32[]{:S(2)}) collective-permute-start(bf16[200,512]{1,0:T(8,128)(2,1)S(1)} %get-tuple-element.88), channel_id=1, source_target_pairs={{0,12},{1,13},{2,14},{3,15},{4,0},{5,1},{6,2},{7,3},{8,4},{9,5},{1... | collective-permute-start | bytes 614408 | tf_op jit(solution)/shard_map/ppermute | solution.py:421
  73.9 12.2 %collective-permute-start.14 = (bf16[200,512]{1,0:T(8,128)(2,1)S(1)}, bf16[200,512]{1,0:T(8,128)(2,1)S(1)}, u32[]{:S(2)}, u32[]{:S(2)}) collective-permute-start(bf16[200,512]{1,0:T(8,128)(2,1)S(1)} %get-tuple-element.76), channel_id=1, source_target_pairs={{0,7},{1,4},{2,5},{3,6},{4,11},{5,8},{6,9},{7,10},{8,15},{9,12},{1... | collective-permute-start | bytes 614408 | tf_op jit(solution)/shard_map/ppermute | solution.py:421
  77.1 14.1 %collective-permute-start.15 = (bf16[200,512]{1,0:T(8,128)(2,1)S(1)}, bf16[200,512]{1,0:T(8,128)(2,1)S(1)}, u32[]{:S(2)}, u32[]{:S(2)}) collective-permute-start(bf16[200,512]{1,0:T(8,128)(2,1)S(1)} %get-tuple-element.77), channel_id=1, source_target_pairs={{0,13},{1,14},{2,15},{3,12},{4,1},{5,2},{6,3},{7,0},{8,5},{9,6},{1... | collective-permute-start | bytes 614408 | tf_op jit(solution)/shard_map/ppermute | solution.py:421
  78.0 13.2 %collective-permute-start.16 = (bf16[200,512]{1,0:T(8,128)(2,1)S(1)}, bf16[200,512]{1,0:T(8,128)(2,1)S(1)}, u32[]{:S(2)}, u32[]{:S(2)}) collective-permute-start(bf16[200,512]{1,0:T(8,128)(2,1)S(1)} %get-tuple-element.78), channel_id=1, source_target_pairs={{0,10},{1,11},{2,8},{3,9},{4,14},{5,15},{6,12},{7,13},{8,2},{9,3},... | collective-permute-start | bytes 614408 | tf_op jit(solution)/shard_map/ppermute | solution.py:421
  81.8 15.7 %collective-permute-start.17 = (bf16[200,512]{1,0:T(8,128)(2,1)S(1)}, bf16[200,512]{1,0:T(8,128)(2,1)S(1)}, u32[]{:S(2)}, u32[]{:S(2)}) collective-permute-start(bf16[200,512]{1,0:T(8,128)(2,1)S(1)} %get-tuple-element.79), channel_id=1, source_target_pairs={{0,9},{1,10},{2,11},{3,8},{4,13},{5,14},{6,15},{7,12},{8,1},{9,2},... | collective-permute-start | bytes 614408 | tf_op jit(solution)/shard_map/ppermute | solution.py:421
  86.1 18.4 %collective-permute-start.18 = (bf16[200,512]{1,0:T(8,128)(2,1)S(1)}, bf16[200,512]{1,0:T(8,128)(2,1)S(1)}, u32[]{:S(2)}, u32[]{:S(2)}) collective-permute-start(bf16[200,512]{1,0:T(8,128)(2,1)S(1)} %get-tuple-element.80), channel_id=1, source_target_pairs={{0,6},{1,7},{2,4},{3,5},{4,10},{5,11},{6,8},{7,9},{8,14},{9,15},{1... | collective-permute-start | bytes 614408 | tf_op jit(solution)/shard_map/ppermute | solution.py:421
  86.1 21.6 %collective-permute-start.19 = (bf16[200,512]{1,0:T(8,128)(2,1)S(1)}, bf16[200,512]{1,0:T(8,128)(2,1)S(1)}, u32[]{:S(2)}, u32[]{:S(2)}) collective-permute-start(bf16[200,512]{1,0:T(8,128)(2,1)S(1)} %get-tuple-element.81), channel_id=1, source_target_pairs={{0,14},{1,15},{2,12},{3,13},{4,2},{5,3},{6,0},{7,1},{8,6},{9,7},{1... | collective-permute-start | bytes 614408 | tf_op jit(solution)/shard_map/ppermute | solution.py:421
  91.2 18.3 %collective-permute-start.12 = (bf16[200,512]{1,0:T(8,128)(2,1)S(1)}, bf16[200,512]{1,0:T(8,128)(2,1)S(1)}, u32[]{:S(2)}, u32[]{:S(2)}) collective-permute-start(bf16[200,512]{1,0:T(8,128)(2,1)S(1)} %get-tuple-element.73), channel_id=1, source_target_pairs={{0,5},{1,6},{2,7},{3,4},{4,9},{5,10},{6,11},{7,8},{8,13},{9,14},{1... | collective-permute-start | bytes 614408 | tf_op jit(solution)/shard_map/ppermute | solution.py:421
  91.2 18.3 %collective-permute-start.13 = (bf16[200,512]{1,0:T(8,128)(2,1)S(1)}, bf16[200,512]{1,0:T(8,128)(2,1)S(1)}, u32[]{:S(2)}, u32[]{:S(2)}) collective-permute-start(bf16[200,512]{1,0:T(8,128)(2,1)S(1)} %get-tuple-element.74), channel_id=1, source_target_pairs={{0,15},{1,12},{2,13},{3,14},{4,3},{5,0},{6,1},{7,2},{8,7},{9,4},{1... | collective-permute-start | bytes 614408 | tf_op jit(solution)/shard_map/ppermute | solution.py:421
